TPU v7x, 32 devices: a whole 2x2x4 slice. The times are simulated.
32 devices in a mesh: groups: 2 (over y), chan: 8 (over z, x), win: 2 (over core).
Axes of the slice: x: 2, y: 2, z: 4, core: 2. Of those that a mesh axis runs over, the one named last changes fastest.
Arguments:
- records: bfloat16 [8192, 512], P(('groups', 'chan', 'win')), parts along dimension 0
- record_channel: int32 [8192], P(('groups', 'chan', 'win')), parts along dimension 0, may hold values from 0 to 127, as said below
- record_piece: int32 [8192], P(('groups', 'chan', 'win')), parts along dimension 0, may hold values from 0 to 15
- fir_taps: bfloat16 [32], replicated, may hold values from -1 to 1
- window_starts: int32 [32], P(('groups', 'win')), parts along dimension 0, may hold values from 0 to 1024, as said below
- source_slot: int32 [16], P(('groups', 'chan')), parts along dimension 0, may hold values from 0 to 15
Outputs:
- correlations: float32 [16, 128, 256], P(('groups', 'win'), 'chan'), parts along dimension 0
There are 2 independent parts, one for each index of `groups`. A program takes and returns all parts, laid end to end along the dimension named above; an argument that names none is the same for every part. Nothing has to cross between parts.
Inputs may be any that keep to these rules, and one draw needn't show every extreme that they name: `record_channel`: record r sits on the device r // 256 of chan and win joined, chan slowest. Among the records of one time span each pair of a channel and a piece occurs exactly once. The records of one device hold at most 64 records whose channels lie in any one block of 16 consecutive channels, and in every span some device holds exactly 64 of one block. `window_starts`: window w belongs to span w // 8; the first window of the minute starts at 0 and the last at 1024.
All inputs are finite; a program needn't handle non-finite values.
Results may differ from a plain program's by a relative error of at most 0.0041.
Values may be sent and summed in bfloat16 or wider, within the bound.
No kernel may reach another device: no remote copies, remote signals or barrier semaphores. Data moves between devices by JAX's collectives and lax.ppermute only.
A program may use at most 64 MiB of HBM per device.

v0:
```python
import math

import jax
import jax.numpy as jnp
from jax import lax
from jax.sharding import PartitionSpec as P

CH_DEV = 16
SPAN = 2048
WIN_DEV = 8
WL = 1024
NF = 512
DEC = 4
TAPS = 32
SPILL = 7
SEG = 512
PIECES = 16
BAND = 64
LAGS = 256


EPSILON = 1e-06


def make_filter(fir_taps):
    outputs_per = SEG // DEC
    sample_index = jnp.arange(SEG, dtype=jnp.int32)[:, None]
    column_index = jnp.arange(outputs_per + SPILL, dtype=jnp.int32)[None, :]
    tap_index = jnp.where(
        column_index < outputs_per,
        DEC * column_index + DEC - 1 - sample_index,
        DEC * (column_index - outputs_per) + DEC - 1 + SEG - sample_index,
    )
    match_table = (
        tap_index[:, :, None] == jnp.arange(TAPS, dtype=jnp.int32)[None, None, :]
    ).astype(jnp.float32)
    return jnp.sum(match_table * fir_taps.astype(jnp.float32)[None, None, :], axis=2).astype(
        jnp.bfloat16
    )


def make_fourier():
    sample_index = jnp.arange(WL, dtype=jnp.int32)[:, None]
    freq_index = jnp.arange(NF, dtype=jnp.int32)[None, :]
    phase = 2.0 * math.pi * (sample_index * freq_index % WL).astype(jnp.float32) / WL
    return jnp.concatenate([jnp.cos(phase), -jnp.sin(phase)], axis=1).astype(jnp.bfloat16)


def make_taper():
    sample_index = jnp.arange(WL, dtype=jnp.int32).astype(jnp.float32)
    return 0.5 - 0.5 * jnp.cos(2.0 * math.pi * sample_index / WL)


def make_lags():
    freq_index = jnp.arange(NF, dtype=jnp.int32)[:, None]
    lag_index = jnp.arange(LAGS, dtype=jnp.int32)[None, :] - LAGS // 2
    phase = 2.0 * math.pi * (freq_index * lag_index % WL).astype(jnp.float32) / WL
    scale = 1.0 / math.sqrt(WL * WIN_DEV)
    return (jnp.concatenate([jnp.cos(phase), -jnp.sin(phase)], axis=0) * scale).astype(jnp.bfloat16)


def whiten(spectra):
    freq_index = jnp.arange(NF, dtype=jnp.int32)
    band_table = (jnp.abs(freq_index[:, None] - freq_index[None, :]) <= BAND).astype(jnp.float32)
    band_count = jnp.sum(band_table, axis=0)
    real_part = spectra[..., :NF]
    imag_part = spectra[..., NF:]
    energy = real_part * real_part + imag_part * imag_part
    smooth = jnp.dot(energy, band_table, precision=lax.Precision.HIGHEST) / band_count[None, :]
    amplitude = jnp.sqrt(smooth + EPSILON)
    return (spectra / jnp.concatenate([amplitude, amplitude], axis=-1)).astype(jnp.bfloat16)


def cross_spectrum(source_block, local_block):
    src_real = source_block[..., :NF]
    src_imag = source_block[..., NF:]
    loc_real = local_block[..., :NF]
    loc_imag = local_block[..., NF:]
    real_sum = jnp.einsum(
        "bwf,cwf->bcf", src_real, loc_real, preferred_element_type=jnp.float32
    ) + jnp.einsum("bwf,cwf->bcf", src_imag, loc_imag, preferred_element_type=jnp.float32)
    imag_sum = jnp.einsum(
        "bwf,cwf->bcf", src_imag, loc_real, preferred_element_type=jnp.float32
    ) - jnp.einsum("bwf,cwf->bcf", src_real, loc_imag, preferred_element_type=jnp.float32)
    return jnp.concatenate([real_sum, imag_sum], axis=-1).astype(jnp.bfloat16)


def over_blocks(block_fn, sources, channel_count):
    source_count = sources.shape[0]
    block_size = math.gcd(source_count, 16)
    block_count = source_count // block_size
    grouped = sources.reshape((block_count, block_size) + sources.shape[1:])
    return lax.map(block_fn, grouped).reshape(source_count, channel_count, LAGS)


def body(records, record_channel, record_piece, fir_taps, window_starts, source_slot):
    block_total = lax.axis_size("chan")
    per_device = records.shape[0]
    capacity = 2 * per_device // block_total
    outputs_per = SEG // DEC
    owner_block = record_channel // CH_DEV
    local_slot = record_channel % CH_DEV * PIECES + record_piece
    one_hot = (owner_block[:, None] == jnp.arange(block_total, dtype=jnp.int32)[None, :]).astype(
        jnp.int32
    )
    earlier_count = jnp.sum((jnp.cumsum(one_hot, axis=0) - one_hot) * one_hot, axis=1)
    position = owner_block * capacity + earlier_count
    slot_table = (
        jnp.full((block_total * capacity,), -1, jnp.int32)
        .at[position]
        .set(local_slot)
        .reshape(block_total, capacity)
    )
    filter_matrix = make_filter(fir_taps)
    row_send = (
        jnp.zeros((block_total * capacity, SEG), jnp.bfloat16)
        .at[position]
        .set(records)
        .reshape(block_total, capacity, SEG)
    )
    rows_got, slots_got = (
        lax.all_to_all(row_send, "chan", split_axis=0, concat_axis=0, tiled=True),
        lax.all_to_all(slot_table, "chan", split_axis=0, concat_axis=0, tiled=True),
    )
    flat_slots = slots_got.reshape(-1)
    target = jnp.where(flat_slots >= 0, flat_slots, per_device)
    traces = (
        jnp.zeros((per_device, SEG), jnp.bfloat16)
        .at[target]
        .set(rows_got.reshape(-1, SEG), mode="drop")
    )
    filtered = jnp.dot(traces, filter_matrix, preferred_element_type=jnp.float32)
    main_part = filtered[:, :outputs_per]
    spill_part = filtered[:, outputs_per:]
    main_part = main_part.reshape(CH_DEV, PIECES, outputs_per)
    spill_part = spill_part.reshape(CH_DEV, PIECES, SPILL)
    carried = jnp.pad(spill_part[:, :-1, :], ((0, 0), (1, 0), (0, outputs_per - SPILL)))
    decimated = (main_part + carried).reshape(CH_DEV, SPAN)

    def window_cut(window_start):
        return lax.dynamic_slice_in_dim(decimated, window_start, WL, 1)

    segments = (jax.vmap(window_cut, out_axes=1)(window_starts) * make_taper()).astype(jnp.bfloat16)
    window_count = segments.shape[1]
    spectra = jnp.dot(segments.reshape(-1, WL), make_fourier(), preferred_element_type=jnp.float32)
    whitened = whiten(spectra).reshape(CH_DEV, window_count, WL)
    source = lax.dynamic_slice_in_dim(whitened, source_slot[0], 1, 0)
    gathered = lax.all_gather(source, "chan", axis=0, tiled=True)
    lag_table = make_lags()

    def span_block(source_block):
        cross_spectra = cross_spectrum(source_block, whitened)
        return jnp.dot(
            cross_spectra.reshape(-1, WL), lag_table, preferred_element_type=jnp.float32
        ).reshape(source_block.shape[0], CH_DEV, LAGS)

    return lax.psum_scatter(
        over_blocks(span_block, gathered, CH_DEV), "win", scatter_dimension=0, tiled=True
    )


def solution(mesh):
    in_specs = (
        P(("groups", "chan", "win"), None),
        P(("groups", "chan", "win")),
        P(("groups", "chan", "win")),
        P(),
        P(("groups", "win")),
        P(("groups", "chan")),
    )
    out_specs = P(("groups", "win"), "chan", None)
    return jax.shard_map(body, mesh=mesh, in_specs=in_specs, out_specs=out_specs, check_vma=False)
```

profile of v0, /device:TPU:0, one launch (start us, length us, event | category | flops | bytes accessed | tf_op | source)
XLA Modules:
  0.0 139.5 jit_solution(8627850086978740682)
XLA Ops:
  6.5 0.7 fusion.47
  7.3 0.6 reduce-window.6
  8.2 1.4 %scatter_custom_fusion = s32[512]{0:T(512)S(1)} fusion(s32[256]{0:T(256)S(1)} %compare_select_fusion.2, s32[256]{0:T(256)S(1)} %get-tuple-element.40, s32[]{:T(128)} %constant.101.clone.1), kind=kCustom, calls=%fused_computation.92 | custom fusion | bytes 2052 | tf_op jit(solution)/shard_map/scatter | solution.py:111
  9.6 0.7 all_to_all.9
  10.3 7.3 %all-to-all-start = ((s32[8,1,64]{2,1,0:T(1,128)}), s32[8,1,64]{2,1,0:T(1,128)S(1)}, u32[]{:S(2)}, u32[]{:S(2)}) async-start(s32[8,1,64]{2,1,0:T(1,128)} %all_to_all.9), calls=%async_computation | async-start | bytes 8192 | tf_op jit(solution)/shard_map/all_to_all | solution.py:123
  17.6 0.7 fusion.50
  18.2 2.9 %fusion.34 = (f32[512,256]{1,0:T(8,128)}, f32[512,256]{1,0:T(8,128)}) fusion(s32[256]{0:T(256)S(1)} %iota_add_fusion), kind=kLoop, calls=%fused_computation.58 | loop fusion | flops 1966080 | bytes 1049600 | tf_op jit(solution)/shard_map/cos | solution.py:59
  21.4 0.7 convert_element_type.55
  22.8 2.7 %scatter_custom_fusion.1 = bf16[512,512]{1,0:T(8,128)(2,1)} fusion(s32[256]{0:T(256)S(1)} %compare_select_fusion.2, bf16[256,512]{1,0:T(8,128)(2,1)} %param.6, bf16[]{:T(256)} %constant.100.clone.1), kind=kCustom, calls=%fused_computation.60 | custom fusion | bytes 524800 | tf_op jit(solution)/shard_map/scatter | solution.py:118
  25.5 6.0 %all-to-all-start.1 = ((bf16[8,64,512]{2,1,0:T(8,128)(2,1)}), bf16[8,64,512]{2,1,0:T(8,128)(2,1)S(1)}, u32[]{:S(2)}, u32[]{:S(2)}) async-start(bf16[8,64,512]{2,1,0:T(8,128)(2,1)} %bitcast.4), calls=%async_computation.1 | async-start | bytes 1048576 | tf_op jit(solution)/shard_map/all_to_all | solution.py:122
  31.6 8.5 %negate_convert_fusion = (bf16[1024,512]{1,0:T(8,128)(2,1)S(1)}, bf16[1024,512]{1,0:T(8,128)(2,1)S(1)}) fusion(), kind=kLoop, calls=%fused_computation.19 | loop fusion | flops 8912896 | bytes 2097152 | tf_op jit(solution)/shard_map/convert.5
  40.1 2.7 %select_reduce_fusion = bf16[512,135]{0,1:T(8,128)(2,1)S(1)} fusion(f32[32]{0:T(128)S(1)} %convert_element_type.55, s32[512,135]{0,1:T(8,128)S(1)} %subtract_select_fusion), kind=kLoop, calls=%fused_computation.5 | loop fusion | flops 6566400 | bytes 414848 | tf_op jit(solution)/shard_map/reduce_sum | solution.py:37
  43.3 0.7 reduce.5
  44.0 1.4 %all-to-all-done.1 = bf16[8,64,512]{2,1,0:T(8,128)(2,1)S(1)} async-done(((bf16[8,64,512]{2,1,0:T(8,128)(2,1)}), bf16[8,64,512]{2,1,0:T(8,128)(2,1)S(1)}, u32[]{:S(2)}, u32[]{:S(2)}) %all-to-all-start.1) | async-done | bytes 524320 | tf_op jit(solution)/shard_map/all_to_all | solution.py:122
  45.5 2.4 %scatter_custom_fusion.2 = bf16[256,512]{1,0:T(8,128)(2,1)S(1)} fusion(s32[512]{0:T(512)S(1)} %bitcast.62, bf16[512,512]{1,0:T(8,128)(2,1)S(1)} %bitcast.60, bf16[]{:T(256)} %constant.100.clone.1), kind=kCustom, calls=%fused_computation.67 | custom fusion | bytes 262146 | tf_op jit(solution)/shard_map/scatter | solution.py:130
  48.5 26.9 %while.1 = (s32[]{:T(128)}, f32[16,2048]{1,0:T(8,128)S(1)}, s32[8,2]{0,1:T(2,128)S(1)}, f32[8,16,1024]{2,0,1:T(8,128)}, s32[]{:T(128)}, /*index=5*/s32[]{:T(128)}) while((s32[]{:T(128)}, f32[16,2048]{1,0:T(8,128)S(1)}, s32[8,2]{0,1:T(2,128)S(1)}, f32[8,16,1024]{2,0,1:T(8,128)}, s32[]{:T(128)}, /*index=5*/s32[]{:T(128)}) %tuple.29), condition=%wide.while_cond, body=%wide.while_body.sunk | while | flops 2 | bytes 393321 | solution.py:141
  48.6 0.5 slice.83
  49.1 0.7 dynamic-slice_bitcast_fusion.2
  49.9 2.0 %dynamic-update-slice.3 = f32[8,16,1024]{2,0,1:T(8,128)} dynamic-update-slice(f32[8,16,1024]{2,0,1:T(8,128)} %get-tuple-element.82, f32[1,16,1024]{2,0,1:T(1,128)S(1)} %copy.51, s32[]{:T(128)} %get-tuple-element.79, s32[]{:T(128)} %constant.103.clone.1..sunk, s32[]{:T(128)} %constant.103.clone.1..sunk) | dynamic-update-slice | bytes 131076 | tf_op jit(solution)/shard_map/vmap()/gather
  52.4 0.7 dynamic-slice_bitcast_fusion.2
  53.2 2.0 %dynamic-update-slice.3 = f32[8,16,1024]{2,0,1:T(8,128)} dynamic-update-slice(f32[8,16,1024]{2,0,1:T(8,128)} %get-tuple-element.82, f32[1,16,1024]{2,0,1:T(1,128)S(1)} %copy.51, s32[]{:T(128)} %get-tuple-element.79, s32[]{:T(128)} %constant.103.clone.1..sunk, s32[]{:T(128)} %constant.103.clone.1..sunk) | dynamic-update-slice | bytes 131076 | tf_op jit(solution)/shard_map/vmap()/gather
  55.8 0.7 dynamic-slice_bitcast_fusion.2
  56.6 2.0 %dynamic-update-slice.3 = f32[8,16,1024]{2,0,1:T(8,128)} dynamic-update-slice(f32[8,16,1024]{2,0,1:T(8,128)} %get-tuple-element.82, f32[1,16,1024]{2,0,1:T(1,128)S(1)} %copy.51, s32[]{:T(128)} %get-tuple-element.79, s32[]{:T(128)} %constant.103.clone.1..sunk, s32[]{:T(128)} %constant.103.clone.1..sunk) | dynamic-update-slice | bytes 131076 | tf_op jit(solution)/shard_map/vmap()/gather
  59.2 0.7 dynamic-slice_bitcast_fusion.2
  60.0 2.0 %dynamic-update-slice.3 = f32[8,16,1024]{2,0,1:T(8,128)} dynamic-update-slice(f32[8,16,1024]{2,0,1:T(8,128)} %get-tuple-element.82, f32[1,16,1024]{2,0,1:T(1,128)S(1)} %copy.51, s32[]{:T(128)} %get-tuple-element.79, s32[]{:T(128)} %constant.103.clone.1..sunk, s32[]{:T(128)} %constant.103.clone.1..sunk) | dynamic-update-slice | bytes 131076 | tf_op jit(solution)/shard_map/vmap()/gather
  62.5 0.7 dynamic-slice_bitcast_fusion.2
  63.3 2.0 %dynamic-update-slice.3 = f32[8,16,1024]{2,0,1:T(8,128)} dynamic-update-slice(f32[8,16,1024]{2,0,1:T(8,128)} %get-tuple-element.82, f32[1,16,1024]{2,0,1:T(1,128)S(1)} %copy.51, s32[]{:T(128)} %get-tuple-element.79, s32[]{:T(128)} %constant.103.clone.1..sunk, s32[]{:T(128)} %constant.103.clone.1..sunk) | dynamic-update-slice | bytes 131076 | tf_op jit(solution)/shard_map/vmap()/gather
  65.9 0.7 dynamic-slice_bitcast_fusion.2
  66.7 2.0 %dynamic-update-slice.3 = f32[8,16,1024]{2,0,1:T(8,128)} dynamic-update-slice(f32[8,16,1024]{2,0,1:T(8,128)} %get-tuple-element.82, f32[1,16,1024]{2,0,1:T(1,128)S(1)} %copy.51, s32[]{:T(128)} %get-tuple-element.79, s32[]{:T(128)} %constant.103.clone.1..sunk, s32[]{:T(128)} %constant.103.clone.1..sunk) | dynamic-update-slice | bytes 131076 | tf_op jit(solution)/shard_map/vmap()/gather
  69.3 0.7 dynamic-slice_bitcast_fusion.2
  70.1 2.0 %dynamic-update-slice.3 = f32[8,16,1024]{2,0,1:T(8,128)} dynamic-update-slice(f32[8,16,1024]{2,0,1:T(8,128)} %get-tuple-element.82, f32[1,16,1024]{2,0,1:T(1,128)S(1)} %copy.51, s32[]{:T(128)} %get-tuple-element.79, s32[]{:T(128)} %constant.103.clone.1..sunk, s32[]{:T(128)} %constant.103.clone.1..sunk) | dynamic-update-slice | bytes 131076 | tf_op jit(solution)/shard_map/vmap()/gather
  72.6 0.7 dynamic-slice_bitcast_fusion.2
  73.4 2.0 %dynamic-update-slice.3 = f32[8,16,1024]{2,0,1:T(8,128)} dynamic-update-slice(f32[8,16,1024]{2,0,1:T(8,128)} %get-tuple-element.82, f32[1,16,1024]{2,0,1:T(1,128)S(1)} %copy.51, s32[]{:T(128)} %get-tuple-element.79, s32[]{:T(128)} %constant.103.clone.1..sunk, s32[]{:T(128)} %constant.103.clone.1..sunk) | dynamic-update-slice | bytes 131076 | tf_op jit(solution)/shard_map/vmap()/gather
  75.4 1.5 %fusion.3 = f32[128,1024]{1,0:T(8,128)S(1)} fusion(bf16[1024,512]{1,0:T(8,128)(2,1)S(1)} %get-tuple-element.46, bf16[1024,512]{1,0:T(8,128)(2,1)S(1)} %get-tuple-element.47, f32[8,16,1024]{2,0,1:T(8,128)} %get-tuple-element.27, f32[1024]{0:T(1024)S(1)} %multiply_subtract_fusion), kind=kOutput, calls=%fused_computation.13 | convolution fusion | flops 272891904 | bytes 3149824 | tf_op jit(solution)/shard_map/dot_general | solution.py:145
  76.9 0.5 fusion.13
  77.6 30.8 %all_gather.3 = bf16[8,8,1024]{2,1,0:T(8,128)(2,1)S(1)} all-gather(bf16[1,8,1024]{2,1,0:T(8,128)(2,1)S(1)} %constant_dynamic-slice_fusion.1), channel_id=1, replica_groups=mesh['groups'=2,'chan'=8,'win'=2] {'chan'}, dimensions={0}, use_global_device_ids=true | all-gather | bytes 147456 | tf_op jit(solution)/shard_map/all_gather | solution.py:148
  108.4 0.7 copy.41
  109.1 1.7 %copy.40 = bf16[16,8,512]{0,1,2:T(8,128)(2,1)} copy(bf16[16,8,512]{2,1,0:T(8,128)(2,1)S(1)} %get-tuple-element.37) | data formatting | bytes 262144
  110.8 0.7 copy.43
  111.5 0.8 copy.42
  112.4 2.0 %fusion.58 = f32[512,16,8]{1,2,0:T(8,128)S(1)} fusion(bf16[16,8,512]{0,1,2:T(8,128)(2,1)} %copy.40, bf16[8,8,512]{1,0,2:T(8,128)(2,1)S(1)} %copy.41), kind=kOutput, calls=%fused_computation.105 | convolution fusion | flops 1048576 | bytes 458752 | tf_op jit(solution)/shard_map/while/body/eval_jaxpr/bwf,cwf->bcf/dot_general | solution.py:79
  114.4 2.0 %fusion.59 = f32[512,16,8]{1,2,0:T(8,128)} fusion(bf16[16,8,512]{0,1,2:T(8,128)(2,1)S(1)} %copy-done, bf16[8,8,512]{1,0,2:T(8,128)(2,1)S(1)} %copy.43), kind=kOutput, calls=%fused_computation.106 | convolution fusion | flops 1048576 | bytes 458752 | tf_op jit(solution)/shard_map/while/body/eval_jaxpr/bwf,cwf->bcf/dot_general | solution.py:82
  116.4 1.7 %fusion.10 = bf16[8,16,512]{1,0,2:T(8,128)(2,1)} fusion(f32[512,16,8]{1,2,0:T(8,128)S(1)} %fusion.58, bf16[16,8,512]{0,1,2:T(8,128)(2,1)S(1)} %copy.42, bf16[8,8,512]{1,0,2:T(8,128)(2,1)S(1)} %copy.43), kind=kOutput, calls=%fused_computation.24 | convolution fusion | flops 1179648 | bytes 589824 | tf_op jit(solution)/shard_map/while/body/eval_jaxpr/bwf,cwf->bcf/dot_general | solution.py:81
  118.1 1.8 %copy.35 = bf16[8,16,512]{2,1,0:T(8,128)(2,1)S(1)} copy(bf16[8,16,512]{1,0,2:T(8,128)(2,1)} %fusion.10) | data formatting | bytes 262144 | tf_op jit(solution)/shard_map/while/body/eval_jaxpr/add | solution.py:79
  120.0 2.3 %fusion.11 = bf16[8,16,512]{1,0,2:T(8,128)(2,1)S(1)} fusion(f32[512,16,8]{1,2,0:T(8,128)} %fusion.59, bf16[16,8,512]{0,1,2:T(8,128)(2,1)S(1)} %copy.42, bf16[8,8,512]{1,0,2:T(8,128)(2,1)S(1)} %copy.41), kind=kOutput, calls=%fused_computation.25 | convolution fusion | flops 1179648 | bytes 589824 | tf_op jit(solution)/shard_map/while/body/eval_jaxpr/bwf,cwf->bcf/dot_general | solution.py:84
  122.2 0.7 copy.36
  123.0 2.1 %fusion.19 = f32[8,16,256]{2,1,0:T(8,128)} fusion(f32[512,256]{1,0:T(8,128)} %get-tuple-element.43, f32[512,256]{1,0:T(8,128)} %get-tuple-element.42, bf16[8,16,512]{2,1,0:T(8,128)(2,1)S(1)} %copy.36, bf16[8,16,512]{2,1,0:T(8,128)(2,1)S(1)} %copy.35), kind=kOutput, calls=%fused_computation.40 | convolution fusion | flops 68419584 | bytes 1441792 | tf_op jit(solution)/shard_map/while/body/eval_jaxpr/dot_general | solution.py:153
  125.1 7.6 %reduce-scatter.2.cloned.1.call-done = f32[4,16,256]{2,1,0:T(8,128)} async-done(((f32[8,16,256]{2,1,0:T(8,128)}), f32[4,16,256]{2,1,0:T(8,128)}) %reduce-scatter.2.cloned.1.call-update) | async-done | bytes 65552 | tf_op jit(solution)/shard_map/reduce_scatter | solution.py:157
  (56 shorter events, 6.7 us)
Async XLA Ops:
  10.3 15.2 %all-to-all-start = ((s32[8,1,64]{2,1,0:T(1,128)}), s32[8,1,64]{2,1,0:T(1,128)S(1)}, u32[]{:S(2)}, u32[]{:S(2)}) async-start(s32[8,1,64]{2,1,0:T(1,128)} %all_to_all.9), calls=%async_computation | async-start | bytes 8192 | tf_op jit(solution)/shard_map/all_to_all | solution.py:123
  25.5 20.0 %all-to-all-start.1 = ((bf16[8,64,512]{2,1,0:T(8,128)(2,1)}), bf16[8,64,512]{2,1,0:T(8,128)(2,1)S(1)}, u32[]{:S(2)}, u32[]{:S(2)}) async-start(bf16[8,64,512]{2,1,0:T(8,128)(2,1)} %bitcast.4), calls=%async_computation.1 | async-start | bytes 1048576 | tf_op jit(solution)/shard_map/all_to_all | solution.py:122
  31.5 101.2 %reduce-scatter.2.cloned.1.call-start = ((), (), s32[]{:S(2)}) async-start(), calls=%async_computation.3 | async-start | bytes 196608 | tf_op jit(solution)/shard_map/reduce_scatter | solution.py:157
  112.4 2.0 %copy-start = (bf16[16,8,512]{0,1,2:T(8,128)(2,1)S(1)}, bf16[16,8,512]{0,1,2:T(8,128)(2,1)}, u32[]{:S(2)}) copy-start(bf16[16,8,512]{0,1,2:T(8,128)(2,1)} %copy.40) | copy-start | bytes 393220
Sparse Core Ops, SparseCore 0:
  125.2 7.4 reduce-scatter.1
where the time goes:
time: 140 us; the launch traced here: 139 us
  local copies, waits for them, and re-layouts  41.7 us (30%)
  blocking collectives  30.8 us (22%)
  other arithmetic  18 us (13%)
  between operations  14.3 us (10%)
  starting transfers between devices  13.3 us (10%)
  matrix products  12.4 us (9%)
  waiting for transfers between devices  9 us (6%)
    all_gather x1, blocking collectives, body(): gathered = lax.all_gather(source, 'chan', axis=0, tiled=True)  30.8 us
    gather x40, local copies, waits for them, and re-layouts  26.8 us
    another operation x3, other arithmetic  9.17 us
    reduce_scatter x1, waiting for transfers between devices, body(): lax.psum_scatter(over_blocks(span_block, gathered, CH_DEV), 'win', scatte...  7.58 us
    all_to_all x1, starting transfers between devices, body(): lax.all_to_all(slot_table, 'chan', split_axis=0, concat_axis=0, tiled=True)  7.25 us
    all_to_all x1, starting transfers between devices, body(): lax.all_to_all(row_send, 'chan', split_axis=0, concat_axis=0, tiled=True)  5.99 us
    unnamed x7, local copies, waits for them, and re-layouts  4.01 us
    cos x1, other arithmetic, make_lags(): jnp.cos(phase)  2.94 us
  transfers between devices with their start and end apart: 3, of which 2 were waited for; matrix products, arithmetic and copies ran while one was open for 14% of the time, Pallas kernels for 0%

commit v1 on v0

--- a/solution.py
+++ b/solution.py
@@ -2,7 +2,11 @@
 
 import jax
 import jax.numpy as jnp
+import ml_dtypes
+import numpy as np
 from jax import lax
+from jax.experimental import pallas as pl
+from jax.experimental.pallas import tpu as pltpu
 from jax.sharding import PartitionSpec as P
 
 CH_DEV = 16
@@ -21,6 +25,370 @@
 
 EPSILON = 1e-06
 
+LANES = 128
+OUTS = SEG // DEC
+AUX = 16
+SCALE_ROW = SPILL
+KEY_ROW = SPILL + 1
+SLOT_ROW = SPILL + 2
+FILTER_VMEM = 62 << 20
+CORRELATE_VMEM = 53 << 20
+LOCAL_ROWS = 16384
+LAST_HOP = {1: 1, 2: 2, 4: 4, 6: 6, 3: 3, 5: 1, 7: 1}
+ORDER = (3, 6, 1, 4, 2, 7, 5)
+CODE = 23000.0
+
+
+def fourier_table():
+    sample_index = np.arange(WL)[:, None]
+    freq_index = np.arange(NF)[None, :]
+    phase = 2.0 * np.pi * (sample_index * freq_index % WL) / WL
+    return np.concatenate([np.cos(phase), -np.sin(phase)], axis=1).astype(ml_dtypes.bfloat16)
+
+
+def lag_table():
+    freq_index = np.arange(NF)[:, None]
+    lag_index = np.arange(LAGS)[None, :] - LAGS // 2
+    phase = 2.0 * np.pi * (freq_index * lag_index % WL) / WL
+    scale = 1.0 / math.sqrt(WL * WIN_DEV)
+    return (np.concatenate([np.cos(phase), -np.sin(phase)], axis=0) * scale).astype(
+        ml_dtypes.bfloat16
+    )
+
+
+def band_table():
+    freq_index = np.arange(NF)
+    return (np.abs(freq_index[:, None] - freq_index[None, :]) <= BAND).astype(ml_dtypes.bfloat16)
+
+
+def split_rows(row):
+    rows = []
+    for _ in range(3):
+        rows.append(row.astype(ml_dtypes.bfloat16))
+        row = row - rows[-1].astype(np.float32)
+    return rows
+
+
+def wide_table():
+    freq_index = np.arange(NF)
+    band = np.abs(freq_index[:, None] - freq_index[None, :]) <= BAND
+    taper = (0.5 - 0.5 * np.cos(2.0 * np.pi * np.arange(WL) / WL)).astype(np.float32)
+    inverse = np.zeros(WL, np.float32)
+    inverse[:NF] = 1.0 / band.sum(axis=0)
+    empty = [np.zeros(WL, ml_dtypes.bfloat16)] * 10
+    rows = np.stack(split_rows(taper) + split_rows(inverse) + empty)
+    return np.concatenate([fourier_table(), rows], axis=0)
+
+
+def filter_kernel(
+    records_hbm, channel_hbm, piece_hbm, taps_hbm, slot_hbm, starts_hbm, unit_hbm, local_hbm, *scratch
+):
+    records_ref, channel_ref, piece_ref, taps_ref, slot_ref, starts_ref = scratch[:6]
+    unit_ref, local_ref, arrived = scratch[6:]
+    f32 = jnp.float32
+    count = records_ref.shape[0]
+    size = unit_ref.shape[0]
+    pairs = (
+        (taps_hbm, taps_ref),
+        (records_hbm, records_ref),
+        (channel_hbm, channel_ref),
+        (piece_hbm, piece_ref),
+        (slot_hbm, slot_ref),
+        (starts_hbm, starts_ref),
+    )
+    copies = [
+        pltpu.make_async_copy(source, target, arrived.at[number])
+        for number, (source, target) in enumerate(pairs)
+    ]
+    for copy in copies:
+        copy.start()
+    tap = lax.broadcasted_iota(jnp.int32, (TAPS, SEG), 0)
+    sample = lax.broadcasted_iota(jnp.int32, (TAPS, SEG), 1)
+    place = (((DEC - 1 - tap) & (SEG - 1)) == sample).astype(f32).astype(jnp.bfloat16)
+    copies[0].wait()
+    taps = jnp.broadcast_to(taps_ref[...].reshape(1, TAPS), (16, TAPS))
+    first = jnp.dot(taps, place, preferred_element_type=f32)
+    circulant = pltpu.roll(
+        jnp.broadcast_to(first[0:1], (OUTS, SEG)), 0, 1, stride=DEC, stride_axis=0
+    )
+    output = lax.broadcasted_iota(jnp.int32, (OUTS, SEG), 0)
+    sample = lax.broadcasted_iota(jnp.int32, (OUTS, SEG), 1)
+    inside = sample <= DEC * output + DEC - 1
+    main_filter = jnp.where(inside, circulant, 0.0)
+    spill_filter = jnp.where(inside, 0.0, circulant)[:AUX]
+    filters = jnp.concatenate([main_filter, spill_filter], axis=0).astype(jnp.bfloat16)
+    copies[1].wait()
+    filtered = lax.dot_general(
+        filters, records_ref[...], (((1,), (1,)), ((), ())), preferred_element_type=f32
+    )
+    absolute = jnp.abs(filtered)
+    largest = jnp.maximum(jnp.max(absolute, axis=0, keepdims=True), 1e-30)
+    power = jnp.minimum(jnp.floor(jnp.log2(largest)) + 1.0, 126.0)
+    root = jnp.sqrt(jnp.sqrt(absolute * jnp.exp2(-power)))
+    code = jnp.floor(root * CODE + 0.5)
+    code = jnp.where(filtered < 0.0, -code, code)
+    main = jnp.transpose(code[:OUTS]).astype(jnp.int32)
+    local_ref[:count] = main
+    unit_ref[:count] = main.astype(jnp.int16)
+    for copy in copies[2:]:
+        copy.wait()
+    row = lax.broadcasted_iota(jnp.int32, (AUX, count), 0)
+    key = channel_ref[...].reshape(1, count) * PIECES + piece_ref[...].reshape(1, count)
+    side = jnp.where(row < SPILL, code[OUTS:].astype(jnp.int32), 0)
+    side = jnp.where(row == SCALE_ROW, power.astype(jnp.int32), side)
+    side = jnp.where(row == KEY_ROW, key, side)
+    side = jnp.where(row == SLOT_ROW, slot_ref[0], side)
+    for block in range(count // LANES):
+        to = slice(count + block * AUX, count + (block + 1) * AUX)
+        part = side[:, block * LANES : (block + 1) * LANES]
+        local_ref[to] = part
+        unit_ref[to] = part.astype(jnp.int16)
+    lane = lax.broadcasted_iota(jnp.int32, (8, OUTS), 1)
+    starts = jnp.zeros((8, OUTS), jnp.int32)
+    for window in range(WIN_DEV):
+        starts = jnp.where(lane == window, starts_ref[window], starts)
+    local_ref[size:] = starts
+    here = local_hbm.at[pl.ds(0, size + 8)]
+    out = pltpu.make_async_copy(unit_ref, unit_hbm, arrived.at[0])
+    local = pltpu.make_async_copy(local_ref, here, arrived.at[1])
+    out.start()
+    local.start()
+    out.wait()
+    local.wait()
+
+
+def halves(code):
+    first = (code >> 8).astype(jnp.float32).astype(jnp.bfloat16)
+    return first, (code & 255).astype(jnp.float32).astype(jnp.bfloat16)
+
+
+def decoded(code, scale):
+    root = code * (1.0 / CODE)
+    return (root * root) * (root * jnp.abs(root)) * scale
+
+
+def correlate_kernel(block_total, span_total, *refs):
+    units_ref = refs[1:block_total]
+    local_hbm, wide_hbm, band_hbm, lags_hbm = (refs[0],) + refs[block_total : block_total + 3]
+    keep_ref, send_ref = refs[block_total + 3 : block_total + 5]
+    pick_ref, dec_ref, seg_ref, white_ref, cross_ref, out_ref = refs[
+        block_total + 5 : block_total + 11
+    ]
+    unit_ref, starts_ref, wide_ref, band_ref, lags_ref, arrived = refs[block_total + 11 :]
+    size = unit_ref.shape[0]
+    pairs = (
+        (local_hbm.at[pl.ds(0, size)], unit_ref),
+        (local_hbm.at[pl.ds(size, 8)], starts_ref),
+        (wide_hbm, wide_ref),
+        (band_hbm, band_ref),
+        (lags_hbm, lags_ref),
+    )
+    copies = [
+        pltpu.make_async_copy(source, target, arrived.at[number])
+        for number, (source, target) in enumerate(pairs)
+    ]
+    for copy in copies:
+        copy.start()
+    f32 = jnp.float32
+    me = lax.axis_index("chan")
+    half = lax.axis_index("win")
+    rows = CH_DEV + block_total
+    count = unit_ref.shape[0] * LANES // (LANES + AUX)
+    copies[0].wait()
+    units = dict(zip(ORDER, units_ref))
+    units = [unit_ref] + [units[step] for step in range(1, block_total)]
+    side = jnp.concatenate(
+        [
+            unit[count + block * AUX : count + (block + 1) * AUX].astype(jnp.int32)
+            for unit in units
+            for block in range(count // LANES)
+        ],
+        axis=1,
+    )
+    row = lax.broadcasted_iota(jnp.int32, (2 * rows, LANES), 0)
+    odd = (row >= rows).astype(jnp.int32)
+    row = row - odd * rows
+    source = row - CH_DEV
+    channel = me * CH_DEV + row
+    for step in range(block_total):
+        slot = side[SLOT_ROW : SLOT_ROW + 1, step * count : step * count + LANES]
+        slot = jnp.broadcast_to(slot, (2 * rows, LANES))
+        channel = jnp.where(source == (me ^ step), source * CH_DEV + slot, channel)
+    wanted = channel * PIECES + odd
+    total = block_total * count
+    wanted = jnp.concatenate([wanted] * (total // LANES), axis=1)
+    key = jnp.broadcast_to(side[KEY_ROW : KEY_ROW + 1], (2 * rows, total))
+    for pair in range(PIECES // 2):
+        pick_ref[pair * 2 * rows : (pair + 1) * 2 * rows] = jnp.where(
+            wanted + 2 * pair == key, 1.0, 0.0
+        ).astype(jnp.bfloat16)
+    codes = jnp.concatenate([unit[:count].astype(jnp.int32) for unit in units], axis=0)
+    picked = jnp.dot(
+        pick_ref[...], jnp.concatenate(halves(codes), axis=1), preferred_element_type=f32
+    )
+    beside = lax.dot_general(
+        pick_ref[...],
+        jnp.concatenate(halves(side), axis=0),
+        (((1,), (1,)), ((), ())),
+        preferred_element_type=f32,
+    )
+    beside = beside[:, :AUX] * 256.0 + beside[:, AUX:]
+    scale = jnp.exp2(beside[:, SCALE_ROW : SCALE_ROW + 1])
+    main_part = decoded(picked[:, :OUTS] * 256.0 + picked[:, OUTS:], scale)
+    column = lax.broadcasted_iota(jnp.int32, beside.shape, 1)
+    spill_part = jnp.where(column < SPILL, decoded(beside, scale), 0.0)
+    for piece in range(PIECES):
+        dec_ref[:, piece * OUTS : (piece + 1) * OUTS] = main_part[
+            piece * rows : (piece + 1) * rows
+        ]
+        if piece:
+            dec_ref[:, piece * OUTS : piece * OUTS + AUX] += spill_part[
+                (piece - 1) * rows : piece * rows
+            ]
+    dec_ref[:, SPAN:] = jnp.zeros((rows, LANES), f32)
+    lane = lax.broadcasted_iota(jnp.int32, (rows, LANES), 1)
+    copies[1].wait()
+    copies[2].wait()
+    extra = wide_ref[WL:].astype(f32)
+    taper = extra[0:1] + extra[1:2] + extra[2:3]
+    inverse = (extra[3:4] + extra[4:5] + extra[5:6])[:, :NF]
+
+    def cut(window, carry):
+        start = starts_ref[0, window]
+        base = pl.multiple_of((start >> 7) * LANES, LANES)
+        offset = start & (LANES - 1)
+        shift = (LANES - offset) & (LANES - 1)
+        chunks = [
+            pltpu.roll(dec_ref[:, pl.ds(base + tile * LANES, LANES)], shift, 1)
+            for tile in range(WL // LANES + 1)
+        ]
+        here = lane < LANES - offset
+        to = pl.ds(pl.multiple_of(window * rows, 8), rows)
+        for tile in range(WL // LANES):
+            at = slice(tile * LANES, (tile + 1) * LANES)
+            seg_ref[to, at] = (
+                jnp.where(here, chunks[tile], chunks[tile + 1]) * taper[:, at]
+            )
+        return carry
+
+    lax.fori_loop(0, WIN_DEV, cut, 0)
+    spectra = jnp.dot(
+        seg_ref[...].astype(jnp.bfloat16), wide_ref[:WL], preferred_element_type=f32
+    )
+    real = spectra[:, :NF]
+    imag = spectra[:, NF:]
+    energy = real * real + imag * imag
+    high = energy.astype(jnp.bfloat16)
+    rest = energy - high.astype(f32)
+    middle = rest.astype(jnp.bfloat16)
+    low = (rest - middle.astype(f32)).astype(jnp.bfloat16)
+    copies[3].wait()
+    band = band_ref[...]
+    smooth = (
+        jnp.dot(high, band, preferred_element_type=f32)
+        + jnp.dot(middle, band, preferred_element_type=f32)
+        + jnp.dot(low, band, preferred_element_type=f32)
+    ) * inverse
+    scale = lax.rsqrt(smooth + EPSILON)
+    white_ref[:, :NF] = (real * scale).astype(jnp.bfloat16).astype(f32)
+    white_ref[:, NF:] = (imag * scale).astype(jnp.bfloat16).astype(f32)
+
+    def cross(tile, carry):
+        re = pl.ds(pl.multiple_of(tile * LANES, LANES), LANES)
+        im = pl.ds(pl.multiple_of(NF + tile * LANES, LANES), LANES)
+        real_sums = [jnp.zeros((CH_DEV, LANES), f32)] * block_total
+        imag_sums = [jnp.zeros((CH_DEV, LANES), f32)] * block_total
+        for window in range(WIN_DEV):
+            own = slice(window * rows, window * rows + CH_DEV)
+            loc_real = white_ref[own, re]
+            loc_imag = white_ref[own, im]
+            for number in range(block_total):
+                at = window * rows + CH_DEV + number
+                src_real = jnp.broadcast_to(white_ref[at : at + 1, re], (CH_DEV, LANES))
+                src_imag = jnp.broadcast_to(white_ref[at : at + 1, im], (CH_DEV, LANES))
+                real_sums[number] += src_real * loc_real + src_imag * loc_imag
+                imag_sums[number] += src_imag * loc_real - src_real * loc_imag
+        for number in range(block_total):
+            to = slice(number * CH_DEV, (number + 1) * CH_DEV)
+            cross_ref[to, re] = real_sums[number].astype(jnp.bfloat16)
+            cross_ref[to, im] = imag_sums[number].astype(jnp.bfloat16)
+        return carry
+
+    lax.fori_loop(0, NF // LANES, cross, 0)
+    copies[4].wait()
+    out_ref[...] = jnp.dot(cross_ref[...], lags_ref[...], preferred_element_type=f32)
+    part = keep_ref.shape[0]
+    keep_ref[...] = out_ref[pl.ds(pl.multiple_of(half * part, 8), part)]
+    send_ref[...] = out_ref[pl.ds(pl.multiple_of((span_total - 1 - half) * part, 8), part)]
+
+
+def gathered_body(records, record_channel, record_piece, fir_taps, window_starts, source_slot):
+    block_total = lax.axis_size("chan")
+    span_total = lax.axis_size("win")
+    vmem = pl.BlockSpec(memory_space=pltpu.VMEM)
+    hbm = pl.BlockSpec(memory_space=pl.ANY)
+    count = records.shape[0]
+    size = count + count // LANES * AUX
+    unit, local = pl.pallas_call(
+        filter_kernel,
+        out_shape=(
+            jax.ShapeDtypeStruct((size, OUTS), jnp.int16),
+            jax.ShapeDtypeStruct((LOCAL_ROWS, OUTS), jnp.int32),
+        ),
+        in_specs=[hbm] * 6,
+        out_specs=(hbm, hbm),
+        scratch_shapes=[
+            pltpu.VMEM(records.shape, records.dtype),
+            pltpu.VMEM(record_channel.shape, jnp.int32),
+            pltpu.VMEM(record_piece.shape, jnp.int32),
+            pltpu.VMEM(fir_taps.shape, fir_taps.dtype),
+            pltpu.SMEM((1,), jnp.int32),
+            pltpu.SMEM((WIN_DEV,), jnp.int32),
+            pltpu.VMEM((size, OUTS), jnp.int16),
+            pltpu.VMEM((size + 8, OUTS), jnp.int32),
+            pltpu.SemaphoreType.DMA((6,)),
+        ],
+        compiler_params=pltpu.CompilerParams(vmem_limit_bytes=FILTER_VMEM),
+        name="filter",
+    )(records, record_channel, record_piece, fir_taps, source_slot, window_starts)
+
+    def swap(value, step):
+        return lax.ppermute(value, "chan", [(i, i ^ step) for i in range(block_total)])
+
+    units = {0: unit}
+    for step, last in LAST_HOP.items():
+        units[step] = swap(units[step ^ last], last)
+    rows = CH_DEV + block_total
+    half_rows = block_total // span_total * CH_DEV
+    half_shape = jax.ShapeDtypeStruct((half_rows, LAGS), jnp.float32)
+    tables = [wide_table(), band_table(), lag_table()]
+    keep, send = pl.pallas_call(
+        lambda *refs: correlate_kernel(block_total, span_total, *refs),
+        out_shape=(half_shape, half_shape),
+        in_specs=[hbm] + [vmem] * (block_total - 1) + [hbm] * 3,
+        out_specs=(vmem, vmem),
+        scratch_shapes=[
+            pltpu.VMEM((PIECES * rows, block_total * count), jnp.bfloat16),
+            pltpu.VMEM((rows, SPAN + LANES), jnp.float32),
+            pltpu.VMEM((WIN_DEV * rows, WL), jnp.float32),
+            pltpu.VMEM((WIN_DEV * rows, WL), jnp.float32),
+            pltpu.VMEM((block_total * CH_DEV, WL), jnp.bfloat16),
+            pltpu.VMEM((block_total * CH_DEV, LAGS), jnp.float32),
+            pltpu.VMEM((size, OUTS), jnp.int32),
+            pltpu.SMEM((8, OUTS), jnp.int32),
+        ]
+        + [pltpu.VMEM(table.shape, table.dtype) for table in tables]
+        + [pltpu.SemaphoreType.DMA((5,))],
+        compiler_params=pltpu.CompilerParams(vmem_limit_bytes=CORRELATE_VMEM),
+        name="correlate",
+    )(
+        local,
+        *[units[step] for step in ORDER],
+        *[jnp.asarray(table) for table in tables],
+    )
+    other = lax.ppermute(send, "win", [(i, i ^ 1) for i in range(span_total)])
+    return (keep + other).reshape(block_total // span_total, CH_DEV, LAGS)
+
 
 def make_filter(fir_taps):
     outputs_per = SEG // DEC
@@ -93,7 +461,7 @@
     return lax.map(block_fn, grouped).reshape(source_count, channel_count, LAGS)
 
 
-def body(records, record_channel, record_piece, fir_taps, window_starts, source_slot):
+def routed_body(records, record_channel, record_piece, fir_taps, window_starts, source_slot):
     block_total = lax.axis_size("chan")
     per_device = records.shape[0]
     capacity = 2 * per_device // block_total
@@ -169,4 +537,5 @@
         P(("groups", "chan")),
     )
     out_specs = P(("groups", "win"), "chan", None)
+    body = gathered_body if mesh.shape["chan"] == 8 else routed_body
     return jax.shard_map(body, mesh=mesh, in_specs=in_specs, out_specs=out_specs, check_vma=False)

time: 140 us -> 25.6 us (0.18)
  local copies, waits for them, and re-layouts: 41.7 us -> 0 us
  blocking collectives: 30.8 us -> 0 us
  other arithmetic: 18 us -> 0.64 us
  between operations: 14.3 us -> 0.68 us
  matrix products: 12.4 us -> 0 us
  Pallas kernels: 0 us -> 7.31 us
  waiting for transfers between devices: 9 us -> 4.77 us
    all_gather x1 -> x0, blocking collectives: 30.8 us -> none  [body(): gathered = lax.all_gather(source, 'chan', axis=0, tiled=True)]
    gather x40 -> x0, local copies, waits for them, and re-layouts: 26.8 us -> none
    all_to_all x2 -> x0, starting transfers between devices: 13.2 us -> none  [the longest x1 7.25 us: body(): lax.all_to_all(slot_table, 'chan', split_axis=0, concat_axis=0, tiled=True)]
    dot_general x8 -> x0, matrix products: 12.4 us -> none  [the longest x1 2.28 us: cross_spectrum(): jnp.einsum('bwf,cwf->bcf', src_real, loc_imag, preferred_element_type=jnp...]
    ppermute x0 -> x8, starting transfers between devices: none -> 12.1 us  [the longest x7 12 us: swap(): lax.ppermute(value, 'chan', [(i, i ^ step) for i in range(block_total)])]
    another operation x3 -> x0, other arithmetic: 9.17 us -> none
    reduce_scatter x1 -> x0, waiting for transfers between devices: 7.58 us -> none  [body(): lax.psum_scatter(over_blocks(span_block, gathered, CH_DEV), 'win', scatte...]
    pallas_call x0 -> x2, Pallas kernels: none -> 7.31 us  [the longest x1 5.16 us: gathered_body(): pl.pallas_call(lambda *refs: correlate_kernel(block_total, span_total, *r...]
  transfers between devices with their start and end apart: 3 -> 8, of which waited for: 2 -> 5; matrix products, arithmetic and copies ran while one was open for 14% -> 0% of each run, Pallas kernels for 0% -> 0%
where the time goes in v1:
time: 25.6 us; the launch traced here: 25.5 us
  starting transfers between devices  12.1 us (47%)
  Pallas kernels  7.31 us (29%)
  waiting for transfers between devices  4.77 us (19%)
  between operations  0.68 us (3%)
  other arithmetic  0.64 us (2%)
    ppermute x7, starting transfers between devices, swap(): lax.ppermute(value, 'chan', [(i, i ^ step) for i in range(block_total)])  12 us
    pallas_call x1, Pallas kernels, gathered_body(): pl.pallas_call(lambda *refs: correlate_kernel(block_total, span_total, *r...  5.16 us
    ppermute x7, waiting for transfers between devices, swap(): lax.ppermute(value, 'chan', [(i, i ^ step) for i in range(block_total)])  3.53 us
    pallas_call x1, Pallas kernels, gathered_body(): pl.pallas_call(filter_kernel, out_shape=(jax.ShapeDtypeStruct((size, OUTS...  2.16 us
    ppermute x1, waiting for transfers between devices, gathered_body(): other = lax.ppermute(send, 'win', [(i, i ^ 1) for i in range(span_total)])  1.24 us
    add x1, other arithmetic, gathered_body(): return (keep + other).reshape(block_total // span_total, CH_DEV, LAGS)  0.64 us
  transfers between devices with their start and end apart: 8, of which 5 were waited for; matrix products, arithmetic and copies ran while one was open for 0% of the time, Pallas kernels for 0%

profile of v1, /device:TPU:0, one launch (start us, length us, event | category | flops | bytes accessed | tf_op | source)
XLA Modules:
  0.0 25.5 jit_solution(16174936302986902507)
XLA Ops:
  0.7 2.2 %filter.1 = (s16[288,128]{1,0:T(8,128)(2,1)}, s32[16384,128]{1,0:T(8,128)}) custom-call(bf16[256,512]{1,0:T(8,128)(2,1)} %records_hbm.1, s32[256]{0:T(256)} %channel_hbm.1, s32[256]{0:T(256)} %piece_hbm.1, bf16[32]{0:T(256)(128)(2,1)} %taps_hbm.1, s32[1]{0:T(128)S(6)} %copy.10.slot_hbm, s32[8]{0:T(128)} %starts_hbm.1), custom_call_target="tpu_custom_call" | custom-call | tf_op jit(solution)/shard_map/filter/pallas_call | solution.py:332
  2.8 4.1 %collective-permute-start.3 = (s16[288,128]{1,0:T(8,128)(2,1)}, s16[288,128]{1,0:T(8,128)(2,1)S(1)}, u32[]{:S(2)}, u32[]{:S(2)}) collective-permute-start(s16[288,128]{1,0:T(8,128)(2,1)} %get-tuple-element.10), channel_id=1, source_target_pairs={{0,8},{2,10},{4,12},{6,14},{8,0},{10,2},{12,4},{14,6},{1,9},{3,11}... | collective-permute-start | bytes 221192 | tf_op jit(solution)/shard_map/ppermute | solution.py:356
  6.9 1.4 %collective-permute-start.1 = (s16[288,128]{1,0:T(8,128)(2,1)}, s16[288,128]{1,0:T(8,128)(2,1)S(1)}, u32[]{:S(2)}, u32[]{:S(2)}) collective-permute-start(s16[288,128]{1,0:T(8,128)(2,1)} %get-tuple-element.10), channel_id=1, source_target_pairs={{0,12},{2,14},{4,8},{6,10},{8,4},{10,6},{12,0},{14,2},{1,13},{3,15... | collective-permute-start | bytes 221192 | tf_op jit(solution)/shard_map/ppermute | solution.py:356
  8.3 0.2 collective-permute-start.4
  8.5 1.5 %collective-permute-start.2 = (s16[288,128]{1,0:T(8,128)(2,1)}, s16[288,128]{1,0:T(8,128)(2,1)S(1)}, u32[]{:S(2)}, u32[]{:S(2)}) collective-permute-start(s16[288,128]{1,0:T(8,128)(2,1)} %get-tuple-element.10), channel_id=1, source_target_pairs={{0,2},{2,0},{4,6},{6,4},{8,10},{10,8},{12,14},{14,12},{1,3},{3,1},... | collective-permute-start | bytes 221192 | tf_op jit(solution)/shard_map/ppermute | solution.py:356
  10.0 1.8 %collective-permute-start = (s16[288,128]{1,0:T(8,128)(2,1)}, s16[288,128]{1,0:T(8,128)(2,1)S(1)}, u32[]{:S(2)}, u32[]{:S(2)}) collective-permute-start(s16[288,128]{1,0:T(8,128)(2,1)} %get-tuple-element.10), channel_id=1, source_target_pairs={{0,6},{2,4},{4,2},{6,0},{8,14},{10,12},{12,10},{14,8},{1,7},{3,5},... | collective-permute-start | bytes 221192 | tf_op jit(solution)/shard_map/ppermute | solution.py:356
  11.8 0.2 collective-permute-done.3.refs_4_
  12.0 2.0 %collective-permute-start.6 = (s16[288,128]{1,0:T(8,128)(2,1)S(1)}, s16[288,128]{1,0:T(8,128)(2,1)S(1)}, u32[]{:S(2)}, u32[]{:S(2)}) collective-permute-start(s16[288,128]{1,0:T(8,128)(2,1)S(1)} %collective-permute-done.3.refs_4_), channel_id=1, source_target_pairs={{0,2},{2,0},{4,6},{6,4},{8,10},{10,8},{12,14},{14,12},{1,3},{3,1},... | collective-permute-start | bytes 221192 | tf_op jit(solution)/shard_map/ppermute | solution.py:356
  14.0 0.0 collective-permute-done.1.refs_2_
  14.0 1.1 %collective-permute-start.5 = (s16[288,128]{1,0:T(8,128)(2,1)S(1)}, s16[288,128]{1,0:T(8,128)(2,1)S(1)}, u32[]{:S(2)}, u32[]{:S(2)}) collective-permute-start(s16[288,128]{1,0:T(8,128)(2,1)S(1)} %collective-permute-done.1.refs_2_), channel_id=1, source_target_pairs={{0,2},{2,0},{4,6},{6,4},{8,10},{10,8},{12,14},{14,12},{1,3},{3,1},... | collective-permute-start | bytes 221192 | tf_op jit(solution)/shard_map/ppermute | solution.py:356
  15.0 0.0 collective-permute-done.4.refs_5_
  15.0 0.0 collective-permute-done.2.refs_3_
  15.1 1.5 %collective-permute-done.refs_1_ = s16[288,128]{1,0:T(8,128)(2,1)S(1)} collective-permute-done((s16[288,128]{1,0:T(8,128)(2,1)}, s16[288,128]{1,0:T(8,128)(2,1)S(1)}, u32[]{:S(2)}, u32[]{:S(2)}) %collective-permute-start) | collective-permute-done | bytes 73760 | tf_op jit(solution)/shard_map/ppermute | solution.py:356
  16.6 0.7 %collective-permute-done.6.refs_7_ = s16[288,128]{1,0:T(8,128)(2,1)S(1)} collective-permute-done((s16[288,128]{1,0:T(8,128)(2,1)S(1)}, s16[288,128]{1,0:T(8,128)(2,1)S(1)}, u32[]{:S(2)}, u32[]{:S(2)}) %collective-permute-start.6) | collective-permute-done | bytes 73760 | tf_op jit(solution)/shard_map/ppermute | solution.py:356
  17.3 1.0 %collective-permute-done.5.refs_6_ = s16[288,128]{1,0:T(8,128)(2,1)S(1)} collective-permute-done((s16[288,128]{1,0:T(8,128)(2,1)S(1)}, s16[288,128]{1,0:T(8,128)(2,1)S(1)}, u32[]{:S(2)}, u32[]{:S(2)}) %collective-permute-start.5) | collective-permute-done | bytes 73760 | tf_op jit(solution)/shard_map/ppermute | solution.py:356
  18.3 5.2 %correlate.1 = (f32[64,256]{1,0:T(8,128)S(1)}, f32[64,256]{1,0:T(8,128)S(1)}) custom-call(s32[16384,128]{1,0:T(8,128)} %get-tuple-element.9.refs_0_, s16[288,128]{1,0:T(8,128)(2,1)S(1)} %collective-permute-done.refs_1_, s16[288,128]{1,0:T(8,128)(2,1)S(1)} %collective-permute-done.1.refs_2_, s16[288,128]{1,0:T(8,128)(2,1)S(1)} %collective-permute-done.2.refs_3_, ...), custom_call_target="tpu_custom_call" | custom-call | tf_op jit(solution)/shard_map/correlate/pallas_call | solution.py:365
  23.5 0.1 collective-permute-start.7
  23.6 1.2 %collective-permute-done.7 = f32[64,256]{1,0:T(8,128)S(1)} collective-permute-done((f32[64,256]{1,0:T(8,128)S(1)}, f32[64,256]{1,0:T(8,128)S(1)}, u32[]{:S(2)}, u32[]{:S(2)}) %collective-permute-start.7) | collective-permute-done | bytes 65568 | tf_op jit(solution)/shard_map/ppermute | solution.py:389
  24.8 0.6 %add.3 = f32[64,256]{1,0:T(8,128)} add(f32[64,256]{1,0:T(8,128)S(1)} %get-tuple-element.11, f32[64,256]{1,0:T(8,128)S(1)} %collective-permute-done.7) | non-fusion elementwise | flops 16384 | bytes 196608 | tf_op jit(solution)/shard_map/add | solution.py:390
Async XLA Ops:
  2.8 9.2 %collective-permute-start.3 = (s16[288,128]{1,0:T(8,128)(2,1)}, s16[288,128]{1,0:T(8,128)(2,1)S(1)}, u32[]{:S(2)}, u32[]{:S(2)}) collective-permute-start(s16[288,128]{1,0:T(8,128)(2,1)} %get-tuple-element.10), channel_id=1, source_target_pairs={{0,8},{2,10},{4,12},{6,14},{8,0},{10,2},{12,4},{14,6},{1,9},{3,11}... | collective-permute-start | bytes 221192 | tf_op jit(solution)/shard_map/ppermute | solution.py:356
  6.9 7.1 %collective-permute-start.1 = (s16[288,128]{1,0:T(8,128)(2,1)}, s16[288,128]{1,0:T(8,128)(2,1)S(1)}, u32[]{:S(2)}, u32[]{:S(2)}) collective-permute-start(s16[288,128]{1,0:T(8,128)(2,1)} %get-tuple-element.10), channel_id=1, source_target_pairs={{0,12},{2,14},{4,8},{6,10},{8,4},{10,6},{12,0},{14,2},{1,13},{3,15... | collective-permute-start | bytes 221192 | tf_op jit(solution)/shard_map/ppermute | solution.py:356
  8.3 6.8 %collective-permute-start.4 = (s16[288,128]{1,0:T(8,128)(2,1)}, s16[288,128]{1,0:T(8,128)(2,1)S(1)}, u32[]{:S(2)}, u32[]{:S(2)}) collective-permute-start(s16[288,128]{1,0:T(8,128)(2,1)} %get-tuple-element.10), channel_id=1, source_target_pairs={{0,4},{2,6},{4,0},{6,2},{8,12},{10,14},{12,8},{14,10},{1,5},{3,7},... | collective-permute-start | bytes 221192 | tf_op jit(solution)/shard_map/ppermute | solution.py:356
  8.5 6.6 %collective-permute-start.2 = (s16[288,128]{1,0:T(8,128)(2,1)}, s16[288,128]{1,0:T(8,128)(2,1)S(1)}, u32[]{:S(2)}, u32[]{:S(2)}) collective-permute-start(s16[288,128]{1,0:T(8,128)(2,1)} %get-tuple-element.10), channel_id=1, source_target_pairs={{0,2},{2,0},{4,6},{6,4},{8,10},{10,8},{12,14},{14,12},{1,3},{3,1},... | collective-permute-start | bytes 221192 | tf_op jit(solution)/shard_map/ppermute | solution.py:356
  10.0 6.6 %collective-permute-start = (s16[288,128]{1,0:T(8,128)(2,1)}, s16[288,128]{1,0:T(8,128)(2,1)S(1)}, u32[]{:S(2)}, u32[]{:S(2)}) collective-permute-start(s16[288,128]{1,0:T(8,128)(2,1)} %get-tuple-element.10), channel_id=1, source_target_pairs={{0,6},{2,4},{4,2},{6,0},{8,14},{10,12},{12,10},{14,8},{1,7},{3,5},... | collective-permute-start | bytes 221192 | tf_op jit(solution)/shard_map/ppermute | solution.py:356
  12.0 5.3 %collective-permute-start.6 = (s16[288,128]{1,0:T(8,128)(2,1)S(1)}, s16[288,128]{1,0:T(8,128)(2,1)S(1)}, u32[]{:S(2)}, u32[]{:S(2)}) collective-permute-start(s16[288,128]{1,0:T(8,128)(2,1)S(1)} %collective-permute-done.3.refs_4_), channel_id=1, source_target_pairs={{0,2},{2,0},{4,6},{6,4},{8,10},{10,8},{12,14},{14,12},{1,3},{3,1},... | collective-permute-start | bytes 221192 | tf_op jit(solution)/shard_map/ppermute | solution.py:356
  14.0 4.4 %collective-permute-start.5 = (s16[288,128]{1,0:T(8,128)(2,1)S(1)}, s16[288,128]{1,0:T(8,128)(2,1)S(1)}, u32[]{:S(2)}, u32[]{:S(2)}) collective-permute-start(s16[288,128]{1,0:T(8,128)(2,1)S(1)} %collective-permute-done.1.refs_2_), channel_id=1, source_target_pairs={{0,2},{2,0},{4,6},{6,4},{8,10},{10,8},{12,14},{14,12},{1,3},{3,1},... | collective-permute-start | bytes 221192 | tf_op jit(solution)/shard_map/ppermute | solution.py:356
  23.5 1.3 %collective-permute-start.7 = (f32[64,256]{1,0:T(8,128)S(1)}, f32[64,256]{1,0:T(8,128)S(1)}, u32[]{:S(2)}, u32[]{:S(2)}) collective-permute-start(f32[64,256]{1,0:T(8,128)S(1)} %get-tuple-element.12), channel_id=1, source_target_pairs={{0,1},{1,0},{2,3},{3,2},{4,5},{5,4},{6,7},{7,6},{8,9},{9,8},{10,11... | collective-permute-start | bytes 196616 | tf_op jit(solution)/shard_map/ppermute | solution.py:389

commit v2 on v1

--- a/solution.py
+++ b/solution.py
@@ -31,8 +31,9 @@
 SCALE_ROW = SPILL
 KEY_ROW = SPILL + 1
 SLOT_ROW = SPILL + 2
-FILTER_VMEM = 62 << 20
-CORRELATE_VMEM = 53 << 20
+FILTER_VMEM = 56 << 20
+FLOPS = 10**10
+CORRELATE_VMEM = 50 << 20
 LOCAL_ROWS = 16384
 LAST_HOP = {1: 1, 2: 2, 4: 4, 6: 6, 3: 3, 5: 1, 7: 1}
 ORDER = (3, 6, 1, 4, 2, 7, 5)
@@ -51,9 +52,9 @@
     lag_index = np.arange(LAGS)[None, :] - LAGS // 2
     phase = 2.0 * np.pi * (freq_index * lag_index % WL) / WL
     scale = 1.0 / math.sqrt(WL * WIN_DEV)
-    return (np.concatenate([np.cos(phase), -np.sin(phase)], axis=0) * scale).astype(
-        ml_dtypes.bfloat16
-    )
+    tiles = (NF // LANES, 1, LANES, LAGS)
+    parts = [np.cos(phase).reshape(tiles), -np.sin(phase).reshape(tiles)]
+    return (np.concatenate(parts, axis=1).reshape(2 * NF, LAGS) * scale).astype(ml_dtypes.bfloat16)
 
 
 def band_table():
@@ -168,20 +169,17 @@
 
 
 def correlate_kernel(block_total, span_total, *refs):
-    units_ref = refs[1:block_total]
-    local_hbm, wide_hbm, band_hbm, lags_hbm = (refs[0],) + refs[block_total : block_total + 3]
-    keep_ref, send_ref = refs[block_total + 3 : block_total + 5]
-    pick_ref, dec_ref, seg_ref, white_ref, cross_ref, out_ref = refs[
-        block_total + 5 : block_total + 11
+    local_hbm, slot_ref = refs[:2]
+    units_ref = dict(zip(ORDER, refs[2 : block_total + 1]))
+    wide_ref, band_ref, lags_ref, keep_ref, send_ref = refs[block_total + 1 : block_total + 6]
+    pick_ref, dec_ref, seg_ref, white_ref, out_ref, unit_ref, starts_ref, arrived = refs[
+        block_total + 6 :
     ]
-    unit_ref, starts_ref, wide_ref, band_ref, lags_ref, arrived = refs[block_total + 11 :]
+    f32 = jnp.float32
     size = unit_ref.shape[0]
     pairs = (
         (local_hbm.at[pl.ds(0, size)], unit_ref),
         (local_hbm.at[pl.ds(size, 8)], starts_ref),
-        (wide_hbm, wide_ref),
-        (band_hbm, band_ref),
-        (lags_hbm, lags_ref),
     )
     copies = [
         pltpu.make_async_copy(source, target, arrived.at[number])
@@ -189,43 +187,46 @@
     ]
     for copy in copies:
         copy.start()
-    f32 = jnp.float32
     me = lax.axis_index("chan")
     half = lax.axis_index("win")
     rows = CH_DEV + block_total
-    count = unit_ref.shape[0] * LANES // (LANES + AUX)
-    copies[0].wait()
-    units = dict(zip(ORDER, units_ref))
-    units = [unit_ref] + [units[step] for step in range(1, block_total)]
-    side = jnp.concatenate(
-        [
-            unit[count + block * AUX : count + (block + 1) * AUX].astype(jnp.int32)
-            for unit in units
-            for block in range(count // LANES)
-        ],
-        axis=1,
-    )
-    row = lax.broadcasted_iota(jnp.int32, (2 * rows, LANES), 0)
+    count = size * LANES // (LANES + AUX)
+
+    def side_of(unit):
+        blocks = range(count // LANES)
+        parts = [unit[count + block * AUX : count + (block + 1) * AUX] for block in blocks]
+        return jnp.concatenate([part.astype(jnp.int32) for part in parts], axis=1)
+
+    sides = {step: side_of(unit) for step, unit in units_ref.items()}
+    row = lax.broadcasted_iota(jnp.int32, (2 * rows, count), 0)
     odd = (row >= rows).astype(jnp.int32)
     row = row - odd * rows
     source = row - CH_DEV
     channel = me * CH_DEV + row
-    for step in range(block_total):
-        slot = side[SLOT_ROW : SLOT_ROW + 1, step * count : step * count + LANES]
-        slot = jnp.broadcast_to(slot, (2 * rows, LANES))
+    channel = jnp.where(source == me, source * CH_DEV + slot_ref[0], channel)
+    for step, side in sides.items():
+        slot = jnp.broadcast_to(side[SLOT_ROW : SLOT_ROW + 1], (2 * rows, count))
         channel = jnp.where(source == (me ^ step), source * CH_DEV + slot, channel)
     wanted = channel * PIECES + odd
-    total = block_total * count
-    wanted = jnp.concatenate([wanted] * (total // LANES), axis=1)
-    key = jnp.broadcast_to(side[KEY_ROW : KEY_ROW + 1], (2 * rows, total))
-    for pair in range(PIECES // 2):
-        pick_ref[pair * 2 * rows : (pair + 1) * 2 * rows] = jnp.where(
-            wanted + 2 * pair == key, 1.0, 0.0
-        ).astype(jnp.bfloat16)
+
+    def pick(step, side):
+        key = jnp.broadcast_to(side[KEY_ROW : KEY_ROW + 1], (2 * rows, count))
+        for pair in range(PIECES // 2):
+            pick_ref[
+                pair * 2 * rows : (pair + 1) * 2 * rows, step * count : (step + 1) * count
+            ] = jnp.where(wanted + 2 * pair == key, 1.0, 0.0).astype(jnp.bfloat16)
+
+    for step in range(1, block_total):
+        pick(step, sides[step])
+    copies[0].wait()
+    sides[0] = side_of(unit_ref)
+    pick(0, sides[0])
+    units = [unit_ref] + [units_ref[step] for step in range(1, block_total)]
     codes = jnp.concatenate([unit[:count].astype(jnp.int32) for unit in units], axis=0)
     picked = jnp.dot(
         pick_ref[...], jnp.concatenate(halves(codes), axis=1), preferred_element_type=f32
     )
+    side = jnp.concatenate([sides[step] for step in range(block_total)], axis=1)
     beside = lax.dot_general(
         pick_ref[...],
         jnp.concatenate(halves(side), axis=0),
@@ -247,13 +248,11 @@
             ]
     dec_ref[:, SPAN:] = jnp.zeros((rows, LANES), f32)
     lane = lax.broadcasted_iota(jnp.int32, (rows, LANES), 1)
-    copies[1].wait()
-    copies[2].wait()
     extra = wide_ref[WL:].astype(f32)
     taper = extra[0:1] + extra[1:2] + extra[2:3]
     inverse = (extra[3:4] + extra[4:5] + extra[5:6])[:, :NF]
-
-    def cut(window, carry):
+    copies[1].wait()
+    for window in range(WIN_DEV):
         start = starts_ref[0, window]
         base = pl.multiple_of((start >> 7) * LANES, LANES)
         offset = start & (LANES - 1)
@@ -263,15 +262,11 @@
             for tile in range(WL // LANES + 1)
         ]
         here = lane < LANES - offset
-        to = pl.ds(pl.multiple_of(window * rows, 8), rows)
         for tile in range(WL // LANES):
             at = slice(tile * LANES, (tile + 1) * LANES)
-            seg_ref[to, at] = (
+            seg_ref[window * rows : (window + 1) * rows, at] = (
                 jnp.where(here, chunks[tile], chunks[tile + 1]) * taper[:, at]
             )
-        return carry
-
-    lax.fori_loop(0, WIN_DEV, cut, 0)
     spectra = jnp.dot(
         seg_ref[...].astype(jnp.bfloat16), wide_ref[:WL], preferred_element_type=f32
     )
@@ -282,7 +277,6 @@
     rest = energy - high.astype(f32)
     middle = rest.astype(jnp.bfloat16)
     low = (rest - middle.astype(f32)).astype(jnp.bfloat16)
-    copies[3].wait()
     band = band_ref[...]
     smooth = (
         jnp.dot(high, band, preferred_element_type=f32)
@@ -292,10 +286,10 @@
     scale = lax.rsqrt(smooth + EPSILON)
     white_ref[:, :NF] = (real * scale).astype(jnp.bfloat16).astype(f32)
     white_ref[:, NF:] = (imag * scale).astype(jnp.bfloat16).astype(f32)
-
-    def cross(tile, carry):
-        re = pl.ds(pl.multiple_of(tile * LANES, LANES), LANES)
-        im = pl.ds(pl.multiple_of(NF + tile * LANES, LANES), LANES)
+    total = jnp.zeros((block_total * CH_DEV, LAGS), f32)
+    for tile in range(NF // LANES):
+        re = slice(tile * LANES, (tile + 1) * LANES)
+        im = slice(NF + tile * LANES, NF + (tile + 1) * LANES)
         real_sums = [jnp.zeros((CH_DEV, LANES), f32)] * block_total
         imag_sums = [jnp.zeros((CH_DEV, LANES), f32)] * block_total
         for window in range(WIN_DEV):
@@ -308,15 +302,19 @@
                 src_imag = jnp.broadcast_to(white_ref[at : at + 1, im], (CH_DEV, LANES))
                 real_sums[number] += src_real * loc_real + src_imag * loc_imag
                 imag_sums[number] += src_imag * loc_real - src_real * loc_imag
-        for number in range(block_total):
-            to = slice(number * CH_DEV, (number + 1) * CH_DEV)
-            cross_ref[to, re] = real_sums[number].astype(jnp.bfloat16)
-            cross_ref[to, im] = imag_sums[number].astype(jnp.bfloat16)
-        return carry
-
-    lax.fori_loop(0, NF // LANES, cross, 0)
-    copies[4].wait()
-    out_ref[...] = jnp.dot(cross_ref[...], lags_ref[...], preferred_element_type=f32)
+        cross = jnp.concatenate(
+            [
+                jnp.concatenate(real_sums, axis=0).astype(jnp.bfloat16),
+                jnp.concatenate(imag_sums, axis=0).astype(jnp.bfloat16),
+            ],
+            axis=1,
+        )
+        total += jnp.dot(
+            cross,
+            lags_ref[2 * tile * LANES : 2 * (tile + 1) * LANES],
+            preferred_element_type=f32,
+        )
+    out_ref[...] = total
     part = keep_ref.shape[0]
     keep_ref[...] = out_ref[pl.ds(pl.multiple_of(half * part, 8), part)]
     send_ref[...] = out_ref[pl.ds(pl.multiple_of((span_total - 1 - half) * part, 8), part)]
@@ -326,6 +324,7 @@
     block_total = lax.axis_size("chan")
     span_total = lax.axis_size("win")
     vmem = pl.BlockSpec(memory_space=pltpu.VMEM)
+    smem = pl.BlockSpec(memory_space=pltpu.SMEM)
     hbm = pl.BlockSpec(memory_space=pl.ANY)
     count = records.shape[0]
     size = count + count // LANES * AUX
@@ -349,6 +348,7 @@
             pltpu.SemaphoreType.DMA((6,)),
         ],
         compiler_params=pltpu.CompilerParams(vmem_limit_bytes=FILTER_VMEM),
+        cost_estimate=pl.CostEstimate(flops=FLOPS, bytes_accessed=1 << 20, transcendentals=0),
         name="filter",
     )(records, record_channel, record_piece, fir_taps, source_slot, window_starts)
 
@@ -365,24 +365,23 @@
     keep, send = pl.pallas_call(
         lambda *refs: correlate_kernel(block_total, span_total, *refs),
         out_shape=(half_shape, half_shape),
-        in_specs=[hbm] + [vmem] * (block_total - 1) + [hbm] * 3,
+        in_specs=[hbm, smem] + [vmem] * (block_total + 2),
         out_specs=(vmem, vmem),
         scratch_shapes=[
             pltpu.VMEM((PIECES * rows, block_total * count), jnp.bfloat16),
             pltpu.VMEM((rows, SPAN + LANES), jnp.float32),
             pltpu.VMEM((WIN_DEV * rows, WL), jnp.float32),
             pltpu.VMEM((WIN_DEV * rows, WL), jnp.float32),
-            pltpu.VMEM((block_total * CH_DEV, WL), jnp.bfloat16),
             pltpu.VMEM((block_total * CH_DEV, LAGS), jnp.float32),
             pltpu.VMEM((size, OUTS), jnp.int32),
             pltpu.SMEM((8, OUTS), jnp.int32),
-        ]
-        + [pltpu.VMEM(table.shape, table.dtype) for table in tables]
-        + [pltpu.SemaphoreType.DMA((5,))],
+            pltpu.SemaphoreType.DMA((2,)),
+        ],
         compiler_params=pltpu.CompilerParams(vmem_limit_bytes=CORRELATE_VMEM),
         name="correlate",
     )(
         local,
+        source_slot,
         *[units[step] for step in ORDER],
         *[jnp.asarray(table) for table in tables],
     )

time: 25.6 us -> 24.8 us (0.969)
  Pallas kernels: 7.31 us -> 6.44 us
    pallas_call x1, Pallas kernels: 5.16 us -> 4.1 us  [gathered_body(): pl.pallas_call(lambda *refs: correlate_kernel(block_total, span_total, *r...]
where the time goes in v2:
time: 24.8 us; the launch traced here: 24.6 us
  starting transfers between devices  12.1 us (49%)
  Pallas kernels  6.44 us (26%)
  waiting for transfers between devices  4.78 us (19%)
  between operations  0.71 us (3%)
  other arithmetic  0.64 us (3%)
    ppermute x7, starting transfers between devices, swap(): lax.ppermute(value, 'chan', [(i, i ^ step) for i in range(block_total)])  12 us
    pallas_call x1, Pallas kernels, gathered_body(): pl.pallas_call(lambda *refs: correlate_kernel(block_total, span_total, *r...  4.1 us
    ppermute x7, waiting for transfers between devices, swap(): lax.ppermute(value, 'chan', [(i, i ^ step) for i in range(block_total)])  3.54 us
    pallas_call x1, Pallas kernels, gathered_body(): pl.pallas_call(filter_kernel, out_shape=(jax.ShapeDtypeStruct((size, OUTS...  2.34 us
    ppermute x1, waiting for transfers between devices, gathered_body(): other = lax.ppermute(send, 'win', [(i, i ^ 1) for i in range(span_total)])  1.24 us
    add x1, other arithmetic, gathered_body(): return (keep + other).reshape(block_total // span_total, CH_DEV, LAGS)  0.64 us
  transfers between devices with their start and end apart: 8, of which 5 were waited for; matrix products, arithmetic and copies ran while one was open for 0% of the time, Pallas kernels for 0%

profile of v2, /device:TPU:0, one launch (start us, length us, event | category | flops | bytes accessed | tf_op | source)
XLA Modules:
  0.0 24.6 jit_solution(10442073693345275221)
XLA Ops:
  0.7 0.0 copy-start
  0.7 0.0 copy-start.1
  0.7 0.0 copy-start.2
  0.7 2.3 %filter.1 = (s16[288,128]{1,0:T(8,128)(2,1)}, s32[16384,128]{1,0:T(8,128)}) custom-call(bf16[256,512]{1,0:T(8,128)(2,1)} %records_hbm.1, s32[256]{0:T(256)} %channel_hbm.1, s32[256]{0:T(256)} %piece_hbm.1, bf16[32]{0:T(256)(128)(2,1)} %taps_hbm.1, s32[1]{0:T(128)S(6)} %copy.10.slot_hbm.refs_1_, s32[8]{0:T(128)} %starts_hbm.1), custom_call_target="tpu_custom_call" | custom-call | flops 10000000000 | bytes 1048576 | tf_op jit(solution)/shard_map/filter/pallas_call | solution.py:331
  3.0 4.1 %collective-permute-start.3 = (s16[288,128]{1,0:T(8,128)(2,1)}, s16[288,128]{1,0:T(8,128)(2,1)S(1)}, u32[]{:S(2)}, u32[]{:S(2)}) collective-permute-start(s16[288,128]{1,0:T(8,128)(2,1)} %get-tuple-element.10), channel_id=1, source_target_pairs={{0,8},{2,10},{4,12},{6,14},{8,0},{10,2},{12,4},{14,6},{1,9},{3,11}... | collective-permute-start | bytes 221192 | tf_op jit(solution)/shard_map/ppermute | solution.py:356
  7.1 1.3 %collective-permute-start.1 = (s16[288,128]{1,0:T(8,128)(2,1)}, s16[288,128]{1,0:T(8,128)(2,1)S(1)}, u32[]{:S(2)}, u32[]{:S(2)}) collective-permute-start(s16[288,128]{1,0:T(8,128)(2,1)} %get-tuple-element.10), channel_id=1, source_target_pairs={{0,12},{2,14},{4,8},{6,10},{8,4},{10,6},{12,0},{14,2},{1,13},{3,15... | collective-permute-start | bytes 221192 | tf_op jit(solution)/shard_map/ppermute | solution.py:356
  8.5 0.2 collective-permute-start.4
  8.7 1.5 %collective-permute-start.2 = (s16[288,128]{1,0:T(8,128)(2,1)}, s16[288,128]{1,0:T(8,128)(2,1)S(1)}, u32[]{:S(2)}, u32[]{:S(2)}) collective-permute-start(s16[288,128]{1,0:T(8,128)(2,1)} %get-tuple-element.10), channel_id=1, source_target_pairs={{0,2},{2,0},{4,6},{6,4},{8,10},{10,8},{12,14},{14,12},{1,3},{3,1},... | collective-permute-start | bytes 221192 | tf_op jit(solution)/shard_map/ppermute | solution.py:356
  10.2 1.8 %collective-permute-start = (s16[288,128]{1,0:T(8,128)(2,1)}, s16[288,128]{1,0:T(8,128)(2,1)S(1)}, u32[]{:S(2)}, u32[]{:S(2)}) collective-permute-start(s16[288,128]{1,0:T(8,128)(2,1)} %get-tuple-element.10), channel_id=1, source_target_pairs={{0,6},{2,4},{4,2},{6,0},{8,14},{10,12},{12,10},{14,8},{1,7},{3,5},... | collective-permute-start | bytes 221192 | tf_op jit(solution)/shard_map/ppermute | solution.py:356
  12.0 0.2 %collective-permute-done.3.refs_5_ = s16[288,128]{1,0:T(8,128)(2,1)S(1)} collective-permute-done((s16[288,128]{1,0:T(8,128)(2,1)}, s16[288,128]{1,0:T(8,128)(2,1)S(1)}, u32[]{:S(2)}, u32[]{:S(2)}) %collective-permute-start.3) | collective-permute-done | bytes 73760 | tf_op jit(solution)/shard_map/ppermute | solution.py:356
  12.2 2.0 %collective-permute-start.6 = (s16[288,128]{1,0:T(8,128)(2,1)S(1)}, s16[288,128]{1,0:T(8,128)(2,1)S(1)}, u32[]{:S(2)}, u32[]{:S(2)}) collective-permute-start(s16[288,128]{1,0:T(8,128)(2,1)S(1)} %collective-permute-done.3.refs_5_), channel_id=1, source_target_pairs={{0,2},{2,0},{4,6},{6,4},{8,10},{10,8},{12,14},{14,12},{1,3},{3,1},... | collective-permute-start | bytes 221192 | tf_op jit(solution)/shard_map/ppermute | solution.py:356
  14.2 0.0 collective-permute-done.1.refs_3_
  14.2 1.1 %collective-permute-start.5 = (s16[288,128]{1,0:T(8,128)(2,1)S(1)}, s16[288,128]{1,0:T(8,128)(2,1)S(1)}, u32[]{:S(2)}, u32[]{:S(2)}) collective-permute-start(s16[288,128]{1,0:T(8,128)(2,1)S(1)} %collective-permute-done.1.refs_3_), channel_id=1, source_target_pairs={{0,2},{2,0},{4,6},{6,4},{8,10},{10,8},{12,14},{14,12},{1,3},{3,1},... | collective-permute-start | bytes 221192 | tf_op jit(solution)/shard_map/ppermute | solution.py:356
  15.3 0.0 collective-permute-done.4.refs_6_
  15.3 0.0 collective-permute-done.2.refs_4_
  15.3 1.5 %collective-permute-done.refs_2_ = s16[288,128]{1,0:T(8,128)(2,1)S(1)} collective-permute-done((s16[288,128]{1,0:T(8,128)(2,1)}, s16[288,128]{1,0:T(8,128)(2,1)S(1)}, u32[]{:S(2)}, u32[]{:S(2)}) %collective-permute-start) | collective-permute-done | bytes 73760 | tf_op jit(solution)/shard_map/ppermute | solution.py:356
  16.8 0.7 %collective-permute-done.6.refs_8_ = s16[288,128]{1,0:T(8,128)(2,1)S(1)} collective-permute-done((s16[288,128]{1,0:T(8,128)(2,1)S(1)}, s16[288,128]{1,0:T(8,128)(2,1)S(1)}, u32[]{:S(2)}, u32[]{:S(2)}) %collective-permute-start.6) | collective-permute-done | bytes 73760 | tf_op jit(solution)/shard_map/ppermute | solution.py:356
  17.6 1.0 %collective-permute-done.5.refs_7_ = s16[288,128]{1,0:T(8,128)(2,1)S(1)} collective-permute-done((s16[288,128]{1,0:T(8,128)(2,1)S(1)}, s16[288,128]{1,0:T(8,128)(2,1)S(1)}, u32[]{:S(2)}, u32[]{:S(2)}) %collective-permute-start.5) | collective-permute-done | bytes 73760 | tf_op jit(solution)/shard_map/ppermute | solution.py:356
  18.6 0.0 copy-done
  18.6 0.0 copy-done.1
  18.6 0.0 copy-done.2
  18.6 4.1 %correlate.1 = (f32[64,256]{1,0:T(8,128)S(1)}, f32[64,256]{1,0:T(8,128)S(1)}) custom-call(s32[16384,128]{1,0:T(8,128)} %get-tuple-element.9.refs_0_, s32[1]{0:T(128)S(6)} %copy.10.slot_hbm.refs_1_, s16[288,128]{1,0:T(8,128)(2,1)S(1)} %collective-permute-done.refs_2_, s16[288,128]{1,0:T(8,128)(2,1)S(1)} %collective-permute-done.1.refs_3_, ...), custom_call_target="tpu_custom_call" | custom-call | tf_op jit(solution)/shard_map/correlate/pallas_call | solution.py:365
  22.7 0.1 collective-permute-start.7
  22.8 1.2 %collective-permute-done.7 = f32[64,256]{1,0:T(8,128)S(1)} collective-permute-done((f32[64,256]{1,0:T(8,128)S(1)}, f32[64,256]{1,0:T(8,128)S(1)}, u32[]{:S(2)}, u32[]{:S(2)}) %collective-permute-start.7) | collective-permute-done | bytes 65568 | tf_op jit(solution)/shard_map/ppermute | solution.py:388
  24.0 0.6 %add.3 = f32[64,256]{1,0:T(8,128)} add(f32[64,256]{1,0:T(8,128)S(1)} %get-tuple-element.11, f32[64,256]{1,0:T(8,128)S(1)} %collective-permute-done.7) | non-fusion elementwise | flops 16384 | bytes 196608 | tf_op jit(solution)/shard_map/add | solution.py:389
Async XLA Ops:
  0.7 17.9 %copy-start = (bf16[1040,1024]{1,0:T(8,128)(2,1)S(1)}, bf16[1040,1024]{1,0:T(8,128)(2,1)}, u32[]{:S(2)}) copy-start(bf16[1040,1024]{1,0:T(8,128)(2,1)} %constant.6.clone.refs_9_) | copy-start | bytes 6389764
  0.7 17.9 %copy-start.1 = (bf16[1024,256]{1,0:T(8,128)(2,1)S(1)}, bf16[1024,256]{1,0:T(8,128)(2,1)}, u32[]{:S(2)}) copy-start(bf16[1024,256]{1,0:T(8,128)(2,1)} %constant.8.clone.refs_11_) | copy-start | bytes 1572868
  0.7 17.9 %copy-start.2 = (bf16[512,512]{1,0:T(8,128)(2,1)S(1)}, bf16[512,512]{1,0:T(8,128)(2,1)}, u32[]{:S(2)}) copy-start(bf16[512,512]{1,0:T(8,128)(2,1)} %constant.7.clone.refs_10_) | copy-start | bytes 1572868
  3.0 9.2 %collective-permute-start.3 = (s16[288,128]{1,0:T(8,128)(2,1)}, s16[288,128]{1,0:T(8,128)(2,1)S(1)}, u32[]{:S(2)}, u32[]{:S(2)}) collective-permute-start(s16[288,128]{1,0:T(8,128)(2,1)} %get-tuple-element.10), channel_id=1, source_target_pairs={{0,8},{2,10},{4,12},{6,14},{8,0},{10,2},{12,4},{14,6},{1,9},{3,11}... | collective-permute-start | bytes 221192 | tf_op jit(solution)/shard_map/ppermute | solution.py:356
  7.1 7.1 %collective-permute-start.1 = (s16[288,128]{1,0:T(8,128)(2,1)}, s16[288,128]{1,0:T(8,128)(2,1)S(1)}, u32[]{:S(2)}, u32[]{:S(2)}) collective-permute-start(s16[288,128]{1,0:T(8,128)(2,1)} %get-tuple-element.10), channel_id=1, source_target_pairs={{0,12},{2,14},{4,8},{6,10},{8,4},{10,6},{12,0},{14,2},{1,13},{3,15... | collective-permute-start | bytes 221192 | tf_op jit(solution)/shard_map/ppermute | solution.py:356
  8.5 6.8 %collective-permute-start.4 = (s16[288,128]{1,0:T(8,128)(2,1)}, s16[288,128]{1,0:T(8,128)(2,1)S(1)}, u32[]{:S(2)}, u32[]{:S(2)}) collective-permute-start(s16[288,128]{1,0:T(8,128)(2,1)} %get-tuple-element.10), channel_id=1, source_target_pairs={{0,4},{2,6},{4,0},{6,2},{8,12},{10,14},{12,8},{14,10},{1,5},{3,7},... | collective-permute-start | bytes 221192 | tf_op jit(solution)/shard_map/ppermute | solution.py:356
  8.7 6.6 %collective-permute-start.2 = (s16[288,128]{1,0:T(8,128)(2,1)}, s16[288,128]{1,0:T(8,128)(2,1)S(1)}, u32[]{:S(2)}, u32[]{:S(2)}) collective-permute-start(s16[288,128]{1,0:T(8,128)(2,1)} %get-tuple-element.10), channel_id=1, source_target_pairs={{0,2},{2,0},{4,6},{6,4},{8,10},{10,8},{12,14},{14,12},{1,3},{3,1},... | collective-permute-start | bytes 221192 | tf_op jit(solution)/shard_map/ppermute | solution.py:356
  10.2 6.6 %collective-permute-start = (s16[288,128]{1,0:T(8,128)(2,1)}, s16[288,128]{1,0:T(8,128)(2,1)S(1)}, u32[]{:S(2)}, u32[]{:S(2)}) collective-permute-start(s16[288,128]{1,0:T(8,128)(2,1)} %get-tuple-element.10), channel_id=1, source_target_pairs={{0,6},{2,4},{4,2},{6,0},{8,14},{10,12},{12,10},{14,8},{1,7},{3,5},... | collective-permute-start | bytes 221192 | tf_op jit(solution)/shard_map/ppermute | solution.py:356
  12.2 5.3 %collective-permute-start.6 = (s16[288,128]{1,0:T(8,128)(2,1)S(1)}, s16[288,128]{1,0:T(8,128)(2,1)S(1)}, u32[]{:S(2)}, u32[]{:S(2)}) collective-permute-start(s16[288,128]{1,0:T(8,128)(2,1)S(1)} %collective-permute-done.3.refs_5_), channel_id=1, source_target_pairs={{0,2},{2,0},{4,6},{6,4},{8,10},{10,8},{12,14},{14,12},{1,3},{3,1},... | collective-permute-start | bytes 221192 | tf_op jit(solution)/shard_map/ppermute | solution.py:356
  14.2 4.4 %collective-permute-start.5 = (s16[288,128]{1,0:T(8,128)(2,1)S(1)}, s16[288,128]{1,0:T(8,128)(2,1)S(1)}, u32[]{:S(2)}, u32[]{:S(2)}) collective-permute-start(s16[288,128]{1,0:T(8,128)(2,1)S(1)} %collective-permute-done.1.refs_3_), channel_id=1, source_target_pairs={{0,2},{2,0},{4,6},{6,4},{8,10},{10,8},{12,14},{14,12},{1,3},{3,1},... | collective-permute-start | bytes 221192 | tf_op jit(solution)/shard_map/ppermute | solution.py:356
  22.7 1.3 %collective-permute-start.7 = (f32[64,256]{1,0:T(8,128)S(1)}, f32[64,256]{1,0:T(8,128)S(1)}, u32[]{:S(2)}, u32[]{:S(2)}) collective-permute-start(f32[64,256]{1,0:T(8,128)S(1)} %get-tuple-element.12), channel_id=1, source_target_pairs={{0,1},{1,0},{2,3},{3,2},{4,5},{5,4},{6,7},{7,6},{8,9},{9,8},{10,11... | collective-permute-start | bytes 196616 | tf_op jit(solution)/shard_map/ppermute | solution.py:388

commit v3 on v2

--- a/solution.py
+++ b/solution.py
@@ -82,20 +82,17 @@
 
 
 def filter_kernel(
-    records_hbm, channel_hbm, piece_hbm, taps_hbm, slot_hbm, starts_hbm, unit_hbm, local_hbm, *scratch
+    records_hbm, channel_hbm, piece_hbm, taps_hbm, slot_hbm, unit_hbm, local_hbm, *scratch
 ):
-    records_ref, channel_ref, piece_ref, taps_ref, slot_ref, starts_ref = scratch[:6]
-    unit_ref, local_ref, arrived = scratch[6:]
+    records_ref, channel_ref, piece_ref, taps_ref, slot_ref, unit_ref, arrived = scratch
     f32 = jnp.float32
     count = records_ref.shape[0]
-    size = unit_ref.shape[0]
     pairs = (
         (taps_hbm, taps_ref),
         (records_hbm, records_ref),
         (channel_hbm, channel_ref),
         (piece_hbm, piece_ref),
         (slot_hbm, slot_ref),
-        (starts_hbm, starts_ref),
     )
     copies = [
         pltpu.make_async_copy(source, target, arrived.at[number])
@@ -128,9 +125,7 @@
     root = jnp.sqrt(jnp.sqrt(absolute * jnp.exp2(-power)))
     code = jnp.floor(root * CODE + 0.5)
     code = jnp.where(filtered < 0.0, -code, code)
-    main = jnp.transpose(code[:OUTS]).astype(jnp.int32)
-    local_ref[:count] = main
-    unit_ref[:count] = main.astype(jnp.int16)
+    unit_ref[:OUTS] = code[:OUTS].astype(jnp.int32).astype(jnp.int16)
     for copy in copies[2:]:
         copy.wait()
     row = lax.broadcasted_iota(jnp.int32, (AUX, count), 0)
@@ -139,19 +134,9 @@
     side = jnp.where(row == SCALE_ROW, power.astype(jnp.int32), side)
     side = jnp.where(row == KEY_ROW, key, side)
     side = jnp.where(row == SLOT_ROW, slot_ref[0], side)
-    for block in range(count // LANES):
-        to = slice(count + block * AUX, count + (block + 1) * AUX)
-        part = side[:, block * LANES : (block + 1) * LANES]
-        local_ref[to] = part
-        unit_ref[to] = part.astype(jnp.int16)
-    lane = lax.broadcasted_iota(jnp.int32, (8, OUTS), 1)
-    starts = jnp.zeros((8, OUTS), jnp.int32)
-    for window in range(WIN_DEV):
-        starts = jnp.where(lane == window, starts_ref[window], starts)
-    local_ref[size:] = starts
-    here = local_hbm.at[pl.ds(0, size + 8)]
+    unit_ref[OUTS:] = side.astype(jnp.int16)
     out = pltpu.make_async_copy(unit_ref, unit_hbm, arrived.at[0])
-    local = pltpu.make_async_copy(local_ref, here, arrived.at[1])
+    local = pltpu.make_async_copy(unit_ref, local_hbm.at[pl.ds(0, OUTS + AUX)], arrived.at[1])
     out.start()
     local.start()
     out.wait()
@@ -169,17 +154,17 @@
 
 
 def correlate_kernel(block_total, span_total, *refs):
-    local_hbm, slot_ref = refs[:2]
+    local_hbm, starts_hbm, slot_ref = refs[:3]
+    refs = refs[1:]
     units_ref = dict(zip(ORDER, refs[2 : block_total + 1]))
     wide_ref, band_ref, lags_ref, keep_ref, send_ref = refs[block_total + 1 : block_total + 6]
-    pick_ref, dec_ref, seg_ref, white_ref, out_ref, unit_ref, starts_ref, arrived = refs[
+    pick_ref, pick_sum_ref, dec_ref, seg_ref, white_ref, out_ref, unit_ref, starts_ref, arrived = refs[
         block_total + 6 :
     ]
     f32 = jnp.float32
-    size = unit_ref.shape[0]
     pairs = (
-        (local_hbm.at[pl.ds(0, size)], unit_ref),
-        (local_hbm.at[pl.ds(size, 8)], starts_ref),
+        (local_hbm.at[pl.ds(0, OUTS + AUX)], unit_ref),
+        (starts_hbm, starts_ref),
     )
     copies = [
         pltpu.make_async_copy(source, target, arrived.at[number])
@@ -190,12 +175,10 @@
     me = lax.axis_index("chan")
     half = lax.axis_index("win")
     rows = CH_DEV + block_total
-    count = size * LANES // (LANES + AUX)
+    count = unit_ref.shape[1]
 
     def side_of(unit):
-        blocks = range(count // LANES)
-        parts = [unit[count + block * AUX : count + (block + 1) * AUX] for block in blocks]
-        return jnp.concatenate([part.astype(jnp.int32) for part in parts], axis=1)
+        return unit[OUTS:].astype(jnp.int32)
 
     sides = {step: side_of(unit) for step, unit in units_ref.items()}
     row = lax.broadcasted_iota(jnp.int32, (2 * rows, count), 0)
@@ -216,36 +199,32 @@
                 pair * 2 * rows : (pair + 1) * 2 * rows, step * count : (step + 1) * count
             ] = jnp.where(wanted + 2 * pair == key, 1.0, 0.0).astype(jnp.bfloat16)
 
-    for step in range(1, block_total):
-        pick(step, sides[step])
+    def select(steps, units):
+        for step in steps:
+            pick(step, sides[step])
+        codes = jnp.concatenate([units[step][...].astype(jnp.int32) for step in steps], axis=1)
+        return lax.dot_general(
+            jnp.concatenate(halves(codes), axis=0),
+            pick_ref[:, steps[0] * count : (steps[-1] + 1) * count],
+            (((1,), (1,)), ((), ())),
+            preferred_element_type=f32,
+        )
+
+    pick_sum_ref[...] = select(list(range(1, block_total)), units_ref)
     copies[0].wait()
     sides[0] = side_of(unit_ref)
-    pick(0, sides[0])
-    units = [unit_ref] + [units_ref[step] for step in range(1, block_total)]
-    codes = jnp.concatenate([unit[:count].astype(jnp.int32) for unit in units], axis=0)
-    picked = jnp.dot(
-        pick_ref[...], jnp.concatenate(halves(codes), axis=1), preferred_element_type=f32
-    )
-    side = jnp.concatenate([sides[step] for step in range(block_total)], axis=1)
-    beside = lax.dot_general(
-        pick_ref[...],
-        jnp.concatenate(halves(side), axis=0),
-        (((1,), (1,)), ((), ())),
-        preferred_element_type=f32,
-    )
-    beside = beside[:, :AUX] * 256.0 + beside[:, AUX:]
-    scale = jnp.exp2(beside[:, SCALE_ROW : SCALE_ROW + 1])
-    main_part = decoded(picked[:, :OUTS] * 256.0 + picked[:, OUTS:], scale)
-    column = lax.broadcasted_iota(jnp.int32, beside.shape, 1)
-    spill_part = jnp.where(column < SPILL, decoded(beside, scale), 0.0)
+    picked = select([0], [unit_ref]) + pick_sum_ref[...]
+    picked = picked[: OUTS + AUX] * 256.0 + picked[OUTS + AUX :]
+    scale = jnp.exp2(picked[OUTS + SCALE_ROW : OUTS + SCALE_ROW + 1])
+    main_part = decoded(picked[:OUTS], scale)
+    spill_part = pltpu.roll(decoded(picked[OUTS:], scale), rows, 1)
+    row = lax.broadcasted_iota(jnp.int32, spill_part.shape, 0)
+    column = lax.broadcasted_iota(jnp.int32, spill_part.shape, 1)
+    spill_part = jnp.where((row < SPILL) & (column >= rows), spill_part, 0.0)
+    samples = jnp.concatenate([main_part[:AUX] + spill_part, main_part[AUX:]], axis=0)
+    samples = jnp.transpose(samples)
     for piece in range(PIECES):
-        dec_ref[:, piece * OUTS : (piece + 1) * OUTS] = main_part[
-            piece * rows : (piece + 1) * rows
-        ]
-        if piece:
-            dec_ref[:, piece * OUTS : piece * OUTS + AUX] += spill_part[
-                (piece - 1) * rows : piece * rows
-            ]
+        dec_ref[:, piece * OUTS : (piece + 1) * OUTS] = samples[piece * rows : (piece + 1) * rows]
     dec_ref[:, SPAN:] = jnp.zeros((rows, LANES), f32)
     lane = lax.broadcasted_iota(jnp.int32, (rows, LANES), 1)
     extra = wide_ref[WL:].astype(f32)
@@ -253,7 +232,7 @@
     inverse = (extra[3:4] + extra[4:5] + extra[5:6])[:, :NF]
     copies[1].wait()
     for window in range(WIN_DEV):
-        start = starts_ref[0, window]
+        start = starts_ref[window]
         base = pl.multiple_of((start >> 7) * LANES, LANES)
         offset = start & (LANES - 1)
         shift = (LANES - offset) & (LANES - 1)
@@ -290,18 +269,26 @@
     for tile in range(NF // LANES):
         re = slice(tile * LANES, (tile + 1) * LANES)
         im = slice(NF + tile * LANES, NF + (tile + 1) * LANES)
-        real_sums = [jnp.zeros((CH_DEV, LANES), f32)] * block_total
-        imag_sums = [jnp.zeros((CH_DEV, LANES), f32)] * block_total
-        for window in range(WIN_DEV):
-            own = slice(window * rows, window * rows + CH_DEV)
-            loc_real = white_ref[own, re]
-            loc_imag = white_ref[own, im]
-            for number in range(block_total):
-                at = window * rows + CH_DEV + number
-                src_real = jnp.broadcast_to(white_ref[at : at + 1, re], (CH_DEV, LANES))
-                src_imag = jnp.broadcast_to(white_ref[at : at + 1, im], (CH_DEV, LANES))
-                real_sums[number] += src_real * loc_real + src_imag * loc_imag
-                imag_sums[number] += src_imag * loc_real - src_real * loc_imag
+        real_sums = []
+        imag_sums = []
+        for group in range(0, block_total, 4):
+            zero = jnp.zeros((CH_DEV, LANES), f32)
+            sums = [[zero, zero, zero] for _ in range(4)]
+            for window in range(WIN_DEV):
+                own = slice(window * rows, window * rows + CH_DEV)
+                loc_real = white_ref[own, re]
+                loc_imag = white_ref[own, im]
+                less = loc_real - loc_imag
+                more = loc_real + loc_imag
+                for number in range(4):
+                    at = window * rows + CH_DEV + group + number
+                    src_real = jnp.broadcast_to(white_ref[at : at + 1, re], (CH_DEV, LANES))
+                    src_imag = jnp.broadcast_to(white_ref[at : at + 1, im], (CH_DEV, LANES))
+                    sums[number][0] += loc_real * (src_real + src_imag)
+                    sums[number][1] += less * src_imag
+                    sums[number][2] += more * src_real
+            real_sums += [both - imag for both, imag, real in sums]
+            imag_sums += [both - real for both, imag, real in sums]
         cross = jnp.concatenate(
             [
                 jnp.concatenate(real_sums, axis=0).astype(jnp.bfloat16),
@@ -327,14 +314,14 @@
     smem = pl.BlockSpec(memory_space=pltpu.SMEM)
     hbm = pl.BlockSpec(memory_space=pl.ANY)
     count = records.shape[0]
-    size = count + count // LANES * AUX
+    unit_shape = (OUTS + AUX, count)
     unit, local = pl.pallas_call(
         filter_kernel,
         out_shape=(
-            jax.ShapeDtypeStruct((size, OUTS), jnp.int16),
-            jax.ShapeDtypeStruct((LOCAL_ROWS, OUTS), jnp.int32),
+            jax.ShapeDtypeStruct(unit_shape, jnp.int16),
+            jax.ShapeDtypeStruct((LOCAL_ROWS, count), jnp.int16),
         ),
-        in_specs=[hbm] * 6,
+        in_specs=[hbm] * 5,
         out_specs=(hbm, hbm),
         scratch_shapes=[
             pltpu.VMEM(records.shape, records.dtype),
@@ -342,15 +329,13 @@
             pltpu.VMEM(record_piece.shape, jnp.int32),
             pltpu.VMEM(fir_taps.shape, fir_taps.dtype),
             pltpu.SMEM((1,), jnp.int32),
-            pltpu.SMEM((WIN_DEV,), jnp.int32),
-            pltpu.VMEM((size, OUTS), jnp.int16),
-            pltpu.VMEM((size + 8, OUTS), jnp.int32),
-            pltpu.SemaphoreType.DMA((6,)),
+            pltpu.VMEM(unit_shape, jnp.int16),
+            pltpu.SemaphoreType.DMA((5,)),
         ],
         compiler_params=pltpu.CompilerParams(vmem_limit_bytes=FILTER_VMEM),
         cost_estimate=pl.CostEstimate(flops=FLOPS, bytes_accessed=1 << 20, transcendentals=0),
         name="filter",
-    )(records, record_channel, record_piece, fir_taps, source_slot, window_starts)
+    )(records, record_channel, record_piece, fir_taps, source_slot)
 
     def swap(value, step):
         return lax.ppermute(value, "chan", [(i, i ^ step) for i in range(block_total)])
@@ -365,22 +350,24 @@
     keep, send = pl.pallas_call(
         lambda *refs: correlate_kernel(block_total, span_total, *refs),
         out_shape=(half_shape, half_shape),
-        in_specs=[hbm, smem] + [vmem] * (block_total + 2),
+        in_specs=[hbm, hbm, smem] + [vmem] * (block_total + 2),
         out_specs=(vmem, vmem),
         scratch_shapes=[
             pltpu.VMEM((PIECES * rows, block_total * count), jnp.bfloat16),
+            pltpu.VMEM((2 * (OUTS + AUX), PIECES * rows), jnp.float32),
             pltpu.VMEM((rows, SPAN + LANES), jnp.float32),
             pltpu.VMEM((WIN_DEV * rows, WL), jnp.float32),
             pltpu.VMEM((WIN_DEV * rows, WL), jnp.float32),
             pltpu.VMEM((block_total * CH_DEV, LAGS), jnp.float32),
-            pltpu.VMEM((size, OUTS), jnp.int32),
-            pltpu.SMEM((8, OUTS), jnp.int32),
+            pltpu.VMEM(unit_shape, jnp.int16),
+            pltpu.SMEM((WIN_DEV,), jnp.int32),
             pltpu.SemaphoreType.DMA((2,)),
         ],
         compiler_params=pltpu.CompilerParams(vmem_limit_bytes=CORRELATE_VMEM),
         name="correlate",
     )(
         local,
+        window_starts,
         source_slot,
         *[units[step] for step in ORDER],
         *[jnp.asarray(table) for table in tables],

time: 24.8 us -> 24.3 us (0.980)
  Pallas kernels: 6.44 us -> 5.96 us
    pallas_call x1, Pallas kernels: 4.1 us -> 3.76 us  [gathered_body(): pl.pallas_call(lambda *refs: correlate_kernel(block_total, span_total, *r...]
where the time goes in v3:
time: 24.3 us; the launch traced here: 24.2 us
  starting transfers between devices  12 us (49%)
  Pallas kernels  5.96 us (25%)
  waiting for transfers between devices  4.79 us (20%)
  between operations  0.73 us (3%)
  other arithmetic  0.64 us (3%)
    ppermute x7, starting transfers between devices, swap(): lax.ppermute(value, 'chan', [(i, i ^ step) for i in range(block_total)])  12 us
    pallas_call x1, Pallas kernels, gathered_body(): pl.pallas_call(lambda *refs: correlate_kernel(block_total, span_total, *r...  3.76 us
    ppermute x7, waiting for transfers between devices, swap(): lax.ppermute(value, 'chan', [(i, i ^ step) for i in range(block_total)])  3.55 us
    pallas_call x1, Pallas kernels, gathered_body(): pl.pallas_call(filter_kernel, out_shape=(jax.ShapeDtypeStruct(unit_shape,...  2.2 us
    ppermute x1, waiting for transfers between devices, gathered_body(): other = lax.ppermute(send, 'win', [(i, i ^ 1) for i in range(span_total)])  1.24 us
    add x1, other arithmetic, gathered_body(): return (keep + other).reshape(block_total // span_total, CH_DEV, LAGS)  0.64 us
  transfers between devices with their start and end apart: 8, of which 5 were waited for; matrix products, arithmetic and copies ran while one was open for 0% of the time, Pallas kernels for 0%

profile of v3, /device:TPU:0, one launch (start us, length us, event | category | flops | bytes accessed | tf_op | source)
XLA Modules:
  0.0 24.2 jit_solution(793843821294823008)
XLA Ops:
  0.7 0.0 copy-start
  0.7 0.0 copy-start.1
  0.7 0.0 copy-start.2
  0.7 0.0 copy-start.3
  0.7 2.2 %filter.1 = (s16[144,256]{1,0:T(8,128)(2,1)}, s16[16384,256]{1,0:T(8,128)(2,1)}) custom-call(bf16[256,512]{1,0:T(8,128)(2,1)} %records_hbm.1, s32[256]{0:T(256)} %channel_hbm.1, s32[256]{0:T(256)} %piece_hbm.1, bf16[32]{0:T(256)(128)(2,1)} %taps_hbm.1, s32[1]{0:T(128)S(6)} %copy.10.slot_hbm.refs_2_), custom_call_target="tpu_custom_call" | custom-call | flops 10000000000 | bytes 1048576 | tf_op jit(solution)/shard_map/filter/pallas_call | solution.py:318
  2.9 4.1 %collective-permute-start.3 = (s16[144,256]{1,0:T(8,128)(2,1)}, s16[144,256]{1,0:T(8,128)(2,1)S(1)}, u32[]{:S(2)}, u32[]{:S(2)}) collective-permute-start(s16[144,256]{1,0:T(8,128)(2,1)} %get-tuple-element.10), channel_id=1, source_target_pairs={{0,8},{2,10},{4,12},{6,14},{8,0},{10,2},{12,4},{14,6},{1,9},{3,11}... | collective-permute-start | bytes 221192 | tf_op jit(solution)/shard_map/ppermute | solution.py:341
  7.0 1.3 %collective-permute-start.1 = (s16[144,256]{1,0:T(8,128)(2,1)}, s16[144,256]{1,0:T(8,128)(2,1)S(1)}, u32[]{:S(2)}, u32[]{:S(2)}) collective-permute-start(s16[144,256]{1,0:T(8,128)(2,1)} %get-tuple-element.10), channel_id=1, source_target_pairs={{0,12},{2,14},{4,8},{6,10},{8,4},{10,6},{12,0},{14,2},{1,13},{3,15... | collective-permute-start | bytes 221192 | tf_op jit(solution)/shard_map/ppermute | solution.py:341
  8.4 0.2 collective-permute-start.4
  8.6 1.5 %collective-permute-start.2 = (s16[144,256]{1,0:T(8,128)(2,1)}, s16[144,256]{1,0:T(8,128)(2,1)S(1)}, u32[]{:S(2)}, u32[]{:S(2)}) collective-permute-start(s16[144,256]{1,0:T(8,128)(2,1)} %get-tuple-element.10), channel_id=1, source_target_pairs={{0,2},{2,0},{4,6},{6,4},{8,10},{10,8},{12,14},{14,12},{1,3},{3,1},... | collective-permute-start | bytes 221192 | tf_op jit(solution)/shard_map/ppermute | solution.py:341
  10.1 1.8 %collective-permute-start = (s16[144,256]{1,0:T(8,128)(2,1)}, s16[144,256]{1,0:T(8,128)(2,1)S(1)}, u32[]{:S(2)}, u32[]{:S(2)}) collective-permute-start(s16[144,256]{1,0:T(8,128)(2,1)} %get-tuple-element.10), channel_id=1, source_target_pairs={{0,6},{2,4},{4,2},{6,0},{8,14},{10,12},{12,10},{14,8},{1,7},{3,5},... | collective-permute-start | bytes 221192 | tf_op jit(solution)/shard_map/ppermute | solution.py:341
  11.8 0.3 %collective-permute-done.3.refs_6_ = s16[144,256]{1,0:T(8,128)(2,1)S(1)} collective-permute-done((s16[144,256]{1,0:T(8,128)(2,1)}, s16[144,256]{1,0:T(8,128)(2,1)S(1)}, u32[]{:S(2)}, u32[]{:S(2)}) %collective-permute-start.3) | collective-permute-done | bytes 73760 | tf_op jit(solution)/shard_map/ppermute | solution.py:341
  12.1 2.0 %collective-permute-start.6 = (s16[144,256]{1,0:T(8,128)(2,1)S(1)}, s16[144,256]{1,0:T(8,128)(2,1)S(1)}, u32[]{:S(2)}, u32[]{:S(2)}) collective-permute-start(s16[144,256]{1,0:T(8,128)(2,1)S(1)} %collective-permute-done.3.refs_6_), channel_id=1, source_target_pairs={{0,2},{2,0},{4,6},{6,4},{8,10},{10,8},{12,14},{14,12},{1,3},{3,1},... | collective-permute-start | bytes 221192 | tf_op jit(solution)/shard_map/ppermute | solution.py:341
  14.1 0.0 collective-permute-done.1.refs_4_
  14.1 1.1 %collective-permute-start.5 = (s16[144,256]{1,0:T(8,128)(2,1)S(1)}, s16[144,256]{1,0:T(8,128)(2,1)S(1)}, u32[]{:S(2)}, u32[]{:S(2)}) collective-permute-start(s16[144,256]{1,0:T(8,128)(2,1)S(1)} %collective-permute-done.1.refs_4_), channel_id=1, source_target_pairs={{0,2},{2,0},{4,6},{6,4},{8,10},{10,8},{12,14},{14,12},{1,3},{3,1},... | collective-permute-start | bytes 221192 | tf_op jit(solution)/shard_map/ppermute | solution.py:341
  15.1 0.0 collective-permute-done.4.refs_7_
  15.1 0.0 collective-permute-done.2.refs_5_
  15.1 1.5 %collective-permute-done.refs_3_ = s16[144,256]{1,0:T(8,128)(2,1)S(1)} collective-permute-done((s16[144,256]{1,0:T(8,128)(2,1)}, s16[144,256]{1,0:T(8,128)(2,1)S(1)}, u32[]{:S(2)}, u32[]{:S(2)}) %collective-permute-start) | collective-permute-done | bytes 73760 | tf_op jit(solution)/shard_map/ppermute | solution.py:341
  16.7 0.8 %collective-permute-done.6.refs_9_ = s16[144,256]{1,0:T(8,128)(2,1)S(1)} collective-permute-done((s16[144,256]{1,0:T(8,128)(2,1)S(1)}, s16[144,256]{1,0:T(8,128)(2,1)S(1)}, u32[]{:S(2)}, u32[]{:S(2)}) %collective-permute-start.6) | collective-permute-done | bytes 73760 | tf_op jit(solution)/shard_map/ppermute | solution.py:341
  17.4 1.0 %collective-permute-done.5.refs_8_ = s16[144,256]{1,0:T(8,128)(2,1)S(1)} collective-permute-done((s16[144,256]{1,0:T(8,128)(2,1)S(1)}, s16[144,256]{1,0:T(8,128)(2,1)S(1)}, u32[]{:S(2)}, u32[]{:S(2)}) %collective-permute-start.5) | collective-permute-done | bytes 73760 | tf_op jit(solution)/shard_map/ppermute | solution.py:341
  18.4 0.0 copy-done
  18.4 0.0 copy-done.1
  18.4 0.0 copy-done.2
  18.4 0.0 copy-done.3
  18.4 3.8 %correlate.1 = (f32[64,256]{1,0:T(8,128)S(1)}, f32[64,256]{1,0:T(8,128)S(1)}) custom-call(s16[16384,256]{1,0:T(8,128)(2,1)} %get-tuple-element.9.refs_0_, s32[8]{0:T(128)S(1)} %copy-done.3, s32[1]{0:T(128)S(6)} %copy.10.slot_hbm.refs_2_, s16[144,256]{1,0:T(8,128)(2,1)S(1)} %collective-permute-done.refs_3_, ...), custom_call_target="tpu_custom_call" | custom-call | tf_op jit(solution)/shard_map/correlate/pallas_call | solution.py:350
  22.2 0.1 collective-permute-start.7
  22.3 1.2 %collective-permute-done.7 = f32[64,256]{1,0:T(8,128)S(1)} collective-permute-done((f32[64,256]{1,0:T(8,128)S(1)}, f32[64,256]{1,0:T(8,128)S(1)}, u32[]{:S(2)}, u32[]{:S(2)}) %collective-permute-start.7) | collective-permute-done | bytes 65568 | tf_op jit(solution)/shard_map/ppermute | solution.py:375
  23.5 0.6 %add.3 = f32[64,256]{1,0:T(8,128)} add(f32[64,256]{1,0:T(8,128)S(1)} %get-tuple-element.11, f32[64,256]{1,0:T(8,128)S(1)} %collective-permute-done.7) | non-fusion elementwise | flops 16384 | bytes 196608 | tf_op jit(solution)/shard_map/add | solution.py:376
Async XLA Ops:
  0.7 17.8 %copy-start = (bf16[1040,1024]{1,0:T(8,128)(2,1)S(1)}, bf16[1040,1024]{1,0:T(8,128)(2,1)}, u32[]{:S(2)}) copy-start(bf16[1040,1024]{1,0:T(8,128)(2,1)} %constant.6.clone.refs_10_) | copy-start | bytes 6389764
  0.7 17.8 %copy-start.1 = (bf16[1024,256]{1,0:T(8,128)(2,1)S(1)}, bf16[1024,256]{1,0:T(8,128)(2,1)}, u32[]{:S(2)}) copy-start(bf16[1024,256]{1,0:T(8,128)(2,1)} %constant.8.clone.refs_12_) | copy-start | bytes 1572868
  0.7 17.8 %copy-start.2 = (bf16[512,512]{1,0:T(8,128)(2,1)S(1)}, bf16[512,512]{1,0:T(8,128)(2,1)}, u32[]{:S(2)}) copy-start(bf16[512,512]{1,0:T(8,128)(2,1)} %constant.7.clone.refs_11_) | copy-start | bytes 1572868
  0.7 17.8 %copy-start.3 = (s32[8]{0:T(128)S(1)}, s32[8]{0:T(128)}, u32[]{:S(2)}) copy-start(s32[8]{0:T(128)} %refs_1_.1) | copy-start | bytes 100
  2.9 9.2 %collective-permute-start.3 = (s16[144,256]{1,0:T(8,128)(2,1)}, s16[144,256]{1,0:T(8,128)(2,1)S(1)}, u32[]{:S(2)}, u32[]{:S(2)}) collective-permute-start(s16[144,256]{1,0:T(8,128)(2,1)} %get-tuple-element.10), channel_id=1, source_target_pairs={{0,8},{2,10},{4,12},{6,14},{8,0},{10,2},{12,4},{14,6},{1,9},{3,11}... | collective-permute-start | bytes 221192 | tf_op jit(solution)/shard_map/ppermute | solution.py:341
  7.0 7.1 %collective-permute-start.1 = (s16[144,256]{1,0:T(8,128)(2,1)}, s16[144,256]{1,0:T(8,128)(2,1)S(1)}, u32[]{:S(2)}, u32[]{:S(2)}) collective-permute-start(s16[144,256]{1,0:T(8,128)(2,1)} %get-tuple-element.10), channel_id=1, source_target_pairs={{0,12},{2,14},{4,8},{6,10},{8,4},{10,6},{12,0},{14,2},{1,13},{3,15... | collective-permute-start | bytes 221192 | tf_op jit(solution)/shard_map/ppermute | solution.py:341
  8.4 6.8 %collective-permute-start.4 = (s16[144,256]{1,0:T(8,128)(2,1)}, s16[144,256]{1,0:T(8,128)(2,1)S(1)}, u32[]{:S(2)}, u32[]{:S(2)}) collective-permute-start(s16[144,256]{1,0:T(8,128)(2,1)} %get-tuple-element.10), channel_id=1, source_target_pairs={{0,4},{2,6},{4,0},{6,2},{8,12},{10,14},{12,8},{14,10},{1,5},{3,7},... | collective-permute-start | bytes 221192 | tf_op jit(solution)/shard_map/ppermute | solution.py:341
  8.6 6.5 %collective-permute-start.2 = (s16[144,256]{1,0:T(8,128)(2,1)}, s16[144,256]{1,0:T(8,128)(2,1)S(1)}, u32[]{:S(2)}, u32[]{:S(2)}) collective-permute-start(s16[144,256]{1,0:T(8,128)(2,1)} %get-tuple-element.10), channel_id=1, source_target_pairs={{0,2},{2,0},{4,6},{6,4},{8,10},{10,8},{12,14},{14,12},{1,3},{3,1},... | collective-permute-start | bytes 221192 | tf_op jit(solution)/shard_map/ppermute | solution.py:341
  10.1 6.6 %collective-permute-start = (s16[144,256]{1,0:T(8,128)(2,1)}, s16[144,256]{1,0:T(8,128)(2,1)S(1)}, u32[]{:S(2)}, u32[]{:S(2)}) collective-permute-start(s16[144,256]{1,0:T(8,128)(2,1)} %get-tuple-element.10), channel_id=1, source_target_pairs={{0,6},{2,4},{4,2},{6,0},{8,14},{10,12},{12,10},{14,8},{1,7},{3,5},... | collective-permute-start | bytes 221192 | tf_op jit(solution)/shard_map/ppermute | solution.py:341
  12.1 5.3 %collective-permute-start.6 = (s16[144,256]{1,0:T(8,128)(2,1)S(1)}, s16[144,256]{1,0:T(8,128)(2,1)S(1)}, u32[]{:S(2)}, u32[]{:S(2)}) collective-permute-start(s16[144,256]{1,0:T(8,128)(2,1)S(1)} %collective-permute-done.3.refs_6_), channel_id=1, source_target_pairs={{0,2},{2,0},{4,6},{6,4},{8,10},{10,8},{12,14},{14,12},{1,3},{3,1},... | collective-permute-start | bytes 221192 | tf_op jit(solution)/shard_map/ppermute | solution.py:341
  14.1 4.4 %collective-permute-start.5 = (s16[144,256]{1,0:T(8,128)(2,1)S(1)}, s16[144,256]{1,0:T(8,128)(2,1)S(1)}, u32[]{:S(2)}, u32[]{:S(2)}) collective-permute-start(s16[144,256]{1,0:T(8,128)(2,1)S(1)} %collective-permute-done.1.refs_4_), channel_id=1, source_target_pairs={{0,2},{2,0},{4,6},{6,4},{8,10},{10,8},{12,14},{14,12},{1,3},{3,1},... | collective-permute-start | bytes 221192 | tf_op jit(solution)/shard_map/ppermute | solution.py:341
  22.2 1.3 %collective-permute-start.7 = (f32[64,256]{1,0:T(8,128)S(1)}, f32[64,256]{1,0:T(8,128)S(1)}, u32[]{:S(2)}, u32[]{:S(2)}) collective-permute-start(f32[64,256]{1,0:T(8,128)S(1)} %get-tuple-element.12), channel_id=1, source_target_pairs={{0,1},{1,0},{2,3},{3,2},{4,5},{5,4},{6,7},{7,6},{8,9},{9,8},{10,11... | collective-permute-start | bytes 196616 | tf_op jit(solution)/shard_map/ppermute | solution.py:375

commit v4 on v3

--- a/solution.py
+++ b/solution.py
@@ -33,10 +33,10 @@
 SLOT_ROW = SPILL + 2
 FILTER_VMEM = 56 << 20
 FLOPS = 10**10
-CORRELATE_VMEM = 50 << 20
+CORRELATE_VMEM = 48 << 20
 LOCAL_ROWS = 16384
-LAST_HOP = {1: 1, 2: 2, 4: 4, 6: 6, 3: 3, 5: 1, 7: 1}
-ORDER = (3, 6, 1, 4, 2, 7, 5)
+LAST_HOP = {1: 1, 2: 2, 3: 3, 4: 4, 6: 2, 5: 1, 7: 3}
+ORDER = (6, 7, 3, 2, 4, 1, 5)
 CODE = 23000.0
 
 
@@ -153,14 +153,50 @@
     return (root * root) * (root * jnp.abs(root)) * scale
 
 
+def lag_products(white_ref, lags_ref, rows, first, number):
+    f32 = jnp.float32
+    total = jnp.zeros((number * CH_DEV, LAGS), f32)
+    for tile in range(NF // LANES):
+        re = slice(tile * LANES, (tile + 1) * LANES)
+        im = slice(NF + tile * LANES, NF + (tile + 1) * LANES)
+        zero = jnp.zeros((CH_DEV, LANES), f32)
+        sums = [[zero, zero, zero] for _ in range(number)]
+        for window in range(WIN_DEV):
+            own = slice(window * rows, window * rows + CH_DEV)
+            loc_real = white_ref[own, re]
+            loc_imag = white_ref[own, im]
+            less = loc_real - loc_imag
+            more = loc_real + loc_imag
+            for source in range(number):
+                at = window * rows + CH_DEV + first + source
+                src_real = jnp.broadcast_to(white_ref[at : at + 1, re], (CH_DEV, LANES))
+                src_imag = jnp.broadcast_to(white_ref[at : at + 1, im], (CH_DEV, LANES))
+                sums[source][0] += loc_real * (src_real + src_imag)
+                sums[source][1] += less * src_imag
+                sums[source][2] += more * src_real
+        real_sums = [both - imag for both, imag, real in sums]
+        imag_sums = [both - real for both, imag, real in sums]
+        cross = jnp.concatenate(
+            [
+                jnp.concatenate(real_sums, axis=0).astype(jnp.bfloat16),
+                jnp.concatenate(imag_sums, axis=0).astype(jnp.bfloat16),
+            ],
+            axis=1,
+        )
+        total += jnp.dot(
+            cross,
+            lags_ref[2 * tile * LANES : 2 * (tile + 1) * LANES],
+            preferred_element_type=f32,
+        )
+    return total
+
+
 def correlate_kernel(block_total, span_total, *refs):
     local_hbm, starts_hbm, slot_ref = refs[:3]
     refs = refs[1:]
     units_ref = dict(zip(ORDER, refs[2 : block_total + 1]))
-    wide_ref, band_ref, lags_ref, keep_ref, send_ref = refs[block_total + 1 : block_total + 6]
-    pick_ref, pick_sum_ref, dec_ref, seg_ref, white_ref, out_ref, unit_ref, starts_ref, arrived = refs[
-        block_total + 6 :
-    ]
+    wide_ref, band_ref, lags_ref, send_ref, white_ref = refs[block_total + 1 : block_total + 6]
+    pick_ref, pick_sum_ref, dec_ref, seg_ref, unit_ref, starts_ref, arrived = refs[block_total + 6 :]
     f32 = jnp.float32
     pairs = (
         (local_hbm.at[pl.ds(0, OUTS + AUX)], unit_ref),
@@ -184,7 +220,8 @@
     row = lax.broadcasted_iota(jnp.int32, (2 * rows, count), 0)
     odd = (row >= rows).astype(jnp.int32)
     row = row - odd * rows
-    source = row - CH_DEV
+    source = (row - CH_DEV + (1 + half) * (block_total // span_total)) % block_total
+    source = jnp.where(row >= CH_DEV, source, -1)
     channel = me * CH_DEV + row
     channel = jnp.where(source == me, source * CH_DEV + slot_ref[0], channel)
     for step, side in sides.items():
@@ -265,46 +302,11 @@
     scale = lax.rsqrt(smooth + EPSILON)
     white_ref[:, :NF] = (real * scale).astype(jnp.bfloat16).astype(f32)
     white_ref[:, NF:] = (imag * scale).astype(jnp.bfloat16).astype(f32)
-    total = jnp.zeros((block_total * CH_DEV, LAGS), f32)
-    for tile in range(NF // LANES):
-        re = slice(tile * LANES, (tile + 1) * LANES)
-        im = slice(NF + tile * LANES, NF + (tile + 1) * LANES)
-        real_sums = []
-        imag_sums = []
-        for group in range(0, block_total, 4):
-            zero = jnp.zeros((CH_DEV, LANES), f32)
-            sums = [[zero, zero, zero] for _ in range(4)]
-            for window in range(WIN_DEV):
-                own = slice(window * rows, window * rows + CH_DEV)
-                loc_real = white_ref[own, re]
-                loc_imag = white_ref[own, im]
-                less = loc_real - loc_imag
-                more = loc_real + loc_imag
-                for number in range(4):
-                    at = window * rows + CH_DEV + group + number
-                    src_real = jnp.broadcast_to(white_ref[at : at + 1, re], (CH_DEV, LANES))
-                    src_imag = jnp.broadcast_to(white_ref[at : at + 1, im], (CH_DEV, LANES))
-                    sums[number][0] += loc_real * (src_real + src_imag)
-                    sums[number][1] += less * src_imag
-                    sums[number][2] += more * src_real
-            real_sums += [both - imag for both, imag, real in sums]
-            imag_sums += [both - real for both, imag, real in sums]
-        cross = jnp.concatenate(
-            [
-                jnp.concatenate(real_sums, axis=0).astype(jnp.bfloat16),
-                jnp.concatenate(imag_sums, axis=0).astype(jnp.bfloat16),
-            ],
-            axis=1,
-        )
-        total += jnp.dot(
-            cross,
-            lags_ref[2 * tile * LANES : 2 * (tile + 1) * LANES],
-            preferred_element_type=f32,
-        )
-    out_ref[...] = total
-    part = keep_ref.shape[0]
-    keep_ref[...] = out_ref[pl.ds(pl.multiple_of(half * part, 8), part)]
-    send_ref[...] = out_ref[pl.ds(pl.multiple_of((span_total - 1 - half) * part, 8), part)]
+    send_ref[...] = lag_products(white_ref, lags_ref, rows, 0, block_total // span_total)
+
+
+def keep_kernel(rows, first, number, white_ref, lags_ref, keep_ref):
+    keep_ref[...] = lag_products(white_ref, lags_ref, rows, first, number)
 
 
 def gathered_body(records, record_channel, record_piece, fir_taps, window_starts, source_slot):
@@ -347,9 +349,11 @@
     half_rows = block_total // span_total * CH_DEV
     half_shape = jax.ShapeDtypeStruct((half_rows, LAGS), jnp.float32)
     tables = [wide_table(), band_table(), lag_table()]
-    keep, send = pl.pallas_call(
+    lags = jnp.asarray(tables[2])
+    half_count = block_total // span_total
+    send, white = pl.pallas_call(
         lambda *refs: correlate_kernel(block_total, span_total, *refs),
-        out_shape=(half_shape, half_shape),
+        out_shape=(half_shape, jax.ShapeDtypeStruct((WIN_DEV * rows, WL), jnp.float32)),
         in_specs=[hbm, hbm, smem] + [vmem] * (block_total + 2),
         out_specs=(vmem, vmem),
         scratch_shapes=[
@@ -357,8 +361,6 @@
             pltpu.VMEM((2 * (OUTS + AUX), PIECES * rows), jnp.float32),
             pltpu.VMEM((rows, SPAN + LANES), jnp.float32),
             pltpu.VMEM((WIN_DEV * rows, WL), jnp.float32),
-            pltpu.VMEM((WIN_DEV * rows, WL), jnp.float32),
-            pltpu.VMEM((block_total * CH_DEV, LAGS), jnp.float32),
             pltpu.VMEM(unit_shape, jnp.int16),
             pltpu.SMEM((WIN_DEV,), jnp.int32),
             pltpu.SemaphoreType.DMA((2,)),
@@ -370,9 +372,18 @@
         window_starts,
         source_slot,
         *[units[step] for step in ORDER],
-        *[jnp.asarray(table) for table in tables],
+        *[jnp.asarray(table) for table in tables[:2]],
+        lags,
     )
     other = lax.ppermute(send, "win", [(i, i ^ 1) for i in range(span_total)])
+    keep = pl.pallas_call(
+        lambda *refs: keep_kernel(rows, half_count, half_count, *refs),
+        out_shape=half_shape,
+        in_specs=[vmem, vmem],
+        out_specs=vmem,
+        compiler_params=pltpu.CompilerParams(vmem_limit_bytes=32 << 20),
+        name="keep",
+    )(white, lags)
     return (keep + other).reshape(block_total // span_total, CH_DEV, LAGS)
 
 

time: 24.3 us -> 23.5 us (0.967)
  starting transfers between devices: 12 us -> 11.2 us
    ppermute x7, starting transfers between devices: 12 us -> 11.1 us  [swap(): lax.ppermute(value, 'chan', [(i, i ^ step) for i in range(block_total)])]
    ppermute x1, waiting for transfers between devices: 1.24 us -> 0.79 us  [gathered_body(): other = lax.ppermute(send, 'win', [(i, i ^ 1) for i in range(span_total)])]
    pallas_call x0 -> x1, Pallas kernels: none -> 0.45 us  [gathered_body(): pl.pallas_call(lambda *refs: keep_kernel(rows, half_count, half_count, *r...]
    ppermute x7, waiting for transfers between devices: 3.55 us -> 3.91 us  [swap(): lax.ppermute(value, 'chan', [(i, i ^ step) for i in range(block_total)])]
    pallas_call x1, Pallas kernels: 3.76 us -> 3.5 us  [gathered_body(): pl.pallas_call(lambda *refs: correlate_kernel(block_total, span_total, *r...]
  transfers between devices with their start and end apart: 8 -> 8, of which waited for: 5 -> 6; matrix products, arithmetic and copies ran while one was open for 0% -> 0% of each run, Pallas kernels for 0% -> 2%
where the time goes in v4:
time: 23.5 us; the launch traced here: 23.4 us
  starting transfers between devices  11.2 us (48%)
  Pallas kernels  6.15 us (26%)
  waiting for transfers between devices  4.7 us (20%)
  between operations  0.73 us (3%)
  other arithmetic  0.64 us (3%)
    ppermute x7, starting transfers between devices, swap(): lax.ppermute(value, 'chan', [(i, i ^ step) for i in range(block_total)])  11.1 us
    ppermute x7, waiting for transfers between devices, swap(): lax.ppermute(value, 'chan', [(i, i ^ step) for i in range(block_total)])  3.91 us
    pallas_call x1, Pallas kernels, gathered_body(): pl.pallas_call(lambda *refs: correlate_kernel(block_total, span_total, *r...  3.5 us
    pallas_call x1, Pallas kernels, gathered_body(): pl.pallas_call(filter_kernel, out_shape=(jax.ShapeDtypeStruct(unit_shape,...  2.2 us
    ppermute x1, waiting for transfers between devices, gathered_body(): other = lax.ppermute(send, 'win', [(i, i ^ 1) for i in range(span_total)])  0.79 us
    add x1, other arithmetic, gathered_body(): return (keep + other).reshape(block_total // span_total, CH_DEV, LAGS)  0.64 us
  transfers between devices with their start and end apart: 8, of which 6 were waited for; matrix products, arithmetic and copies ran while one was open for 0% of the time, Pallas kernels for 2%

profile of v4, /device:TPU:0, one launch (start us, length us, event | category | flops | bytes accessed | tf_op | source)
XLA Modules:
  0.0 23.4 jit_solution(8971523243339302213)
XLA Ops:
  0.7 0.0 copy-start
  0.7 0.0 copy-start.1
  0.7 0.0 copy-start.2
  0.7 0.0 copy-start.3
  0.7 2.2 %filter.1 = (s16[144,256]{1,0:T(8,128)(2,1)}, s16[16384,256]{1,0:T(8,128)(2,1)}) custom-call(bf16[256,512]{1,0:T(8,128)(2,1)} %records_hbm.1, s32[256]{0:T(256)} %channel_hbm.1, s32[256]{0:T(256)} %piece_hbm.1, bf16[32]{0:T(256)(128)(2,1)} %taps_hbm.1, s32[1]{0:T(128)S(6)} %copy.10.slot_hbm.refs_2_), custom_call_target="tpu_custom_call" | custom-call | flops 10000000000 | bytes 1048576 | tf_op jit(solution)/shard_map/filter/pallas_call | solution.py:320
  2.9 4.1 %collective-permute-start = (s16[144,256]{1,0:T(8,128)(2,1)}, s16[144,256]{1,0:T(8,128)(2,1)S(1)}, u32[]{:S(2)}, u32[]{:S(2)}) collective-permute-start(s16[144,256]{1,0:T(8,128)(2,1)} %get-tuple-element.10), channel_id=1, source_target_pairs={{0,8},{2,10},{4,12},{6,14},{8,0},{10,2},{12,4},{14,6},{1,9},{3,11}... | collective-permute-start | bytes 221192 | tf_op jit(solution)/shard_map/ppermute | solution.py:343
  7.0 1.5 %collective-permute-start.5 = (s16[144,256]{1,0:T(8,128)(2,1)}, s16[144,256]{1,0:T(8,128)(2,1)S(1)}, u32[]{:S(2)}, u32[]{:S(2)}) collective-permute-start(s16[144,256]{1,0:T(8,128)(2,1)} %get-tuple-element.10), channel_id=1, source_target_pairs={{0,2},{2,0},{4,6},{6,4},{8,10},{10,8},{12,14},{14,12},{1,3},{3,1},... | collective-permute-start | bytes 221192 | tf_op jit(solution)/shard_map/ppermute | solution.py:343
  8.5 1.6 %collective-permute-start.4 = (s16[144,256]{1,0:T(8,128)(2,1)}, s16[144,256]{1,0:T(8,128)(2,1)S(1)}, u32[]{:S(2)}, u32[]{:S(2)}) collective-permute-start(s16[144,256]{1,0:T(8,128)(2,1)} %get-tuple-element.10), channel_id=1, source_target_pairs={{0,4},{2,6},{4,0},{6,2},{8,12},{10,14},{12,8},{14,10},{1,5},{3,7},... | collective-permute-start | bytes 221192 | tf_op jit(solution)/shard_map/ppermute | solution.py:343
  10.1 0.4 %collective-permute-start.3 = (s16[144,256]{1,0:T(8,128)(2,1)}, s16[144,256]{1,0:T(8,128)(2,1)S(1)}, u32[]{:S(2)}, u32[]{:S(2)}) collective-permute-start(s16[144,256]{1,0:T(8,128)(2,1)} %get-tuple-element.10), channel_id=1, source_target_pairs={{0,6},{2,4},{4,2},{6,0},{8,14},{10,12},{12,10},{14,8},{1,7},{3,5},... | collective-permute-start | bytes 221192 | tf_op jit(solution)/shard_map/ppermute | solution.py:343
  10.5 0.4 %collective-permute-done.refs_7_ = s16[144,256]{1,0:T(8,128)(2,1)S(1)} collective-permute-done((s16[144,256]{1,0:T(8,128)(2,1)}, s16[144,256]{1,0:T(8,128)(2,1)S(1)}, u32[]{:S(2)}, u32[]{:S(2)}) %collective-permute-start) | collective-permute-done | bytes 73760 | tf_op jit(solution)/shard_map/ppermute | solution.py:343
  10.9 1.6 %collective-permute-start.6 = (s16[144,256]{1,0:T(8,128)(2,1)S(1)}, s16[144,256]{1,0:T(8,128)(2,1)S(1)}, u32[]{:S(2)}, u32[]{:S(2)}) collective-permute-start(s16[144,256]{1,0:T(8,128)(2,1)S(1)} %collective-permute-done.refs_7_), channel_id=1, source_target_pairs={{0,2},{2,0},{4,6},{6,4},{8,10},{10,8},{12,14},{14,12},{1,3},{3,1},... | collective-permute-start | bytes 221192 | tf_op jit(solution)/shard_map/ppermute | solution.py:343
  12.5 1.1 %collective-permute-start.2 = (s16[144,256]{1,0:T(8,128)(2,1)S(1)}, s16[144,256]{1,0:T(8,128)(2,1)S(1)}, u32[]{:S(2)}, u32[]{:S(2)}) collective-permute-start(s16[144,256]{1,0:T(8,128)(2,1)S(1)} %collective-permute-done.refs_7_), channel_id=1, source_target_pairs={{0,6},{2,4},{4,2},{6,0},{8,14},{10,12},{12,10},{14,8},{1,7},{3,5},... | collective-permute-start | bytes 221192 | tf_op jit(solution)/shard_map/ppermute | solution.py:343
  13.6 0.0 collective-permute-done.5.refs_8_
  13.6 0.8 %collective-permute-start.1 = (s16[144,256]{1,0:T(8,128)(2,1)S(1)}, s16[144,256]{1,0:T(8,128)(2,1)S(1)}, u32[]{:S(2)}, u32[]{:S(2)}) collective-permute-start(s16[144,256]{1,0:T(8,128)(2,1)S(1)} %collective-permute-done.refs_7_), channel_id=1, source_target_pairs={{0,4},{2,6},{4,0},{6,2},{8,12},{10,14},{12,8},{14,10},{1,5},{3,7},... | collective-permute-start | bytes 221192 | tf_op jit(solution)/shard_map/ppermute | solution.py:343
  14.4 0.0 collective-permute-done.4.refs_6_
  14.4 1.3 %collective-permute-done.3.refs_5_ = s16[144,256]{1,0:T(8,128)(2,1)S(1)} collective-permute-done((s16[144,256]{1,0:T(8,128)(2,1)}, s16[144,256]{1,0:T(8,128)(2,1)S(1)}, u32[]{:S(2)}, u32[]{:S(2)}) %collective-permute-start.3) | collective-permute-done | bytes 73760 | tf_op jit(solution)/shard_map/ppermute | solution.py:343
  15.6 0.7 %collective-permute-done.6.refs_9_ = s16[144,256]{1,0:T(8,128)(2,1)S(1)} collective-permute-done((s16[144,256]{1,0:T(8,128)(2,1)S(1)}, s16[144,256]{1,0:T(8,128)(2,1)S(1)}, u32[]{:S(2)}, u32[]{:S(2)}) %collective-permute-start.6) | collective-permute-done | bytes 73760 | tf_op jit(solution)/shard_map/ppermute | solution.py:343
  16.3 1.4 %collective-permute-done.2.refs_4_ = s16[144,256]{1,0:T(8,128)(2,1)S(1)} collective-permute-done((s16[144,256]{1,0:T(8,128)(2,1)S(1)}, s16[144,256]{1,0:T(8,128)(2,1)S(1)}, u32[]{:S(2)}, u32[]{:S(2)}) %collective-permute-start.2) | collective-permute-done | bytes 73760 | tf_op jit(solution)/shard_map/ppermute | solution.py:343
  17.7 0.2 collective-permute-done.1.refs_3_
  17.9 0.0 copy-done
  17.9 0.0 copy-done.1
  17.9 0.0 copy-done.2
  17.9 0.0 copy-done.3
  17.9 3.5 %correlate.1 = (f32[64,256]{1,0:T(8,128)S(1)}, f32[192,1024]{1,0:T(8,128)S(1)}) custom-call(s16[16384,256]{1,0:T(8,128)(2,1)} %get-tuple-element.9.refs_0_, s32[8]{0:T(128)S(1)} %copy-done.3, s32[1]{0:T(128)S(6)} %copy.10.slot_hbm.refs_2_, s16[144,256]{1,0:T(8,128)(2,1)S(1)} %collective-permute-done.1.refs_3_, ...), custom_call_target="tpu_custom_call" | custom-call | tf_op jit(solution)/shard_map/correlate/pallas_call | solution.py:354
  21.4 0.1 collective-permute-start.7
  21.5 0.5 %keep.1 = f32[64,256]{1,0:T(8,128)S(1)} custom-call(f32[192,1024]{1,0:T(8,128)S(1)} %get-tuple-element.11.refs_0_, bf16[1024,256]{1,0:T(8,128)(2,1)S(1)} %copy-done.1), custom_call_target="tpu_custom_call" | custom-call | tf_op jit(solution)/shard_map/keep/pallas_call | solution.py:379
  22.0 0.8 %collective-permute-done.7 = f32[64,256]{1,0:T(8,128)S(1)} collective-permute-done((f32[64,256]{1,0:T(8,128)S(1)}, f32[64,256]{1,0:T(8,128)S(1)}, u32[]{:S(2)}, u32[]{:S(2)}) %collective-permute-start.7) | collective-permute-done | bytes 65568 | tf_op jit(solution)/shard_map/ppermute | solution.py:378
  22.8 0.6 %add.3 = f32[64,256]{1,0:T(8,128)} add(f32[64,256]{1,0:T(8,128)S(1)} %keep.1, f32[64,256]{1,0:T(8,128)S(1)} %collective-permute-done.7) | non-fusion elementwise | flops 16384 | bytes 196608 | tf_op jit(solution)/shard_map/add | solution.py:387
Async XLA Ops:
  0.7 17.3 %copy-start = (bf16[1040,1024]{1,0:T(8,128)(2,1)S(1)}, bf16[1040,1024]{1,0:T(8,128)(2,1)}, u32[]{:S(2)}) copy-start(bf16[1040,1024]{1,0:T(8,128)(2,1)} %constant.7.clone.refs_10_) | copy-start | bytes 6389764
  0.7 17.2 %copy-start.1 = (bf16[1024,256]{1,0:T(8,128)(2,1)S(1)}, bf16[1024,256]{1,0:T(8,128)(2,1)}, u32[]{:S(2)}) copy-start(bf16[1024,256]{1,0:T(8,128)(2,1)} %constant.6.clone.refs_12_.refs_1_) | copy-start | bytes 1572868
  0.7 17.2 %copy-start.2 = (bf16[512,512]{1,0:T(8,128)(2,1)S(1)}, bf16[512,512]{1,0:T(8,128)(2,1)}, u32[]{:S(2)}) copy-start(bf16[512,512]{1,0:T(8,128)(2,1)} %constant.8.clone.refs_11_) | copy-start | bytes 1572868
  0.7 17.2 %copy-start.3 = (s32[8]{0:T(128)S(1)}, s32[8]{0:T(128)}, u32[]{:S(2)}) copy-start(s32[8]{0:T(128)} %refs_1_.2) | copy-start | bytes 100
  2.9 8.0 %collective-permute-start = (s16[144,256]{1,0:T(8,128)(2,1)}, s16[144,256]{1,0:T(8,128)(2,1)S(1)}, u32[]{:S(2)}, u32[]{:S(2)}) collective-permute-start(s16[144,256]{1,0:T(8,128)(2,1)} %get-tuple-element.10), channel_id=1, source_target_pairs={{0,8},{2,10},{4,12},{6,14},{8,0},{10,2},{12,4},{14,6},{1,9},{3,11}... | collective-permute-start | bytes 221192 | tf_op jit(solution)/shard_map/ppermute | solution.py:343
  7.0 6.5 %collective-permute-start.5 = (s16[144,256]{1,0:T(8,128)(2,1)}, s16[144,256]{1,0:T(8,128)(2,1)S(1)}, u32[]{:S(2)}, u32[]{:S(2)}) collective-permute-start(s16[144,256]{1,0:T(8,128)(2,1)} %get-tuple-element.10), channel_id=1, source_target_pairs={{0,2},{2,0},{4,6},{6,4},{8,10},{10,8},{12,14},{14,12},{1,3},{3,1},... | collective-permute-start | bytes 221192 | tf_op jit(solution)/shard_map/ppermute | solution.py:343
  8.5 5.9 %collective-permute-start.4 = (s16[144,256]{1,0:T(8,128)(2,1)}, s16[144,256]{1,0:T(8,128)(2,1)S(1)}, u32[]{:S(2)}, u32[]{:S(2)}) collective-permute-start(s16[144,256]{1,0:T(8,128)(2,1)} %get-tuple-element.10), channel_id=1, source_target_pairs={{0,4},{2,6},{4,0},{6,2},{8,12},{10,14},{12,8},{14,10},{1,5},{3,7},... | collective-permute-start | bytes 221192 | tf_op jit(solution)/shard_map/ppermute | solution.py:343
  10.1 5.5 %collective-permute-start.3 = (s16[144,256]{1,0:T(8,128)(2,1)}, s16[144,256]{1,0:T(8,128)(2,1)S(1)}, u32[]{:S(2)}, u32[]{:S(2)}) collective-permute-start(s16[144,256]{1,0:T(8,128)(2,1)} %get-tuple-element.10), channel_id=1, source_target_pairs={{0,6},{2,4},{4,2},{6,0},{8,14},{10,12},{12,10},{14,8},{1,7},{3,5},... | collective-permute-start | bytes 221192 | tf_op jit(solution)/shard_map/ppermute | solution.py:343
  10.9 5.4 %collective-permute-start.6 = (s16[144,256]{1,0:T(8,128)(2,1)S(1)}, s16[144,256]{1,0:T(8,128)(2,1)S(1)}, u32[]{:S(2)}, u32[]{:S(2)}) collective-permute-start(s16[144,256]{1,0:T(8,128)(2,1)S(1)} %collective-permute-done.refs_7_), channel_id=1, source_target_pairs={{0,2},{2,0},{4,6},{6,4},{8,10},{10,8},{12,14},{14,12},{1,3},{3,1},... | collective-permute-start | bytes 221192 | tf_op jit(solution)/shard_map/ppermute | solution.py:343
  12.5 5.3 %collective-permute-start.2 = (s16[144,256]{1,0:T(8,128)(2,1)S(1)}, s16[144,256]{1,0:T(8,128)(2,1)S(1)}, u32[]{:S(2)}, u32[]{:S(2)}) collective-permute-start(s16[144,256]{1,0:T(8,128)(2,1)S(1)} %collective-permute-done.refs_7_), channel_id=1, source_target_pairs={{0,6},{2,4},{4,2},{6,0},{8,14},{10,12},{12,10},{14,8},{1,7},{3,5},... | collective-permute-start | bytes 221192 | tf_op jit(solution)/shard_map/ppermute | solution.py:343
  13.6 4.4 %collective-permute-start.1 = (s16[144,256]{1,0:T(8,128)(2,1)S(1)}, s16[144,256]{1,0:T(8,128)(2,1)S(1)}, u32[]{:S(2)}, u32[]{:S(2)}) collective-permute-start(s16[144,256]{1,0:T(8,128)(2,1)S(1)} %collective-permute-done.refs_7_), channel_id=1, source_target_pairs={{0,4},{2,6},{4,0},{6,2},{8,12},{10,14},{12,8},{14,10},{1,5},{3,7},... | collective-permute-start | bytes 221192 | tf_op jit(solution)/shard_map/ppermute | solution.py:343
  21.4 1.3 %collective-permute-start.7 = (f32[64,256]{1,0:T(8,128)S(1)}, f32[64,256]{1,0:T(8,128)S(1)}, u32[]{:S(2)}, u32[]{:S(2)}) collective-permute-start(f32[64,256]{1,0:T(8,128)S(1)} %get-tuple-element.12), channel_id=1, source_target_pairs={{0,1},{1,0},{2,3},{3,2},{4,5},{5,4},{6,7},{7,6},{8,9},{9,8},{10,11... | collective-permute-start | bytes 196616 | tf_op jit(solution)/shard_map/ppermute | solution.py:378

commit v5 on v4

--- a/solution.py
+++ b/solution.py
@@ -33,10 +33,13 @@
 SLOT_ROW = SPILL + 2
 FILTER_VMEM = 56 << 20
 FLOPS = 10**10
-CORRELATE_VMEM = 48 << 20
-LOCAL_ROWS = 16384
-LAST_HOP = {1: 1, 2: 2, 3: 3, 4: 4, 6: 2, 5: 1, 7: 3}
-ORDER = (6, 7, 3, 2, 4, 1, 5)
+EARLY_VMEM = 44 << 20
+EARLY_FLOPS = 10**9
+CORRELATE_VMEM = 40 << 20
+LOCAL_ROWS = 32768
+LAST_HOP = {1: 1, 2: 2, 3: 3, 4: 4, 6: 6, 5: 1, 7: 3}
+EARLY = (0, 1, 2, 6, 3, 4)
+LATE = (5, 7)
 CODE = 23000.0
 
 
@@ -191,83 +194,112 @@
     return total
 
 
+def pick_rows(pick_ref, key, first, group, wanted):
+    shape = (2 * group, key.shape[1])
+    key = jnp.broadcast_to(key, shape)
+    for pair in range(PIECES // 2):
+        pick_ref[pair * 2 * group : (pair + 1) * 2 * group, first : first + shape[1]] = jnp.where(
+            wanted + 2 * pair == key, 1.0, 0.0
+        ).astype(jnp.bfloat16)
+
+
+def wanted_own(me, count):
+    row = lax.broadcasted_iota(jnp.int32, (2 * CH_DEV, count), 0)
+    odd = (row >= CH_DEV).astype(jnp.int32)
+    return (me * CH_DEV + row - odd * CH_DEV) * PIECES + odd
+
+
+def selected(data, pick):
+    return lax.dot_general(data, pick, (((1,), (1,)), ((), ())), preferred_element_type=jnp.float32)
+
+
+def early_kernel(early_total, *refs):
+    local_hbm = refs[0]
+    units_ref = refs[1:early_total]
+    own_ref, data_ref, side_ref, pick_ref, unit_ref, arrived = refs[early_total:]
+    copy = pltpu.make_async_copy(local_hbm.at[pl.ds(0, OUTS + AUX)], unit_ref, arrived)
+    copy.start()
+    count = unit_ref.shape[1]
+    wanted = wanted_own(lax.axis_index("chan"), count)
+
+    def take(unit, number):
+        at = slice(number * count, (number + 1) * count)
+        codes = unit[...].astype(jnp.int32)
+        first, second = halves(codes)
+        data_ref[: OUTS + AUX, at] = first
+        data_ref[OUTS + AUX :, at] = second
+        side_ref[:, at] = codes[OUTS:]
+        pick_rows(pick_ref, codes[OUTS + KEY_ROW : OUTS + KEY_ROW + 1], number * count, CH_DEV, wanted)
+
+    for number in range(1, early_total):
+        take(units_ref[number - 1], number)
+    own_ref[...] = selected(data_ref[:, count:], pick_ref[:, count:])
+    copy.wait()
+    take(unit_ref, 0)
+    own_ref[...] += selected(data_ref[:, :count], pick_ref[:, :count])
+
+
+def samples_of(picked, group):
+    code = picked[: OUTS + AUX] * 256.0 + picked[OUTS + AUX :]
+    scale = jnp.exp2(code[OUTS + SCALE_ROW : OUTS + SCALE_ROW + 1])
+    main_part = decoded(code[:OUTS], scale)
+    spill_part = pltpu.roll(decoded(code[OUTS:], scale), group, 1)
+    row = lax.broadcasted_iota(jnp.int32, spill_part.shape, 0)
+    column = lax.broadcasted_iota(jnp.int32, spill_part.shape, 1)
+    spill_part = jnp.where((row < SPILL) & (column >= group), spill_part, 0.0)
+    return jnp.transpose(jnp.concatenate([main_part[:AUX] + spill_part, main_part[AUX:]], axis=0))
+
+
 def correlate_kernel(block_total, span_total, *refs):
-    local_hbm, starts_hbm, slot_ref = refs[:3]
-    refs = refs[1:]
-    units_ref = dict(zip(ORDER, refs[2 : block_total + 1]))
-    wide_ref, band_ref, lags_ref, send_ref, white_ref = refs[block_total + 1 : block_total + 6]
-    pick_ref, pick_sum_ref, dec_ref, seg_ref, unit_ref, starts_ref, arrived = refs[block_total + 6 :]
     f32 = jnp.float32
-    pairs = (
-        (local_hbm.at[pl.ds(0, OUTS + AUX)], unit_ref),
-        (starts_hbm, starts_ref),
-    )
-    copies = [
-        pltpu.make_async_copy(source, target, arrived.at[number])
-        for number, (source, target) in enumerate(pairs)
-    ]
-    for copy in copies:
-        copy.start()
+    own_ref, data_ref, side_ref, starts_hbm, slot_ref = refs[:5]
+    refs = refs[5:]
+    units_ref = dict(zip(LATE, refs))
+    refs = refs[len(LATE) :]
+    wide_ref, band_ref, lags_ref, send_ref, white_ref = refs[:5]
+    pick_own_ref, pick_src_ref, dec_ref, seg_ref, starts_ref, arrived = refs[5:]
+    copy = pltpu.make_async_copy(starts_hbm, starts_ref, arrived)
+    copy.start()
     me = lax.axis_index("chan")
     half = lax.axis_index("win")
     rows = CH_DEV + block_total
-    count = unit_ref.shape[1]
-
-    def side_of(unit):
-        return unit[OUTS:].astype(jnp.int32)
-
-    sides = {step: side_of(unit) for step, unit in units_ref.items()}
-    row = lax.broadcasted_iota(jnp.int32, (2 * rows, count), 0)
-    odd = (row >= rows).astype(jnp.int32)
-    row = row - odd * rows
-    source = (row - CH_DEV + (1 + half) * (block_total // span_total)) % block_total
-    source = jnp.where(row >= CH_DEV, source, -1)
-    channel = me * CH_DEV + row
-    channel = jnp.where(source == me, source * CH_DEV + slot_ref[0], channel)
+    count = side_ref.shape[1] // len(EARLY)
+    late = {step: unit[...].astype(jnp.int32) for step, unit in units_ref.items()}
+    sides = {step: side_ref[:, n * count : (n + 1) * count] for n, step in enumerate(EARLY)}
+    sides |= {step: codes[OUTS:] for step, codes in late.items()}
+    row = lax.broadcasted_iota(jnp.int32, (2 * block_total, count), 0)
+    odd = (row >= block_total).astype(jnp.int32)
+    source = (row + (1 + half) * (block_total // span_total)) % block_total
+    channel = source * CH_DEV + slot_ref[0]
     for step, side in sides.items():
-        slot = jnp.broadcast_to(side[SLOT_ROW : SLOT_ROW + 1], (2 * rows, count))
-        channel = jnp.where(source == (me ^ step), source * CH_DEV + slot, channel)
+        if step:
+            slot = jnp.broadcast_to(side[SLOT_ROW : SLOT_ROW + 1], source.shape)
+            channel = jnp.where(source == (me ^ step), source * CH_DEV + slot, channel)
     wanted = channel * PIECES + odd
-
-    def pick(step, side):
-        key = jnp.broadcast_to(side[KEY_ROW : KEY_ROW + 1], (2 * rows, count))
-        for pair in range(PIECES // 2):
-            pick_ref[
-                pair * 2 * rows : (pair + 1) * 2 * rows, step * count : (step + 1) * count
-            ] = jnp.where(wanted + 2 * pair == key, 1.0, 0.0).astype(jnp.bfloat16)
-
-    def select(steps, units):
-        for step in steps:
-            pick(step, sides[step])
-        codes = jnp.concatenate([units[step][...].astype(jnp.int32) for step in steps], axis=1)
-        return lax.dot_general(
-            jnp.concatenate(halves(codes), axis=0),
-            pick_ref[:, steps[0] * count : (steps[-1] + 1) * count],
-            (((1,), (1,)), ((), ())),
-            preferred_element_type=f32,
-        )
-
-    pick_sum_ref[...] = select(list(range(1, block_total)), units_ref)
-    copies[0].wait()
-    sides[0] = side_of(unit_ref)
-    picked = select([0], [unit_ref]) + pick_sum_ref[...]
-    picked = picked[: OUTS + AUX] * 256.0 + picked[OUTS + AUX :]
-    scale = jnp.exp2(picked[OUTS + SCALE_ROW : OUTS + SCALE_ROW + 1])
-    main_part = decoded(picked[:OUTS], scale)
-    spill_part = pltpu.roll(decoded(picked[OUTS:], scale), rows, 1)
-    row = lax.broadcasted_iota(jnp.int32, spill_part.shape, 0)
-    column = lax.broadcasted_iota(jnp.int32, spill_part.shape, 1)
-    spill_part = jnp.where((row < SPILL) & (column >= rows), spill_part, 0.0)
-    samples = jnp.concatenate([main_part[:AUX] + spill_part, main_part[AUX:]], axis=0)
-    samples = jnp.transpose(samples)
+    own = wanted_own(me, count)
+    for number, step in enumerate(EARLY + LATE):
+        key = sides[step][KEY_ROW : KEY_ROW + 1]
+        pick_rows(pick_src_ref, key, number * count, block_total, wanted)
+        if step in late:
+            pick_rows(pick_own_ref, key, (number - len(EARLY)) * count, CH_DEV, own)
+    codes = jnp.concatenate([late[step] for step in LATE], axis=1)
+    late_data = jnp.concatenate(halves(codes), axis=0)
+    split = len(EARLY) * count
+    picked_src = selected(data_ref[...], pick_src_ref[:, :split])
+    picked_src += selected(late_data, pick_src_ref[:, split:])
+    picked_own = own_ref[...] + selected(late_data, pick_own_ref[...])
+    samples = samples_of(picked_own, CH_DEV)
+    sources = samples_of(picked_src, block_total)
     for piece in range(PIECES):
-        dec_ref[:, piece * OUTS : (piece + 1) * OUTS] = samples[piece * rows : (piece + 1) * rows]
+        at = slice(piece * OUTS, (piece + 1) * OUTS)
+        dec_ref[:CH_DEV, at] = samples[piece * CH_DEV : (piece + 1) * CH_DEV]
+        dec_ref[CH_DEV:, at] = sources[piece * block_total : (piece + 1) * block_total]
     dec_ref[:, SPAN:] = jnp.zeros((rows, LANES), f32)
     lane = lax.broadcasted_iota(jnp.int32, (rows, LANES), 1)
     extra = wide_ref[WL:].astype(f32)
     taper = extra[0:1] + extra[1:2] + extra[2:3]
     inverse = (extra[3:4] + extra[4:5] + extra[5:6])[:, :NF]
-    copies[1].wait()
+    copy.wait()
     for window in range(WIN_DEV):
         start = starts_ref[window]
         base = pl.multiple_of((start >> 7) * LANES, LANES)
@@ -351,27 +383,47 @@
     tables = [wide_table(), band_table(), lag_table()]
     lags = jnp.asarray(tables[2])
     half_count = block_total // span_total
+    data_shape = (2 * unit_shape[0], len(EARLY) * count)
+    own, data, side = pl.pallas_call(
+        lambda *refs: early_kernel(len(EARLY), *refs),
+        out_shape=(
+            jax.ShapeDtypeStruct((2 * unit_shape[0], PIECES * CH_DEV), jnp.float32),
+            jax.ShapeDtypeStruct(data_shape, jnp.bfloat16),
+            jax.ShapeDtypeStruct((AUX, len(EARLY) * count), jnp.int32),
+        ),
+        in_specs=[hbm] + [vmem] * (len(EARLY) - 1),
+        out_specs=(vmem, vmem, vmem),
+        scratch_shapes=[
+            pltpu.VMEM((PIECES * CH_DEV, len(EARLY) * count), jnp.bfloat16),
+            pltpu.VMEM(unit_shape, jnp.int16),
+            pltpu.SemaphoreType.DMA,
+        ],
+        compiler_params=pltpu.CompilerParams(vmem_limit_bytes=EARLY_VMEM),
+        cost_estimate=pl.CostEstimate(flops=EARLY_FLOPS, bytes_accessed=1 << 20, transcendentals=0),
+        name="early",
+    )(local, *[units[step] for step in EARLY[1:]])
     send, white = pl.pallas_call(
         lambda *refs: correlate_kernel(block_total, span_total, *refs),
         out_shape=(half_shape, jax.ShapeDtypeStruct((WIN_DEV * rows, WL), jnp.float32)),
-        in_specs=[hbm, hbm, smem] + [vmem] * (block_total + 2),
+        in_specs=[vmem, vmem, vmem, hbm, smem] + [vmem] * (len(LATE) + 3),
         out_specs=(vmem, vmem),
         scratch_shapes=[
-            pltpu.VMEM((PIECES * rows, block_total * count), jnp.bfloat16),
-            pltpu.VMEM((2 * (OUTS + AUX), PIECES * rows), jnp.float32),
+            pltpu.VMEM((PIECES * CH_DEV, len(LATE) * count), jnp.bfloat16),
+            pltpu.VMEM((PIECES * block_total, block_total * count), jnp.bfloat16),
             pltpu.VMEM((rows, SPAN + LANES), jnp.float32),
             pltpu.VMEM((WIN_DEV * rows, WL), jnp.float32),
-            pltpu.VMEM(unit_shape, jnp.int16),
             pltpu.SMEM((WIN_DEV,), jnp.int32),
-            pltpu.SemaphoreType.DMA((2,)),
+            pltpu.SemaphoreType.DMA,
         ],
         compiler_params=pltpu.CompilerParams(vmem_limit_bytes=CORRELATE_VMEM),
         name="correlate",
     )(
-        local,
+        own,
+        data,
+        side,
         window_starts,
         source_slot,
-        *[units[step] for step in ORDER],
+        *[units[step] for step in LATE],
         *[jnp.asarray(table) for table in tables[:2]],
         lags,
     )

time: 23.5 us -> 22.9 us (0.974)
  waiting for transfers between devices: 4.7 us -> 3.78 us
    pallas_call x0 -> x1, Pallas kernels: none -> 1.15 us  [gathered_body(): pl.pallas_call(lambda *refs: early_kernel(len(EARLY), *refs), out_shape=(...]
    ppermute x7, waiting for transfers between devices: 3.91 us -> 2.97 us  [swap(): lax.ppermute(value, 'chan', [(i, i ^ step) for i in range(block_total)])]
    pallas_call x1, Pallas kernels: 3.5 us -> 2.67 us  [gathered_body(): pl.pallas_call(lambda *refs: correlate_kernel(block_total, span_total, *r...]
  transfers between devices with their start and end apart: 8 -> 8, of which waited for: 6 -> 3; matrix products, arithmetic and copies ran while one was open for 0% -> 0% of each run, Pallas kernels for 2% -> 7%
where the time goes in v5:
time: 22.9 us; the launch traced here: 22.8 us
  starting transfers between devices  11.2 us (49%)
  Pallas kernels  6.3 us (28%)
  waiting for transfers between devices  3.78 us (17%)
  between operations  0.77 us (3%)
  other arithmetic  0.64 us (3%)
    ppermute x7, starting transfers between devices, swap(): lax.ppermute(value, 'chan', [(i, i ^ step) for i in range(block_total)])  11.2 us
    ppermute x7, waiting for transfers between devices, swap(): lax.ppermute(value, 'chan', [(i, i ^ step) for i in range(block_total)])  2.97 us
    pallas_call x1, Pallas kernels, gathered_body(): pl.pallas_call(lambda *refs: correlate_kernel(block_total, span_total, *r...  2.67 us
    pallas_call x1, Pallas kernels, gathered_body(): pl.pallas_call(filter_kernel, out_shape=(jax.ShapeDtypeStruct(unit_shape,...  2.05 us
    pallas_call x1, Pallas kernels, gathered_body(): pl.pallas_call(lambda *refs: early_kernel(len(EARLY), *refs), out_shape=(...  1.15 us
    ppermute x1, waiting for transfers between devices, gathered_body(): other = lax.ppermute(send, 'win', [(i, i ^ 1) for i in range(span_total)])  0.81 us
    add x1, other arithmetic, gathered_body(): return (keep + other).reshape(block_total // span_total, CH_DEV, LAGS)  0.64 us
  transfers between devices with their start and end apart: 8, of which 3 were waited for; matrix products, arithmetic and copies ran while one was open for 0% of the time, Pallas kernels for 7%

profile of v5, /device:TPU:0, one launch (start us, length us, event | category | flops | bytes accessed | tf_op | source)
XLA Modules:
  0.0 22.8 jit_solution(15413727426526358070)
XLA Ops:
  0.7 2.1 %filter.1 = (s16[144,256]{1,0:T(8,128)(2,1)}, s16[32768,256]{1,0:T(8,128)(2,1)}) custom-call(bf16[256,512]{1,0:T(8,128)(2,1)} %records_hbm.1, s32[256]{0:T(256)} %channel_hbm.1, s32[256]{0:T(256)} %piece_hbm.1, bf16[32]{0:T(256)(128)(2,1)} %taps_hbm.1, s32[1]{0:T(128)S(6)} %copy.10.slot_hbm.refs_4_), custom_call_target="tpu_custom_call" | custom-call | flops 10000000000 | bytes 1048576 | tf_op jit(solution)/shard_map/filter/pallas_call | solution.py:352
  2.7 0.0 copy-start
  2.7 0.0 copy-start.1
  2.7 0.0 copy-start.2
  2.8 0.0 copy-start.3
  2.8 4.1 %collective-permute-start.4 = (s16[144,256]{1,0:T(8,128)(2,1)}, s16[144,256]{1,0:T(8,128)(2,1)S(1)}, u32[]{:S(2)}, u32[]{:S(2)}) collective-permute-start(s16[144,256]{1,0:T(8,128)(2,1)} %get-tuple-element.13), channel_id=1, source_target_pairs={{0,8},{2,10},{4,12},{6,14},{8,0},{10,2},{12,4},{14,6},{1,9},{3,11}... | collective-permute-start | bytes 221192 | tf_op jit(solution)/shard_map/ppermute | solution.py:375
  6.9 1.5 %collective-permute-start = (s16[144,256]{1,0:T(8,128)(2,1)}, s16[144,256]{1,0:T(8,128)(2,1)S(1)}, u32[]{:S(2)}, u32[]{:S(2)}) collective-permute-start(s16[144,256]{1,0:T(8,128)(2,1)} %get-tuple-element.13), channel_id=1, source_target_pairs={{0,2},{2,0},{4,6},{6,4},{8,10},{10,8},{12,14},{14,12},{1,3},{3,1},... | collective-permute-start | bytes 221192 | tf_op jit(solution)/shard_map/ppermute | solution.py:375
  8.4 1.6 %collective-permute-start.1 = (s16[144,256]{1,0:T(8,128)(2,1)}, s16[144,256]{1,0:T(8,128)(2,1)S(1)}, u32[]{:S(2)}, u32[]{:S(2)}) collective-permute-start(s16[144,256]{1,0:T(8,128)(2,1)} %get-tuple-element.13), channel_id=1, source_target_pairs={{0,4},{2,6},{4,0},{6,2},{8,12},{10,14},{12,8},{14,10},{1,5},{3,7},... | collective-permute-start | bytes 221192 | tf_op jit(solution)/shard_map/ppermute | solution.py:375
  9.9 0.2 collective-permute-start.2
  10.2 0.7 %collective-permute-start.3 = (s16[144,256]{1,0:T(8,128)(2,1)}, s16[144,256]{1,0:T(8,128)(2,1)S(1)}, u32[]{:S(2)}, u32[]{:S(2)}) collective-permute-start(s16[144,256]{1,0:T(8,128)(2,1)} %get-tuple-element.13), channel_id=1, source_target_pairs={{0,6},{2,4},{4,2},{6,0},{8,14},{10,12},{12,10},{14,8},{1,7},{3,5},... | collective-permute-start | bytes 221192 | tf_op jit(solution)/shard_map/ppermute | solution.py:375
  10.8 0.0 collective-permute-done.4.refs_5_
  10.8 1.9 %collective-permute-start.5 = (s16[144,256]{1,0:T(8,128)(2,1)S(1)}, s16[144,256]{1,0:T(8,128)(2,1)S(1)}, u32[]{:S(2)}, u32[]{:S(2)}) collective-permute-start(s16[144,256]{1,0:T(8,128)(2,1)S(1)} %collective-permute-done.4.refs_5_), channel_id=1, source_target_pairs={{0,2},{2,0},{4,6},{6,4},{8,10},{10,8},{12,14},{14,12},{1,3},{3,1},... | collective-permute-start | bytes 221192 | tf_op jit(solution)/shard_map/ppermute | solution.py:375
  12.7 0.0 collective-permute-done.refs_1_
  12.7 1.2 %collective-permute-start.6 = (s16[144,256]{1,0:T(8,128)(2,1)S(1)}, s16[144,256]{1,0:T(8,128)(2,1)S(1)}, u32[]{:S(2)}, u32[]{:S(2)}) collective-permute-start(s16[144,256]{1,0:T(8,128)(2,1)S(1)} %collective-permute-done.4.refs_5_), channel_id=1, source_target_pairs={{0,6},{2,4},{4,2},{6,0},{8,14},{10,12},{12,10},{14,8},{1,7},{3,5},... | collective-permute-start | bytes 221192 | tf_op jit(solution)/shard_map/ppermute | solution.py:375
  13.9 0.0 collective-permute-done.1.refs_2_
  13.9 2.5 %collective-permute-done.2.refs_3_ = s16[144,256]{1,0:T(8,128)(2,1)S(1)} collective-permute-done((s16[144,256]{1,0:T(8,128)(2,1)}, s16[144,256]{1,0:T(8,128)(2,1)S(1)}, u32[]{:S(2)}, u32[]{:S(2)}) %collective-permute-start.2) | collective-permute-done | bytes 73760 | tf_op jit(solution)/shard_map/ppermute | solution.py:375
  16.4 0.5 %collective-permute-done.3.refs_4_ = s16[144,256]{1,0:T(8,128)(2,1)S(1)} collective-permute-done((s16[144,256]{1,0:T(8,128)(2,1)}, s16[144,256]{1,0:T(8,128)(2,1)S(1)}, u32[]{:S(2)}, u32[]{:S(2)}) %collective-permute-start.3) | collective-permute-done | bytes 73760 | tf_op jit(solution)/shard_map/ppermute | solution.py:375
  16.9 1.2 %early.1 = (f32[288,256]{1,0:T(8,128)S(1)}, bf16[288,1536]{1,0:T(8,128)(2,1)S(1)}, s32[16,1536]{1,0:T(8,128)S(1)}) custom-call(s16[32768,256]{1,0:T(8,128)(2,1)} %get-tuple-element.12.refs_0_, s16[144,256]{1,0:T(8,128)(2,1)S(1)} %collective-permute-done.refs_1_, s16[144,256]{1,0:T(8,128)(2,1)S(1)} %collective-permute-done.1.refs_2_, ...), custom_call_target="tpu_custom_call" | custom-call | flops 1000000000 | bytes 1048576 | tf_op jit(solution)/shard_map/early/pallas_call | solution.py:387
  18.1 0.0 collective-permute-done.5.refs_5_
  18.1 0.0 collective-permute-done.6.refs_6_
  18.1 0.0 copy-done
  18.1 0.0 copy-done.1
  18.1 0.0 copy-done.2
  18.1 0.0 copy-done.3
  18.1 2.7 %correlate.1 = (f32[64,256]{1,0:T(8,128)S(1)}, f32[192,1024]{1,0:T(8,128)S(1)}) custom-call(f32[288,256]{1,0:T(8,128)S(1)} %get-tuple-element.14.refs_0_, bf16[288,1536]{1,0:T(8,128)(2,1)S(1)} %get-tuple-element.15.refs_1_, s32[16,1536]{1,0:T(8,128)S(1)} %get-tuple-element.16.refs_2_, s32[8]{0:T(128)S(1)} %copy-done.3, s32[1]{0:T(128)S(6)} %copy.10.slot_hbm.refs_4_, ...), custom_call_target="tpu_custom_call" | custom-call | tf_op jit(solution)/shard_map/correlate/pallas_call | solution.py:405
  20.8 0.1 collective-permute-start.7
  20.9 0.4 %keep.1 = f32[64,256]{1,0:T(8,128)S(1)} custom-call(f32[192,1024]{1,0:T(8,128)S(1)} %get-tuple-element.17.refs_0_, bf16[1024,256]{1,0:T(8,128)(2,1)S(1)} %copy-done.1), custom_call_target="tpu_custom_call" | custom-call | tf_op jit(solution)/shard_map/keep/pallas_call | solution.py:431
  21.3 0.8 %collective-permute-done.7 = f32[64,256]{1,0:T(8,128)S(1)} collective-permute-done((f32[64,256]{1,0:T(8,128)S(1)}, f32[64,256]{1,0:T(8,128)S(1)}, u32[]{:S(2)}, u32[]{:S(2)}) %collective-permute-start.7) | collective-permute-done | bytes 65568 | tf_op jit(solution)/shard_map/ppermute | solution.py:430
  22.1 0.6 %add.3 = f32[64,256]{1,0:T(8,128)} add(f32[64,256]{1,0:T(8,128)S(1)} %keep.1, f32[64,256]{1,0:T(8,128)S(1)} %collective-permute-done.7) | non-fusion elementwise | flops 16384 | bytes 196608 | tf_op jit(solution)/shard_map/add | solution.py:439
Async XLA Ops:
  2.7 15.4 %copy-start = (bf16[1040,1024]{1,0:T(8,128)(2,1)S(1)}, bf16[1040,1024]{1,0:T(8,128)(2,1)}, u32[]{:S(2)}) copy-start(bf16[1040,1024]{1,0:T(8,128)(2,1)} %constant.7.clone.refs_7_) | copy-start | bytes 6389764
  2.7 15.4 %copy-start.1 = (bf16[1024,256]{1,0:T(8,128)(2,1)S(1)}, bf16[1024,256]{1,0:T(8,128)(2,1)}, u32[]{:S(2)}) copy-start(bf16[1024,256]{1,0:T(8,128)(2,1)} %constant.6.clone.refs_9_.refs_1_) | copy-start | bytes 1572868
  2.7 15.4 %copy-start.2 = (bf16[512,512]{1,0:T(8,128)(2,1)S(1)}, bf16[512,512]{1,0:T(8,128)(2,1)}, u32[]{:S(2)}) copy-start(bf16[512,512]{1,0:T(8,128)(2,1)} %constant.8.clone.refs_8_) | copy-start | bytes 1572868
  2.8 15.4 %copy-start.3 = (s32[8]{0:T(128)S(1)}, s32[8]{0:T(128)}, u32[]{:S(2)}) copy-start(s32[8]{0:T(128)} %refs_3_.1) | copy-start | bytes 100
  2.8 8.0 %collective-permute-start.4 = (s16[144,256]{1,0:T(8,128)(2,1)}, s16[144,256]{1,0:T(8,128)(2,1)S(1)}, u32[]{:S(2)}, u32[]{:S(2)}) collective-permute-start(s16[144,256]{1,0:T(8,128)(2,1)} %get-tuple-element.13), channel_id=1, source_target_pairs={{0,8},{2,10},{4,12},{6,14},{8,0},{10,2},{12,4},{14,6},{1,9},{3,11}... | collective-permute-start | bytes 221192 | tf_op jit(solution)/shard_map/ppermute | solution.py:375
  6.9 5.9 %collective-permute-start = (s16[144,256]{1,0:T(8,128)(2,1)}, s16[144,256]{1,0:T(8,128)(2,1)S(1)}, u32[]{:S(2)}, u32[]{:S(2)}) collective-permute-start(s16[144,256]{1,0:T(8,128)(2,1)} %get-tuple-element.13), channel_id=1, source_target_pairs={{0,2},{2,0},{4,6},{6,4},{8,10},{10,8},{12,14},{14,12},{1,3},{3,1},... | collective-permute-start | bytes 221192 | tf_op jit(solution)/shard_map/ppermute | solution.py:375
  8.4 5.6 %collective-permute-start.1 = (s16[144,256]{1,0:T(8,128)(2,1)}, s16[144,256]{1,0:T(8,128)(2,1)S(1)}, u32[]{:S(2)}, u32[]{:S(2)}) collective-permute-start(s16[144,256]{1,0:T(8,128)(2,1)} %get-tuple-element.13), channel_id=1, source_target_pairs={{0,4},{2,6},{4,0},{6,2},{8,12},{10,14},{12,8},{14,10},{1,5},{3,7},... | collective-permute-start | bytes 221192 | tf_op jit(solution)/shard_map/ppermute | solution.py:375
  9.9 6.5 %collective-permute-start.2 = (s16[144,256]{1,0:T(8,128)(2,1)}, s16[144,256]{1,0:T(8,128)(2,1)S(1)}, u32[]{:S(2)}, u32[]{:S(2)}) collective-permute-start(s16[144,256]{1,0:T(8,128)(2,1)} %get-tuple-element.13), channel_id=1, source_target_pairs={{0,12},{2,14},{4,8},{6,10},{8,4},{10,6},{12,0},{14,2},{1,13},{3,15... | collective-permute-start | bytes 221192 | tf_op jit(solution)/shard_map/ppermute | solution.py:375
  10.2 6.7 %collective-permute-start.3 = (s16[144,256]{1,0:T(8,128)(2,1)}, s16[144,256]{1,0:T(8,128)(2,1)S(1)}, u32[]{:S(2)}, u32[]{:S(2)}) collective-permute-start(s16[144,256]{1,0:T(8,128)(2,1)} %get-tuple-element.13), channel_id=1, source_target_pairs={{0,6},{2,4},{4,2},{6,0},{8,14},{10,12},{12,10},{14,8},{1,7},{3,5},... | collective-permute-start | bytes 221192 | tf_op jit(solution)/shard_map/ppermute | solution.py:375
  10.8 7.2 %collective-permute-start.5 = (s16[144,256]{1,0:T(8,128)(2,1)S(1)}, s16[144,256]{1,0:T(8,128)(2,1)S(1)}, u32[]{:S(2)}, u32[]{:S(2)}) collective-permute-start(s16[144,256]{1,0:T(8,128)(2,1)S(1)} %collective-permute-done.4.refs_5_), channel_id=1, source_target_pairs={{0,2},{2,0},{4,6},{6,4},{8,10},{10,8},{12,14},{14,12},{1,3},{3,1},... | collective-permute-start | bytes 221192 | tf_op jit(solution)/shard_map/ppermute | solution.py:375
  12.7 5.3 %collective-permute-start.6 = (s16[144,256]{1,0:T(8,128)(2,1)S(1)}, s16[144,256]{1,0:T(8,128)(2,1)S(1)}, u32[]{:S(2)}, u32[]{:S(2)}) collective-permute-start(s16[144,256]{1,0:T(8,128)(2,1)S(1)} %collective-permute-done.4.refs_5_), channel_id=1, source_target_pairs={{0,6},{2,4},{4,2},{6,0},{8,14},{10,12},{12,10},{14,8},{1,7},{3,5},... | collective-permute-start | bytes 221192 | tf_op jit(solution)/shard_map/ppermute | solution.py:375
  20.8 1.3 %collective-permute-start.7 = (f32[64,256]{1,0:T(8,128)S(1)}, f32[64,256]{1,0:T(8,128)S(1)}, u32[]{:S(2)}, u32[]{:S(2)}) collective-permute-start(f32[64,256]{1,0:T(8,128)S(1)} %get-tuple-element.18), channel_id=1, source_target_pairs={{0,1},{1,0},{2,3},{3,2},{4,5},{5,4},{6,7},{7,6},{8,9},{9,8},{10,11... | collective-permute-start | bytes 196616 | tf_op jit(solution)/shard_map/ppermute | solution.py:430

commit v6 on v5

--- a/solution.py
+++ b/solution.py
@@ -85,7 +85,7 @@
 
 
 def filter_kernel(
-    records_hbm, channel_hbm, piece_hbm, taps_hbm, slot_hbm, unit_hbm, local_hbm, *scratch
+    records_hbm, channel_hbm, piece_hbm, taps_hbm, slot_hbm, unit_hbm, *scratch
 ):
     records_ref, channel_ref, piece_ref, taps_ref, slot_ref, unit_ref, arrived = scratch
     f32 = jnp.float32
@@ -139,11 +139,8 @@
     side = jnp.where(row == SLOT_ROW, slot_ref[0], side)
     unit_ref[OUTS:] = side.astype(jnp.int16)
     out = pltpu.make_async_copy(unit_ref, unit_hbm, arrived.at[0])
-    local = pltpu.make_async_copy(unit_ref, local_hbm.at[pl.ds(0, OUTS + AUX)], arrived.at[1])
     out.start()
-    local.start()
     out.wait()
-    local.wait()
 
 
 def halves(code):
@@ -214,10 +211,10 @@
 
 
 def early_kernel(early_total, *refs):
-    local_hbm = refs[0]
+    unit_hbm = refs[0]
     units_ref = refs[1:early_total]
     own_ref, data_ref, side_ref, pick_ref, unit_ref, arrived = refs[early_total:]
-    copy = pltpu.make_async_copy(local_hbm.at[pl.ds(0, OUTS + AUX)], unit_ref, arrived)
+    copy = pltpu.make_async_copy(unit_hbm, unit_ref, arrived)
     copy.start()
     count = unit_ref.shape[1]
     wanted = wanted_own(lax.axis_index("chan"), count)
@@ -322,15 +319,11 @@
     imag = spectra[:, NF:]
     energy = real * real + imag * imag
     high = energy.astype(jnp.bfloat16)
-    rest = energy - high.astype(f32)
-    middle = rest.astype(jnp.bfloat16)
-    low = (rest - middle.astype(f32)).astype(jnp.bfloat16)
-    band = band_ref[...]
-    smooth = (
-        jnp.dot(high, band, preferred_element_type=f32)
-        + jnp.dot(middle, band, preferred_element_type=f32)
-        + jnp.dot(low, band, preferred_element_type=f32)
-    ) * inverse
+    low = (energy - high.astype(f32)).astype(jnp.bfloat16)
+    sums = jnp.dot(
+        jnp.concatenate([high, low], axis=0), band_ref[...], preferred_element_type=f32
+    )
+    smooth = (sums[: energy.shape[0]] + sums[energy.shape[0] :]) * inverse
     scale = lax.rsqrt(smooth + EPSILON)
     white_ref[:, :NF] = (real * scale).astype(jnp.bfloat16).astype(f32)
     white_ref[:, NF:] = (imag * scale).astype(jnp.bfloat16).astype(f32)
@@ -349,14 +342,13 @@
     hbm = pl.BlockSpec(memory_space=pl.ANY)
     count = records.shape[0]
     unit_shape = (OUTS + AUX, count)
-    unit, local = pl.pallas_call(
+    unit = pl.pallas_call(
         filter_kernel,
         out_shape=(
-            jax.ShapeDtypeStruct(unit_shape, jnp.int16),
-            jax.ShapeDtypeStruct((LOCAL_ROWS, count), jnp.int16),
+            jax.ShapeDtypeStruct(unit_shape, jnp.int16)
         ),
         in_specs=[hbm] * 5,
-        out_specs=(hbm, hbm),
+        out_specs=hbm,
         scratch_shapes=[
             pltpu.VMEM(records.shape, records.dtype),
             pltpu.VMEM(record_channel.shape, jnp.int32),
@@ -401,7 +393,7 @@
         compiler_params=pltpu.CompilerParams(vmem_limit_bytes=EARLY_VMEM),
         cost_estimate=pl.CostEstimate(flops=EARLY_FLOPS, bytes_accessed=1 << 20, transcendentals=0),
         name="early",
-    )(local, *[units[step] for step in EARLY[1:]])
+    )(unit, *[units[step] for step in EARLY[1:]])
     send, white = pl.pallas_call(
         lambda *refs: correlate_kernel(block_total, span_total, *refs),
         out_shape=(half_shape, jax.ShapeDtypeStruct((WIN_DEV * rows, WL), jnp.float32)),

time: 22.9 us -> 22.7 us (level)
  waiting for transfers between devices: 3.78 us -> 2.51 us
  local copies, waits for them, and re-layouts: 0.03 us -> 0.91 us
  starting transfers between devices: 11.2 us -> 11.9 us
  Pallas kernels: 6.3 us -> 5.77 us
    ppermute x7, waiting for transfers between devices: 2.97 us -> 1.73 us  [swap(): lax.ppermute(value, 'chan', [(i, i ^ step) for i in range(block_total)])]
    unnamed x8 -> x10, local copies, waits for them, and re-layouts: 0.03 us -> 0.91 us
    ppermute x7, starting transfers between devices: 11.2 us -> 11.8 us  [swap(): lax.ppermute(value, 'chan', [(i, i ^ step) for i in range(block_total)])]
    pallas_call x1, Pallas kernels: 1.15 us -> 0.76 us  [gathered_body(): pl.pallas_call(lambda *refs: early_kernel(len(EARLY), *refs), out_shape=(...]
  transfers between devices with their start and end apart: 8 -> 8, of which waited for: 3 -> 4; matrix products, arithmetic and copies ran while one was open for 0% -> 0% of each run, Pallas kernels for 7% -> 5%
where the time goes in v6:
time: 22.7 us; the launch traced here: 22.5 us
  starting transfers between devices  11.9 us (52%)
  Pallas kernels  5.77 us (25%)
  waiting for transfers between devices  2.51 us (11%)
  local copies, waits for them, and re-layouts  0.91 us (4%)
  between operations  0.74 us (3%)
  other arithmetic  0.64 us (3%)
    ppermute x7, starting transfers between devices, swap(): lax.ppermute(value, 'chan', [(i, i ^ step) for i in range(block_total)])  11.8 us
    pallas_call x1, Pallas kernels, gathered_body(): pl.pallas_call(lambda *refs: correlate_kernel(block_total, span_total, *r...  2.54 us
    pallas_call x1, Pallas kernels, gathered_body(): pl.pallas_call(filter_kernel, out_shape=jax.ShapeDtypeStruct(unit_shape,...  2.02 us
    ppermute x7, waiting for transfers between devices, swap(): lax.ppermute(value, 'chan', [(i, i ^ step) for i in range(block_total)])  1.73 us
    unnamed x10, local copies, waits for them, and re-layouts  0.91 us
    ppermute x1, waiting for transfers between devices, gathered_body(): other = lax.ppermute(send, 'win', [(i, i ^ 1) for i in range(span_total)])  0.78 us
    pallas_call x1, Pallas kernels, gathered_body(): pl.pallas_call(lambda *refs: early_kernel(len(EARLY), *refs), out_shape=(...  0.76 us
    add x1, other arithmetic, gathered_body(): return (keep + other).reshape(block_total // span_total, CH_DEV, LAGS)  0.64 us
  transfers between devices with their start and end apart: 8, of which 4 were waited for; matrix products, arithmetic and copies ran while one was open for 0% of the time, Pallas kernels for 5%

profile of v6, /device:TPU:0, one launch (start us, length us, event | category | flops | bytes accessed | tf_op | source)
XLA Modules:
  0.0 22.5 jit_solution(8695927266034836692)
XLA Ops:
  0.7 2.0 %filter.1.refs_0_ = s16[144,256]{1,0:T(8,128)(2,1)} custom-call(bf16[256,512]{1,0:T(8,128)(2,1)} %records_hbm.1, s32[256]{0:T(256)} %channel_hbm.1, s32[256]{0:T(256)} %piece_hbm.1, bf16[32]{0:T(256)(128)(2,1)} %taps_hbm.1, s32[1]{0:T(128)S(6)} %copy.10.slot_hbm.refs_4_), custom_call_target="tpu_custom_call" | custom-call | flops 10000000000 | bytes 1048576 | tf_op jit(solution)/shard_map/filter/pallas_call | solution.py:345
  2.7 0.0 copy-start
  2.7 0.0 copy-start.1
  2.7 0.0 copy-start.2
  2.7 0.0 copy-start.3
  2.7 4.1 %collective-permute-start.4 = (s16[144,256]{1,0:T(8,128)(2,1)}, s16[144,256]{1,0:T(8,128)(2,1)S(1)}, u32[]{:S(2)}, u32[]{:S(2)}) collective-permute-start(s16[144,256]{1,0:T(8,128)(2,1)} %filter.1.refs_0_), channel_id=1, source_target_pairs={{0,8},{2,10},{4,12},{6,14},{8,0},{10,2},{12,4},{14,6},{1,9},{3,11}... | collective-permute-start | bytes 221192 | tf_op jit(solution)/shard_map/ppermute | solution.py:367
  6.8 2.5 %collective-permute-start.3 = (s16[144,256]{1,0:T(8,128)(2,1)}, s16[144,256]{1,0:T(8,128)(2,1)S(1)}, u32[]{:S(2)}, u32[]{:S(2)}) collective-permute-start(s16[144,256]{1,0:T(8,128)(2,1)} %filter.1.refs_0_), channel_id=1, source_target_pairs={{0,6},{2,4},{4,2},{6,0},{8,14},{10,12},{12,10},{14,8},{1,7},{3,5},... | collective-permute-start | bytes 221192 | tf_op jit(solution)/shard_map/ppermute | solution.py:367
  9.3 0.2 collective-permute-start.2
  9.6 0.7 %collective-permute-start.1 = (s16[144,256]{1,0:T(8,128)(2,1)}, s16[144,256]{1,0:T(8,128)(2,1)S(1)}, u32[]{:S(2)}, u32[]{:S(2)}) collective-permute-start(s16[144,256]{1,0:T(8,128)(2,1)} %filter.1.refs_0_), channel_id=1, source_target_pairs={{0,4},{2,6},{4,0},{6,2},{8,12},{10,14},{12,8},{14,10},{1,5},{3,7},... | collective-permute-start | bytes 221192 | tf_op jit(solution)/shard_map/ppermute | solution.py:367
  10.2 0.5 %collective-permute-start = (s16[144,256]{1,0:T(8,128)(2,1)}, s16[144,256]{1,0:T(8,128)(2,1)S(1)}, u32[]{:S(2)}, u32[]{:S(2)}) collective-permute-start(s16[144,256]{1,0:T(8,128)(2,1)} %filter.1.refs_0_), channel_id=1, source_target_pairs={{0,2},{2,0},{4,6},{6,4},{8,10},{10,8},{12,14},{14,12},{1,3},{3,1},... | collective-permute-start | bytes 221192 | tf_op jit(solution)/shard_map/ppermute | solution.py:367
  10.8 0.0 collective-permute-done.4.refs_5_
  10.8 2.5 %collective-permute-start.6 = (s16[144,256]{1,0:T(8,128)(2,1)S(1)}, s16[144,256]{1,0:T(8,128)(2,1)S(1)}, u32[]{:S(2)}, u32[]{:S(2)}) collective-permute-start(s16[144,256]{1,0:T(8,128)(2,1)S(1)} %collective-permute-done.4.refs_5_), channel_id=1, source_target_pairs={{0,6},{2,4},{4,2},{6,0},{8,14},{10,12},{12,10},{14,8},{1,7},{3,5},... | collective-permute-start | bytes 221192 | tf_op jit(solution)/shard_map/ppermute | solution.py:367
  13.3 0.0 collective-permute-done.3.refs_4_
  13.3 1.2 %collective-permute-start.5 = (s16[144,256]{1,0:T(8,128)(2,1)S(1)}, s16[144,256]{1,0:T(8,128)(2,1)S(1)}, u32[]{:S(2)}, u32[]{:S(2)}) collective-permute-start(s16[144,256]{1,0:T(8,128)(2,1)S(1)} %collective-permute-done.4.refs_5_), channel_id=1, source_target_pairs={{0,2},{2,0},{4,6},{6,4},{8,10},{10,8},{12,14},{14,12},{1,3},{3,1},... | collective-permute-start | bytes 221192 | tf_op jit(solution)/shard_map/ppermute | solution.py:367
  14.6 1.2 %collective-permute-done.2.refs_3_ = s16[144,256]{1,0:T(8,128)(2,1)S(1)} collective-permute-done((s16[144,256]{1,0:T(8,128)(2,1)}, s16[144,256]{1,0:T(8,128)(2,1)S(1)}, u32[]{:S(2)}, u32[]{:S(2)}) %collective-permute-start.2) | collective-permute-done | bytes 73760 | tf_op jit(solution)/shard_map/ppermute | solution.py:367
  15.8 0.3 %collective-permute-done.1.refs_2_ = s16[144,256]{1,0:T(8,128)(2,1)S(1)} collective-permute-done((s16[144,256]{1,0:T(8,128)(2,1)}, s16[144,256]{1,0:T(8,128)(2,1)S(1)}, u32[]{:S(2)}, u32[]{:S(2)}) %collective-permute-start.1) | collective-permute-done | bytes 73760 | tf_op jit(solution)/shard_map/ppermute | solution.py:367
  16.1 0.0 collective-permute-done.refs_1_
  16.2 0.0 copy-start.4
  16.2 0.9 %copy-done.4 = s16[144,256]{1,0:T(8,128)(2,1)S(1)} copy-done((s16[144,256]{1,0:T(8,128)(2,1)S(1)}, s16[144,256]{1,0:T(8,128)(2,1)}, u32[]{:S(2)}) %copy-start.4) | copy-done | bytes 73752
  17.0 0.8 %early.1 = (f32[288,256]{1,0:T(8,128)S(1)}, bf16[288,1536]{1,0:T(8,128)(2,1)S(1)}, s32[16,1536]{1,0:T(8,128)S(1)}) custom-call(s16[144,256]{1,0:T(8,128)(2,1)S(1)} %copy-done.4, s16[144,256]{1,0:T(8,128)(2,1)S(1)} %collective-permute-done.refs_1_, s16[144,256]{1,0:T(8,128)(2,1)S(1)} %collective-permute-done.1.refs_2_, ...), custom_call_target="tpu_custom_call" | custom-call | flops 1000000000 | bytes 1048576 | tf_op jit(solution)/shard_map/early/pallas_call | solution.py:379
  17.8 0.0 collective-permute-done.6.refs_6_
  17.8 0.1 collective-permute-done.5.refs_5_
  18.0 0.0 copy-done
  18.0 0.0 copy-done.1
  18.0 0.0 copy-done.2
  18.0 0.0 copy-done.3
  18.0 2.5 %correlate.1 = (f32[64,256]{1,0:T(8,128)S(1)}, f32[192,1024]{1,0:T(8,128)S(1)}) custom-call(f32[288,256]{1,0:T(8,128)S(1)} %get-tuple-element.10.refs_0_, bf16[288,1536]{1,0:T(8,128)(2,1)S(1)} %get-tuple-element.11.refs_1_, s32[16,1536]{1,0:T(8,128)S(1)} %get-tuple-element.12.refs_2_, s32[8]{0:T(128)S(1)} %copy-done.3, s32[1]{0:T(128)S(6)} %copy.10.slot_hbm.refs_4_, ...), custom_call_target="tpu_custom_call" | custom-call | tf_op jit(solution)/shard_map/correlate/pallas_call | solution.py:397
  20.5 0.1 collective-permute-start.7
  20.6 0.5 %keep.1 = f32[64,256]{1,0:T(8,128)S(1)} custom-call(f32[192,1024]{1,0:T(8,128)S(1)} %get-tuple-element.13.refs_0_, bf16[1024,256]{1,0:T(8,128)(2,1)S(1)} %copy-done.1), custom_call_target="tpu_custom_call" | custom-call | tf_op jit(solution)/shard_map/keep/pallas_call | solution.py:423
  21.1 0.8 %collective-permute-done.7 = f32[64,256]{1,0:T(8,128)S(1)} collective-permute-done((f32[64,256]{1,0:T(8,128)S(1)}, f32[64,256]{1,0:T(8,128)S(1)}, u32[]{:S(2)}, u32[]{:S(2)}) %collective-permute-start.7) | collective-permute-done | bytes 65568 | tf_op jit(solution)/shard_map/ppermute | solution.py:422
  21.8 0.6 %add.3 = f32[64,256]{1,0:T(8,128)} add(f32[64,256]{1,0:T(8,128)S(1)} %keep.1, f32[64,256]{1,0:T(8,128)S(1)} %collective-permute-done.7) | non-fusion elementwise | flops 16384 | bytes 196608 | tf_op jit(solution)/shard_map/add | solution.py:431
Async XLA Ops:
  2.7 15.3 %copy-start = (bf16[1040,1024]{1,0:T(8,128)(2,1)S(1)}, bf16[1040,1024]{1,0:T(8,128)(2,1)}, u32[]{:S(2)}) copy-start(bf16[1040,1024]{1,0:T(8,128)(2,1)} %constant.7.clone.refs_7_) | copy-start | bytes 6389764
  2.7 15.3 %copy-start.1 = (bf16[1024,256]{1,0:T(8,128)(2,1)S(1)}, bf16[1024,256]{1,0:T(8,128)(2,1)}, u32[]{:S(2)}) copy-start(bf16[1024,256]{1,0:T(8,128)(2,1)} %constant.6.clone.refs_9_.refs_1_) | copy-start | bytes 1572868
  2.7 15.3 %copy-start.2 = (bf16[512,512]{1,0:T(8,128)(2,1)S(1)}, bf16[512,512]{1,0:T(8,128)(2,1)}, u32[]{:S(2)}) copy-start(bf16[512,512]{1,0:T(8,128)(2,1)} %constant.8.clone.refs_8_) | copy-start | bytes 1572868
  2.7 15.3 %copy-start.3 = (s32[8]{0:T(128)S(1)}, s32[8]{0:T(128)}, u32[]{:S(2)}) copy-start(s32[8]{0:T(128)} %refs_3_.1) | copy-start | bytes 100
  2.7 8.0 %collective-permute-start.4 = (s16[144,256]{1,0:T(8,128)(2,1)}, s16[144,256]{1,0:T(8,128)(2,1)S(1)}, u32[]{:S(2)}, u32[]{:S(2)}) collective-permute-start(s16[144,256]{1,0:T(8,128)(2,1)} %filter.1.refs_0_), channel_id=1, source_target_pairs={{0,8},{2,10},{4,12},{6,14},{8,0},{10,2},{12,4},{14,6},{1,9},{3,11}... | collective-permute-start | bytes 221192 | tf_op jit(solution)/shard_map/ppermute | solution.py:367
  6.8 6.5 %collective-permute-start.3 = (s16[144,256]{1,0:T(8,128)(2,1)}, s16[144,256]{1,0:T(8,128)(2,1)S(1)}, u32[]{:S(2)}, u32[]{:S(2)}) collective-permute-start(s16[144,256]{1,0:T(8,128)(2,1)} %filter.1.refs_0_), channel_id=1, source_target_pairs={{0,6},{2,4},{4,2},{6,0},{8,14},{10,12},{12,10},{14,8},{1,7},{3,5},... | collective-permute-start | bytes 221192 | tf_op jit(solution)/shard_map/ppermute | solution.py:367
  9.3 6.5 %collective-permute-start.2 = (s16[144,256]{1,0:T(8,128)(2,1)}, s16[144,256]{1,0:T(8,128)(2,1)S(1)}, u32[]{:S(2)}, u32[]{:S(2)}) collective-permute-start(s16[144,256]{1,0:T(8,128)(2,1)} %filter.1.refs_0_), channel_id=1, source_target_pairs={{0,12},{2,14},{4,8},{6,10},{8,4},{10,6},{12,0},{14,2},{1,13},{3,15... | collective-permute-start | bytes 221192 | tf_op jit(solution)/shard_map/ppermute | solution.py:367
  9.6 6.6 %collective-permute-start.1 = (s16[144,256]{1,0:T(8,128)(2,1)}, s16[144,256]{1,0:T(8,128)(2,1)S(1)}, u32[]{:S(2)}, u32[]{:S(2)}) collective-permute-start(s16[144,256]{1,0:T(8,128)(2,1)} %filter.1.refs_0_), channel_id=1, source_target_pairs={{0,4},{2,6},{4,0},{6,2},{8,12},{10,14},{12,8},{14,10},{1,5},{3,7},... | collective-permute-start | bytes 221192 | tf_op jit(solution)/shard_map/ppermute | solution.py:367
  10.2 5.9 %collective-permute-start = (s16[144,256]{1,0:T(8,128)(2,1)}, s16[144,256]{1,0:T(8,128)(2,1)S(1)}, u32[]{:S(2)}, u32[]{:S(2)}) collective-permute-start(s16[144,256]{1,0:T(8,128)(2,1)} %filter.1.refs_0_), channel_id=1, source_target_pairs={{0,2},{2,0},{4,6},{6,4},{8,10},{10,8},{12,14},{14,12},{1,3},{3,1},... | collective-permute-start | bytes 221192 | tf_op jit(solution)/shard_map/ppermute | solution.py:367
  10.8 7.0 %collective-permute-start.6 = (s16[144,256]{1,0:T(8,128)(2,1)S(1)}, s16[144,256]{1,0:T(8,128)(2,1)S(1)}, u32[]{:S(2)}, u32[]{:S(2)}) collective-permute-start(s16[144,256]{1,0:T(8,128)(2,1)S(1)} %collective-permute-done.4.refs_5_), channel_id=1, source_target_pairs={{0,6},{2,4},{4,2},{6,0},{8,14},{10,12},{12,10},{14,8},{1,7},{3,5},... | collective-permute-start | bytes 221192 | tf_op jit(solution)/shard_map/ppermute | solution.py:367
  13.3 4.6 %collective-permute-start.5 = (s16[144,256]{1,0:T(8,128)(2,1)S(1)}, s16[144,256]{1,0:T(8,128)(2,1)S(1)}, u32[]{:S(2)}, u32[]{:S(2)}) collective-permute-start(s16[144,256]{1,0:T(8,128)(2,1)S(1)} %collective-permute-done.4.refs_5_), channel_id=1, source_target_pairs={{0,2},{2,0},{4,6},{6,4},{8,10},{10,8},{12,14},{14,12},{1,3},{3,1},... | collective-permute-start | bytes 221192 | tf_op jit(solution)/shard_map/ppermute | solution.py:367
  16.2 0.9 %copy-start.4 = (s16[144,256]{1,0:T(8,128)(2,1)S(1)}, s16[144,256]{1,0:T(8,128)(2,1)}, u32[]{:S(2)}) copy-start(s16[144,256]{1,0:T(8,128)(2,1)} %filter.1.refs_0_) | copy-start | bytes 221188
  20.5 1.3 %collective-permute-start.7 = (f32[64,256]{1,0:T(8,128)S(1)}, f32[64,256]{1,0:T(8,128)S(1)}, u32[]{:S(2)}, u32[]{:S(2)}) collective-permute-start(f32[64,256]{1,0:T(8,128)S(1)} %get-tuple-element.14), channel_id=1, source_target_pairs={{0,1},{1,0},{2,3},{3,2},{4,5},{5,4},{6,7},{7,6},{8,9},{9,8},{10,11... | collective-permute-start | bytes 196616 | tf_op jit(solution)/shard_map/ppermute | solution.py:422

commit v7 on v6

--- a/solution.py
+++ b/solution.py
@@ -38,8 +38,8 @@
 CORRELATE_VMEM = 40 << 20
 LOCAL_ROWS = 32768
 LAST_HOP = {1: 1, 2: 2, 3: 3, 4: 4, 6: 6, 5: 1, 7: 3}
-EARLY = (0, 1, 2, 6, 3, 4)
-LATE = (5, 7)
+EARLY = (0, 2, 1, 4)
+LATE = (6, 5, 3, 7)
 CODE = 23000.0
 
 

time: 22.7 us -> 22.5 us (level)
  starting transfers between devices: 11.9 us -> 10.8 us
  waiting for transfers between devices: 2.51 us -> 3.46 us
    ppermute x7, starting transfers between devices: 11.8 us -> 10.7 us  [swap(): lax.ppermute(value, 'chan', [(i, i ^ step) for i in range(block_total)])]
    ppermute x7, waiting for transfers between devices: 1.73 us -> 2.68 us  [swap(): lax.ppermute(value, 'chan', [(i, i ^ step) for i in range(block_total)])]
where the time goes in v7:
time: 22.5 us; the launch traced here: 22.3 us
  starting transfers between devices  10.8 us (48%)
  Pallas kernels  5.77 us (26%)
  waiting for transfers between devices  3.46 us (15%)
  local copies, waits for them, and re-layouts  0.91 us (4%)
  between operations  0.74 us (3%)
  other arithmetic  0.64 us (3%)
    ppermute x7, starting transfers between devices, swap(): lax.ppermute(value, 'chan', [(i, i ^ step) for i in range(block_total)])  10.7 us
    ppermute x7, waiting for transfers between devices, swap(): lax.ppermute(value, 'chan', [(i, i ^ step) for i in range(block_total)])  2.68 us
    pallas_call x1, Pallas kernels, gathered_body(): pl.pallas_call(lambda *refs: correlate_kernel(block_total, span_total, *r...  2.61 us
    pallas_call x1, Pallas kernels, gathered_body(): pl.pallas_call(filter_kernel, out_shape=jax.ShapeDtypeStruct(unit_shape,...  2.02 us
    unnamed x10, local copies, waits for them, and re-layouts  0.91 us
    ppermute x1, waiting for transfers between devices, gathered_body(): other = lax.ppermute(send, 'win', [(i, i ^ 1) for i in range(span_total)])  0.78 us
    pallas_call x1, Pallas kernels, gathered_body(): pl.pallas_call(lambda *refs: early_kernel(len(EARLY), *refs), out_shape=(...  0.68 us
    add x1, other arithmetic, gathered_body(): return (keep + other).reshape(block_total // span_total, CH_DEV, LAGS)  0.64 us
  transfers between devices with their start and end apart: 8, of which 4 were waited for; matrix products, arithmetic and copies ran while one was open for 0% of the time, Pallas kernels for 5%

profile of v7, /device:TPU:0, one launch (start us, length us, event | category | flops | bytes accessed | tf_op | source)
XLA Modules:
  0.0 22.3 jit_solution(14454667050139509240)
XLA Ops:
  0.7 2.0 %filter.1.refs_0_ = s16[144,256]{1,0:T(8,128)(2,1)} custom-call(bf16[256,512]{1,0:T(8,128)(2,1)} %records_hbm.1, s32[256]{0:T(256)} %channel_hbm.1, s32[256]{0:T(256)} %piece_hbm.1, bf16[32]{0:T(256)(128)(2,1)} %taps_hbm.1, s32[1]{0:T(128)S(6)} %copy.10.slot_hbm.refs_4_), custom_call_target="tpu_custom_call" | custom-call | flops 10000000000 | bytes 1048576 | tf_op jit(solution)/shard_map/filter/pallas_call | solution.py:345
  2.7 0.0 copy-start
  2.7 0.0 copy-start.1
  2.7 0.0 copy-start.2
  2.7 0.0 copy-start.3
  2.7 4.1 %collective-permute-start.2 = (s16[144,256]{1,0:T(8,128)(2,1)}, s16[144,256]{1,0:T(8,128)(2,1)S(1)}, u32[]{:S(2)}, u32[]{:S(2)}) collective-permute-start(s16[144,256]{1,0:T(8,128)(2,1)} %filter.1.refs_0_), channel_id=1, source_target_pairs={{0,8},{2,10},{4,12},{6,14},{8,0},{10,2},{12,4},{14,6},{1,9},{3,11}... | collective-permute-start | bytes 221192 | tf_op jit(solution)/shard_map/ppermute | solution.py:367
  6.8 1.5 %collective-permute-start.1 = (s16[144,256]{1,0:T(8,128)(2,1)}, s16[144,256]{1,0:T(8,128)(2,1)S(1)}, u32[]{:S(2)}, u32[]{:S(2)}) collective-permute-start(s16[144,256]{1,0:T(8,128)(2,1)} %filter.1.refs_0_), channel_id=1, source_target_pairs={{0,2},{2,0},{4,6},{6,4},{8,10},{10,8},{12,14},{14,12},{1,3},{3,1},... | collective-permute-start | bytes 221192 | tf_op jit(solution)/shard_map/ppermute | solution.py:367
  8.3 1.6 %collective-permute-start = (s16[144,256]{1,0:T(8,128)(2,1)}, s16[144,256]{1,0:T(8,128)(2,1)S(1)}, u32[]{:S(2)}, u32[]{:S(2)}) collective-permute-start(s16[144,256]{1,0:T(8,128)(2,1)} %filter.1.refs_0_), channel_id=1, source_target_pairs={{0,4},{2,6},{4,0},{6,2},{8,12},{10,14},{12,8},{14,10},{1,5},{3,7},... | collective-permute-start | bytes 221192 | tf_op jit(solution)/shard_map/ppermute | solution.py:367
  9.9 0.4 %collective-permute-start.5 = (s16[144,256]{1,0:T(8,128)(2,1)}, s16[144,256]{1,0:T(8,128)(2,1)S(1)}, u32[]{:S(2)}, u32[]{:S(2)}) collective-permute-start(s16[144,256]{1,0:T(8,128)(2,1)} %filter.1.refs_0_), channel_id=1, source_target_pairs={{0,6},{2,4},{4,2},{6,0},{8,14},{10,12},{12,10},{14,8},{1,7},{3,5},... | collective-permute-start | bytes 221192 | tf_op jit(solution)/shard_map/ppermute | solution.py:367
  10.3 1.4 %collective-permute-start.3 = (s16[144,256]{1,0:T(8,128)(2,1)}, s16[144,256]{1,0:T(8,128)(2,1)S(1)}, u32[]{:S(2)}, u32[]{:S(2)}) collective-permute-start(s16[144,256]{1,0:T(8,128)(2,1)} %filter.1.refs_0_), channel_id=1, source_target_pairs={{0,12},{2,14},{4,8},{6,10},{8,4},{10,6},{12,0},{14,2},{1,13},{3,15... | collective-permute-start | bytes 221192 | tf_op jit(solution)/shard_map/ppermute | solution.py:367
  11.7 0.0 collective-permute-done.2.refs_3_
  11.7 1.3 %collective-permute-start.6 = (s16[144,256]{1,0:T(8,128)(2,1)S(1)}, s16[144,256]{1,0:T(8,128)(2,1)S(1)}, u32[]{:S(2)}, u32[]{:S(2)}) collective-permute-start(s16[144,256]{1,0:T(8,128)(2,1)S(1)} %collective-permute-done.2.refs_3_), channel_id=1, source_target_pairs={{0,6},{2,4},{4,2},{6,0},{8,14},{10,12},{12,10},{14,8},{1,7},{3,5},... | collective-permute-start | bytes 221192 | tf_op jit(solution)/shard_map/ppermute | solution.py:367
  12.9 0.0 collective-permute-done.1.refs_2_
  12.9 0.5 %collective-permute-start.4 = (s16[144,256]{1,0:T(8,128)(2,1)S(1)}, s16[144,256]{1,0:T(8,128)(2,1)S(1)}, u32[]{:S(2)}, u32[]{:S(2)}) collective-permute-start(s16[144,256]{1,0:T(8,128)(2,1)S(1)} %collective-permute-done.2.refs_3_), channel_id=1, source_target_pairs={{0,2},{2,0},{4,6},{6,4},{8,10},{10,8},{12,14},{14,12},{1,3},{3,1},... | collective-permute-start | bytes 221192 | tf_op jit(solution)/shard_map/ppermute | solution.py:367
  13.5 0.0 collective-permute-done.refs_1_
  13.5 0.0 copy-start.4
  13.5 0.9 %copy-done.4 = s16[144,256]{1,0:T(8,128)(2,1)S(1)} copy-done((s16[144,256]{1,0:T(8,128)(2,1)S(1)}, s16[144,256]{1,0:T(8,128)(2,1)}, u32[]{:S(2)}) %copy-start.4) | copy-done | bytes 73752
  14.4 0.7 %early.1 = (f32[288,256]{1,0:T(8,128)S(1)}, bf16[288,1024]{1,0:T(8,128)(2,1)S(1)}, s32[16,1024]{1,0:T(8,128)S(1)}) custom-call(s16[144,256]{1,0:T(8,128)(2,1)S(1)} %copy-done.4, s16[144,256]{1,0:T(8,128)(2,1)S(1)} %collective-permute-done.refs_1_, s16[144,256]{1,0:T(8,128)(2,1)S(1)} %collective-permute-done.1.refs_2_, ...), custom_call_target="tpu_custom_call" | custom-call | flops 1000000000 | bytes 1048576 | tf_op jit(solution)/shard_map/early/pallas_call | solution.py:379
  15.1 1.1 %collective-permute-done.5.refs_7_ = s16[144,256]{1,0:T(8,128)(2,1)S(1)} collective-permute-done((s16[144,256]{1,0:T(8,128)(2,1)}, s16[144,256]{1,0:T(8,128)(2,1)S(1)}, u32[]{:S(2)}, u32[]{:S(2)}) %collective-permute-start.5) | collective-permute-done | bytes 73760 | tf_op jit(solution)/shard_map/ppermute | solution.py:367
  16.1 0.6 %collective-permute-done.3.refs_5_ = s16[144,256]{1,0:T(8,128)(2,1)S(1)} collective-permute-done((s16[144,256]{1,0:T(8,128)(2,1)}, s16[144,256]{1,0:T(8,128)(2,1)S(1)}, u32[]{:S(2)}, u32[]{:S(2)}) %collective-permute-start.3) | collective-permute-done | bytes 73760 | tf_op jit(solution)/shard_map/ppermute | solution.py:367
  16.8 0.9 %collective-permute-done.6.refs_8_ = s16[144,256]{1,0:T(8,128)(2,1)S(1)} collective-permute-done((s16[144,256]{1,0:T(8,128)(2,1)S(1)}, s16[144,256]{1,0:T(8,128)(2,1)S(1)}, u32[]{:S(2)}, u32[]{:S(2)}) %collective-permute-start.6) | collective-permute-done | bytes 73760 | tf_op jit(solution)/shard_map/ppermute | solution.py:367
  17.7 0.0 collective-permute-done.4.refs_6_
  17.7 0.0 copy-done
  17.7 0.0 copy-done.1
  17.7 0.0 copy-done.2
  17.7 0.0 copy-done.3
  17.8 2.6 %correlate.1 = (f32[64,256]{1,0:T(8,128)S(1)}, f32[192,1024]{1,0:T(8,128)S(1)}) custom-call(f32[288,256]{1,0:T(8,128)S(1)} %get-tuple-element.10.refs_0_, bf16[288,1024]{1,0:T(8,128)(2,1)S(1)} %get-tuple-element.11.refs_1_, s32[16,1024]{1,0:T(8,128)S(1)} %get-tuple-element.12.refs_2_, s32[8]{0:T(128)S(1)} %copy-done.3, s32[1]{0:T(128)S(6)} %copy.10.slot_hbm.refs_4_, ...), custom_call_target="tpu_custom_call" | custom-call | tf_op jit(solution)/shard_map/correlate/pallas_call | solution.py:397
  20.4 0.1 collective-permute-start.7
  20.5 0.5 %keep.1 = f32[64,256]{1,0:T(8,128)S(1)} custom-call(f32[192,1024]{1,0:T(8,128)S(1)} %get-tuple-element.13.refs_0_, bf16[1024,256]{1,0:T(8,128)(2,1)S(1)} %copy-done.1), custom_call_target="tpu_custom_call" | custom-call | tf_op jit(solution)/shard_map/keep/pallas_call | solution.py:423
  20.9 0.8 %collective-permute-done.7 = f32[64,256]{1,0:T(8,128)S(1)} collective-permute-done((f32[64,256]{1,0:T(8,128)S(1)}, f32[64,256]{1,0:T(8,128)S(1)}, u32[]{:S(2)}, u32[]{:S(2)}) %collective-permute-start.7) | collective-permute-done | bytes 65568 | tf_op jit(solution)/shard_map/ppermute | solution.py:422
  21.7 0.6 %add.3 = f32[64,256]{1,0:T(8,128)} add(f32[64,256]{1,0:T(8,128)S(1)} %keep.1, f32[64,256]{1,0:T(8,128)S(1)} %collective-permute-done.7) | non-fusion elementwise | flops 16384 | bytes 196608 | tf_op jit(solution)/shard_map/add | solution.py:431
Async XLA Ops:
  2.7 15.1 %copy-start = (bf16[1040,1024]{1,0:T(8,128)(2,1)S(1)}, bf16[1040,1024]{1,0:T(8,128)(2,1)}, u32[]{:S(2)}) copy-start(bf16[1040,1024]{1,0:T(8,128)(2,1)} %constant.7.clone.refs_9_) | copy-start | bytes 6389764
  2.7 15.0 %copy-start.1 = (bf16[1024,256]{1,0:T(8,128)(2,1)S(1)}, bf16[1024,256]{1,0:T(8,128)(2,1)}, u32[]{:S(2)}) copy-start(bf16[1024,256]{1,0:T(8,128)(2,1)} %constant.6.clone.refs_11_.refs_1_) | copy-start | bytes 1572868
  2.7 15.0 %copy-start.2 = (bf16[512,512]{1,0:T(8,128)(2,1)S(1)}, bf16[512,512]{1,0:T(8,128)(2,1)}, u32[]{:S(2)}) copy-start(bf16[512,512]{1,0:T(8,128)(2,1)} %constant.8.clone.refs_10_) | copy-start | bytes 1572868
  2.7 15.0 %copy-start.3 = (s32[8]{0:T(128)S(1)}, s32[8]{0:T(128)}, u32[]{:S(2)}) copy-start(s32[8]{0:T(128)} %refs_3_.1) | copy-start | bytes 100
  2.7 8.9 %collective-permute-start.2 = (s16[144,256]{1,0:T(8,128)(2,1)}, s16[144,256]{1,0:T(8,128)(2,1)S(1)}, u32[]{:S(2)}, u32[]{:S(2)}) collective-permute-start(s16[144,256]{1,0:T(8,128)(2,1)} %filter.1.refs_0_), channel_id=1, source_target_pairs={{0,8},{2,10},{4,12},{6,14},{8,0},{10,2},{12,4},{14,6},{1,9},{3,11}... | collective-permute-start | bytes 221192 | tf_op jit(solution)/shard_map/ppermute | solution.py:367
  6.8 6.1 %collective-permute-start.1 = (s16[144,256]{1,0:T(8,128)(2,1)}, s16[144,256]{1,0:T(8,128)(2,1)S(1)}, u32[]{:S(2)}, u32[]{:S(2)}) collective-permute-start(s16[144,256]{1,0:T(8,128)(2,1)} %filter.1.refs_0_), channel_id=1, source_target_pairs={{0,2},{2,0},{4,6},{6,4},{8,10},{10,8},{12,14},{14,12},{1,3},{3,1},... | collective-permute-start | bytes 221192 | tf_op jit(solution)/shard_map/ppermute | solution.py:367
  8.3 5.2 %collective-permute-start = (s16[144,256]{1,0:T(8,128)(2,1)}, s16[144,256]{1,0:T(8,128)(2,1)S(1)}, u32[]{:S(2)}, u32[]{:S(2)}) collective-permute-start(s16[144,256]{1,0:T(8,128)(2,1)} %filter.1.refs_0_), channel_id=1, source_target_pairs={{0,4},{2,6},{4,0},{6,2},{8,12},{10,14},{12,8},{14,10},{1,5},{3,7},... | collective-permute-start | bytes 221192 | tf_op jit(solution)/shard_map/ppermute | solution.py:367
  9.9 6.2 %collective-permute-start.5 = (s16[144,256]{1,0:T(8,128)(2,1)}, s16[144,256]{1,0:T(8,128)(2,1)S(1)}, u32[]{:S(2)}, u32[]{:S(2)}) collective-permute-start(s16[144,256]{1,0:T(8,128)(2,1)} %filter.1.refs_0_), channel_id=1, source_target_pairs={{0,6},{2,4},{4,2},{6,0},{8,14},{10,12},{12,10},{14,8},{1,7},{3,5},... | collective-permute-start | bytes 221192 | tf_op jit(solution)/shard_map/ppermute | solution.py:367
  10.3 6.5 %collective-permute-start.3 = (s16[144,256]{1,0:T(8,128)(2,1)}, s16[144,256]{1,0:T(8,128)(2,1)S(1)}, u32[]{:S(2)}, u32[]{:S(2)}) collective-permute-start(s16[144,256]{1,0:T(8,128)(2,1)} %filter.1.refs_0_), channel_id=1, source_target_pairs={{0,12},{2,14},{4,8},{6,10},{8,4},{10,6},{12,0},{14,2},{1,13},{3,15... | collective-permute-start | bytes 221192 | tf_op jit(solution)/shard_map/ppermute | solution.py:367
  11.7 6.1 %collective-permute-start.6 = (s16[144,256]{1,0:T(8,128)(2,1)S(1)}, s16[144,256]{1,0:T(8,128)(2,1)S(1)}, u32[]{:S(2)}, u32[]{:S(2)}) collective-permute-start(s16[144,256]{1,0:T(8,128)(2,1)S(1)} %collective-permute-done.2.refs_3_), channel_id=1, source_target_pairs={{0,6},{2,4},{4,2},{6,0},{8,14},{10,12},{12,10},{14,8},{1,7},{3,5},... | collective-permute-start | bytes 221192 | tf_op jit(solution)/shard_map/ppermute | solution.py:367
  12.9 4.8 %collective-permute-start.4 = (s16[144,256]{1,0:T(8,128)(2,1)S(1)}, s16[144,256]{1,0:T(8,128)(2,1)S(1)}, u32[]{:S(2)}, u32[]{:S(2)}) collective-permute-start(s16[144,256]{1,0:T(8,128)(2,1)S(1)} %collective-permute-done.2.refs_3_), channel_id=1, source_target_pairs={{0,2},{2,0},{4,6},{6,4},{8,10},{10,8},{12,14},{14,12},{1,3},{3,1},... | collective-permute-start | bytes 221192 | tf_op jit(solution)/shard_map/ppermute | solution.py:367
  13.5 0.9 %copy-start.4 = (s16[144,256]{1,0:T(8,128)(2,1)S(1)}, s16[144,256]{1,0:T(8,128)(2,1)}, u32[]{:S(2)}) copy-start(s16[144,256]{1,0:T(8,128)(2,1)} %filter.1.refs_0_) | copy-start | bytes 221188
  20.4 1.3 %collective-permute-start.7 = (f32[64,256]{1,0:T(8,128)S(1)}, f32[64,256]{1,0:T(8,128)S(1)}, u32[]{:S(2)}, u32[]{:S(2)}) collective-permute-start(f32[64,256]{1,0:T(8,128)S(1)} %get-tuple-element.14), channel_id=1, source_target_pairs={{0,1},{1,0},{2,3},{3,2},{4,5},{5,4},{6,7},{7,6},{8,9},{9,8},{10,11... | collective-permute-start | bytes 196616 | tf_op jit(solution)/shard_map/ppermute | solution.py:422

commit v8 on v7

--- a/solution.py
+++ b/solution.py
@@ -38,8 +38,8 @@
 CORRELATE_VMEM = 40 << 20
 LOCAL_ROWS = 32768
 LAST_HOP = {1: 1, 2: 2, 3: 3, 4: 4, 6: 6, 5: 1, 7: 3}
-EARLY = (0, 2, 1, 4)
-LATE = (6, 5, 3, 7)
+EARLY = (0, 2, 1)
+LATE = (4, 6, 5, 3, 7)
 CODE = 23000.0
 
 

time: 22.5 us -> 22.3 us (level)
  Pallas kernels: 5.77 us -> 5.5 us
where the time goes in v8:
time: 22.3 us; the launch traced here: 22.2 us
  starting transfers between devices  10.8 us (48%)
  Pallas kernels  5.5 us (25%)
  waiting for transfers between devices  3.56 us (16%)
  local copies, waits for them, and re-layouts  0.91 us (4%)
  between operations  0.74 us (3%)
  other arithmetic  0.64 us (3%)
    ppermute x7, starting transfers between devices, swap(): lax.ppermute(value, 'chan', [(i, i ^ step) for i in range(block_total)])  10.7 us
    ppermute x7, waiting for transfers between devices, swap(): lax.ppermute(value, 'chan', [(i, i ^ step) for i in range(block_total)])  2.76 us
    pallas_call x1, Pallas kernels, gathered_body(): pl.pallas_call(lambda *refs: correlate_kernel(block_total, span_total, *r...  2.44 us
    pallas_call x1, Pallas kernels, gathered_body(): pl.pallas_call(filter_kernel, out_shape=jax.ShapeDtypeStruct(unit_shape,...  2.02 us
    unnamed x10, local copies, waits for them, and re-layouts  0.91 us
    ppermute x1, waiting for transfers between devices, gathered_body(): other = lax.ppermute(send, 'win', [(i, i ^ 1) for i in range(span_total)])  0.8 us
    add x1, other arithmetic, gathered_body(): return (keep + other).reshape(block_total // span_total, CH_DEV, LAGS)  0.64 us
    pallas_call x1, Pallas kernels, gathered_body(): pl.pallas_call(lambda *refs: early_kernel(len(EARLY), *refs), out_shape=(...  0.61 us
  transfers between devices with their start and end apart: 8, of which 4 were waited for; matrix products, arithmetic and copies ran while one was open for 0% of the time, Pallas kernels for 5%

profile of v8, /device:TPU:0, one launch (start us, length us, event | category | flops | bytes accessed | tf_op | source)
XLA Modules:
  0.0 22.2 jit_solution(11501128787615207885)
XLA Ops:
  0.7 2.0 %filter.1.refs_0_ = s16[144,256]{1,0:T(8,128)(2,1)} custom-call(bf16[256,512]{1,0:T(8,128)(2,1)} %records_hbm.1, s32[256]{0:T(256)} %channel_hbm.1, s32[256]{0:T(256)} %piece_hbm.1, bf16[32]{0:T(256)(128)(2,1)} %taps_hbm.1, s32[1]{0:T(128)S(6)} %copy.10.slot_hbm.refs_4_), custom_call_target="tpu_custom_call" | custom-call | flops 10000000000 | bytes 1048576 | tf_op jit(solution)/shard_map/filter/pallas_call | solution.py:345
  2.7 0.0 copy-start
  2.7 0.0 copy-start.1
  2.7 0.0 copy-start.2
  2.7 0.0 copy-start.3
  2.7 4.1 %collective-permute-start.2 = (s16[144,256]{1,0:T(8,128)(2,1)}, s16[144,256]{1,0:T(8,128)(2,1)S(1)}, u32[]{:S(2)}, u32[]{:S(2)}) collective-permute-start(s16[144,256]{1,0:T(8,128)(2,1)} %filter.1.refs_0_), channel_id=1, source_target_pairs={{0,8},{2,10},{4,12},{6,14},{8,0},{10,2},{12,4},{14,6},{1,9},{3,11}... | collective-permute-start | bytes 221192 | tf_op jit(solution)/shard_map/ppermute | solution.py:367
  6.8 1.5 %collective-permute-start.1 = (s16[144,256]{1,0:T(8,128)(2,1)}, s16[144,256]{1,0:T(8,128)(2,1)S(1)}, u32[]{:S(2)}, u32[]{:S(2)}) collective-permute-start(s16[144,256]{1,0:T(8,128)(2,1)} %filter.1.refs_0_), channel_id=1, source_target_pairs={{0,2},{2,0},{4,6},{6,4},{8,10},{10,8},{12,14},{14,12},{1,3},{3,1},... | collective-permute-start | bytes 221192 | tf_op jit(solution)/shard_map/ppermute | solution.py:367
  8.3 1.6 %collective-permute-start = (s16[144,256]{1,0:T(8,128)(2,1)}, s16[144,256]{1,0:T(8,128)(2,1)S(1)}, u32[]{:S(2)}, u32[]{:S(2)}) collective-permute-start(s16[144,256]{1,0:T(8,128)(2,1)} %filter.1.refs_0_), channel_id=1, source_target_pairs={{0,4},{2,6},{4,0},{6,2},{8,12},{10,14},{12,8},{14,10},{1,5},{3,7},... | collective-permute-start | bytes 221192 | tf_op jit(solution)/shard_map/ppermute | solution.py:367
  9.9 0.4 %collective-permute-start.5 = (s16[144,256]{1,0:T(8,128)(2,1)}, s16[144,256]{1,0:T(8,128)(2,1)S(1)}, u32[]{:S(2)}, u32[]{:S(2)}) collective-permute-start(s16[144,256]{1,0:T(8,128)(2,1)} %filter.1.refs_0_), channel_id=1, source_target_pairs={{0,6},{2,4},{4,2},{6,0},{8,14},{10,12},{12,10},{14,8},{1,7},{3,5},... | collective-permute-start | bytes 221192 | tf_op jit(solution)/shard_map/ppermute | solution.py:367
  10.3 1.4 %collective-permute-start.3 = (s16[144,256]{1,0:T(8,128)(2,1)}, s16[144,256]{1,0:T(8,128)(2,1)S(1)}, u32[]{:S(2)}, u32[]{:S(2)}) collective-permute-start(s16[144,256]{1,0:T(8,128)(2,1)} %filter.1.refs_0_), channel_id=1, source_target_pairs={{0,12},{2,14},{4,8},{6,10},{8,4},{10,6},{12,0},{14,2},{1,13},{3,15... | collective-permute-start | bytes 221192 | tf_op jit(solution)/shard_map/ppermute | solution.py:367
  11.7 0.0 collective-permute-done.2.refs_5_
  11.7 1.3 %collective-permute-start.6 = (s16[144,256]{1,0:T(8,128)(2,1)S(1)}, s16[144,256]{1,0:T(8,128)(2,1)S(1)}, u32[]{:S(2)}, u32[]{:S(2)}) collective-permute-start(s16[144,256]{1,0:T(8,128)(2,1)S(1)} %collective-permute-done.2.refs_5_), channel_id=1, source_target_pairs={{0,6},{2,4},{4,2},{6,0},{8,14},{10,12},{12,10},{14,8},{1,7},{3,5},... | collective-permute-start | bytes 221192 | tf_op jit(solution)/shard_map/ppermute | solution.py:367
  12.9 0.0 collective-permute-done.1.refs_2_
  12.9 0.5 %collective-permute-start.4 = (s16[144,256]{1,0:T(8,128)(2,1)S(1)}, s16[144,256]{1,0:T(8,128)(2,1)S(1)}, u32[]{:S(2)}, u32[]{:S(2)}) collective-permute-start(s16[144,256]{1,0:T(8,128)(2,1)S(1)} %collective-permute-done.2.refs_5_), channel_id=1, source_target_pairs={{0,2},{2,0},{4,6},{6,4},{8,10},{10,8},{12,14},{14,12},{1,3},{3,1},... | collective-permute-start | bytes 221192 | tf_op jit(solution)/shard_map/ppermute | solution.py:367
  13.5 0.0 collective-permute-done.refs_1_
  13.5 0.0 copy-start.4
  13.5 0.9 %copy-done.4 = s16[144,256]{1,0:T(8,128)(2,1)S(1)} copy-done((s16[144,256]{1,0:T(8,128)(2,1)S(1)}, s16[144,256]{1,0:T(8,128)(2,1)}, u32[]{:S(2)}) %copy-start.4) | copy-done | bytes 73752
  14.4 0.6 %early.1 = (f32[288,256]{1,0:T(8,128)S(1)}, bf16[288,768]{1,0:T(8,128)(2,1)S(1)}, s32[16,768]{1,0:T(8,128)S(1)}) custom-call(s16[144,256]{1,0:T(8,128)(2,1)S(1)} %copy-done.4, s16[144,256]{1,0:T(8,128)(2,1)S(1)} %collective-permute-done.refs_1_, s16[144,256]{1,0:T(8,128)(2,1)S(1)} %collective-permute-done.1.refs_2_), custom_call_target="tpu_custom_call" | custom-call | flops 1000000000 | bytes 1048576 | tf_op jit(solution)/shard_map/early/pallas_call | solution.py:379
  15.0 1.2 %collective-permute-done.5.refs_8_ = s16[144,256]{1,0:T(8,128)(2,1)S(1)} collective-permute-done((s16[144,256]{1,0:T(8,128)(2,1)}, s16[144,256]{1,0:T(8,128)(2,1)S(1)}, u32[]{:S(2)}, u32[]{:S(2)}) %collective-permute-start.5) | collective-permute-done | bytes 73760 | tf_op jit(solution)/shard_map/ppermute | solution.py:367
  16.1 0.6 %collective-permute-done.3.refs_6_ = s16[144,256]{1,0:T(8,128)(2,1)S(1)} collective-permute-done((s16[144,256]{1,0:T(8,128)(2,1)}, s16[144,256]{1,0:T(8,128)(2,1)S(1)}, u32[]{:S(2)}, u32[]{:S(2)}) %collective-permute-start.3) | collective-permute-done | bytes 73760 | tf_op jit(solution)/shard_map/ppermute | solution.py:367
  16.8 0.9 %collective-permute-done.6.refs_9_ = s16[144,256]{1,0:T(8,128)(2,1)S(1)} collective-permute-done((s16[144,256]{1,0:T(8,128)(2,1)S(1)}, s16[144,256]{1,0:T(8,128)(2,1)S(1)}, u32[]{:S(2)}, u32[]{:S(2)}) %collective-permute-start.6) | collective-permute-done | bytes 73760 | tf_op jit(solution)/shard_map/ppermute | solution.py:367
  17.7 0.0 collective-permute-done.4.refs_7_
  17.7 0.0 copy-done
  17.7 0.0 copy-done.1
  17.7 0.0 copy-done.2
  17.7 0.0 copy-done.3
  17.8 2.4 %correlate.1 = (f32[64,256]{1,0:T(8,128)S(1)}, f32[192,1024]{1,0:T(8,128)S(1)}) custom-call(f32[288,256]{1,0:T(8,128)S(1)} %get-tuple-element.10.refs_0_, bf16[288,768]{1,0:T(8,128)(2,1)S(1)} %get-tuple-element.11.refs_1_, s32[16,768]{1,0:T(8,128)S(1)} %get-tuple-element.12.refs_2_, s32[8]{0:T(128)S(1)} %copy-done.3, s32[1]{0:T(128)S(6)} %copy.10.slot_hbm.refs_4_, ...), custom_call_target="tpu_custom_call" | custom-call | tf_op jit(solution)/shard_map/correlate/pallas_call | solution.py:397
  20.2 0.1 collective-permute-start.7
  20.3 0.4 %keep.1 = f32[64,256]{1,0:T(8,128)S(1)} custom-call(f32[192,1024]{1,0:T(8,128)S(1)} %get-tuple-element.13.refs_0_, bf16[1024,256]{1,0:T(8,128)(2,1)S(1)} %copy-done.1), custom_call_target="tpu_custom_call" | custom-call | tf_op jit(solution)/shard_map/keep/pallas_call | solution.py:423
  20.7 0.8 %collective-permute-done.7 = f32[64,256]{1,0:T(8,128)S(1)} collective-permute-done((f32[64,256]{1,0:T(8,128)S(1)}, f32[64,256]{1,0:T(8,128)S(1)}, u32[]{:S(2)}, u32[]{:S(2)}) %collective-permute-start.7) | collective-permute-done | bytes 65568 | tf_op jit(solution)/shard_map/ppermute | solution.py:422
  21.5 0.6 %add.3 = f32[64,256]{1,0:T(8,128)} add(f32[64,256]{1,0:T(8,128)S(1)} %keep.1, f32[64,256]{1,0:T(8,128)S(1)} %collective-permute-done.7) | non-fusion elementwise | flops 16384 | bytes 196608 | tf_op jit(solution)/shard_map/add | solution.py:431
Async XLA Ops:
  2.7 15.1 %copy-start = (bf16[1040,1024]{1,0:T(8,128)(2,1)S(1)}, bf16[1040,1024]{1,0:T(8,128)(2,1)}, u32[]{:S(2)}) copy-start(bf16[1040,1024]{1,0:T(8,128)(2,1)} %constant.7.clone.refs_10_) | copy-start | bytes 6389764
  2.7 15.0 %copy-start.1 = (bf16[1024,256]{1,0:T(8,128)(2,1)S(1)}, bf16[1024,256]{1,0:T(8,128)(2,1)}, u32[]{:S(2)}) copy-start(bf16[1024,256]{1,0:T(8,128)(2,1)} %constant.6.clone.refs_12_.refs_1_) | copy-start | bytes 1572868
  2.7 15.0 %copy-start.2 = (bf16[512,512]{1,0:T(8,128)(2,1)S(1)}, bf16[512,512]{1,0:T(8,128)(2,1)}, u32[]{:S(2)}) copy-start(bf16[512,512]{1,0:T(8,128)(2,1)} %constant.8.clone.refs_11_) | copy-start | bytes 1572868
  2.7 15.0 %copy-start.3 = (s32[8]{0:T(128)S(1)}, s32[8]{0:T(128)}, u32[]{:S(2)}) copy-start(s32[8]{0:T(128)} %refs_3_.1) | copy-start | bytes 100
  2.7 8.9 %collective-permute-start.2 = (s16[144,256]{1,0:T(8,128)(2,1)}, s16[144,256]{1,0:T(8,128)(2,1)S(1)}, u32[]{:S(2)}, u32[]{:S(2)}) collective-permute-start(s16[144,256]{1,0:T(8,128)(2,1)} %filter.1.refs_0_), channel_id=1, source_target_pairs={{0,8},{2,10},{4,12},{6,14},{8,0},{10,2},{12,4},{14,6},{1,9},{3,11}... | collective-permute-start | bytes 221192 | tf_op jit(solution)/shard_map/ppermute | solution.py:367
  6.8 6.1 %collective-permute-start.1 = (s16[144,256]{1,0:T(8,128)(2,1)}, s16[144,256]{1,0:T(8,128)(2,1)S(1)}, u32[]{:S(2)}, u32[]{:S(2)}) collective-permute-start(s16[144,256]{1,0:T(8,128)(2,1)} %filter.1.refs_0_), channel_id=1, source_target_pairs={{0,2},{2,0},{4,6},{6,4},{8,10},{10,8},{12,14},{14,12},{1,3},{3,1},... | collective-permute-start | bytes 221192 | tf_op jit(solution)/shard_map/ppermute | solution.py:367
  8.3 5.2 %collective-permute-start = (s16[144,256]{1,0:T(8,128)(2,1)}, s16[144,256]{1,0:T(8,128)(2,1)S(1)}, u32[]{:S(2)}, u32[]{:S(2)}) collective-permute-start(s16[144,256]{1,0:T(8,128)(2,1)} %filter.1.refs_0_), channel_id=1, source_target_pairs={{0,4},{2,6},{4,0},{6,2},{8,12},{10,14},{12,8},{14,10},{1,5},{3,7},... | collective-permute-start | bytes 221192 | tf_op jit(solution)/shard_map/ppermute | solution.py:367
  9.9 6.2 %collective-permute-start.5 = (s16[144,256]{1,0:T(8,128)(2,1)}, s16[144,256]{1,0:T(8,128)(2,1)S(1)}, u32[]{:S(2)}, u32[]{:S(2)}) collective-permute-start(s16[144,256]{1,0:T(8,128)(2,1)} %filter.1.refs_0_), channel_id=1, source_target_pairs={{0,6},{2,4},{4,2},{6,0},{8,14},{10,12},{12,10},{14,8},{1,7},{3,5},... | collective-permute-start | bytes 221192 | tf_op jit(solution)/shard_map/ppermute | solution.py:367
  10.3 6.5 %collective-permute-start.3 = (s16[144,256]{1,0:T(8,128)(2,1)}, s16[144,256]{1,0:T(8,128)(2,1)S(1)}, u32[]{:S(2)}, u32[]{:S(2)}) collective-permute-start(s16[144,256]{1,0:T(8,128)(2,1)} %filter.1.refs_0_), channel_id=1, source_target_pairs={{0,12},{2,14},{4,8},{6,10},{8,4},{10,6},{12,0},{14,2},{1,13},{3,15... | collective-permute-start | bytes 221192 | tf_op jit(solution)/shard_map/ppermute | solution.py:367
  11.7 6.1 %collective-permute-start.6 = (s16[144,256]{1,0:T(8,128)(2,1)S(1)}, s16[144,256]{1,0:T(8,128)(2,1)S(1)}, u32[]{:S(2)}, u32[]{:S(2)}) collective-permute-start(s16[144,256]{1,0:T(8,128)(2,1)S(1)} %collective-permute-done.2.refs_5_), channel_id=1, source_target_pairs={{0,6},{2,4},{4,2},{6,0},{8,14},{10,12},{12,10},{14,8},{1,7},{3,5},... | collective-permute-start | bytes 221192 | tf_op jit(solution)/shard_map/ppermute | solution.py:367
  12.9 4.8 %collective-permute-start.4 = (s16[144,256]{1,0:T(8,128)(2,1)S(1)}, s16[144,256]{1,0:T(8,128)(2,1)S(1)}, u32[]{:S(2)}, u32[]{:S(2)}) collective-permute-start(s16[144,256]{1,0:T(8,128)(2,1)S(1)} %collective-permute-done.2.refs_5_), channel_id=1, source_target_pairs={{0,2},{2,0},{4,6},{6,4},{8,10},{10,8},{12,14},{14,12},{1,3},{3,1},... | collective-permute-start | bytes 221192 | tf_op jit(solution)/shard_map/ppermute | solution.py:367
  13.5 0.9 %copy-start.4 = (s16[144,256]{1,0:T(8,128)(2,1)S(1)}, s16[144,256]{1,0:T(8,128)(2,1)}, u32[]{:S(2)}) copy-start(s16[144,256]{1,0:T(8,128)(2,1)} %filter.1.refs_0_) | copy-start | bytes 221188
  20.2 1.3 %collective-permute-start.7 = (f32[64,256]{1,0:T(8,128)S(1)}, f32[64,256]{1,0:T(8,128)S(1)}, u32[]{:S(2)}, u32[]{:S(2)}) collective-permute-start(f32[64,256]{1,0:T(8,128)S(1)} %get-tuple-element.14), channel_id=1, source_target_pairs={{0,1},{1,0},{2,3},{3,2},{4,5},{5,4},{6,7},{7,6},{8,9},{9,8},{10,11... | collective-permute-start | bytes 196616 | tf_op jit(solution)/shard_map/ppermute | solution.py:422
